TPU v7x, 32 devices: a whole 2x2x4 slice. The times are simulated.
32 devices in a mesh: seq: 16 (over z, y, core), mp: 2 (over x).
Axes of the slice: x: 2, y: 2, z: 4, core: 2. Of those that a mesh axis runs over, the one named last changes fastest.
Arguments:
- tokens: float32 [8192, 1024], P('seq'), may hold values from -6 to 6
- window_state: float32 [2, 1024, 16], P(None, ('seq', 'mp')), may hold values from -6 to 6
- norm1_gain: float32 [1024], replicated, may hold values from 0.5 to 1.5
- norm1_bias: float32 [1024], replicated, may hold values from -3 to 3
- in_coef: float32 [1024, 16], P(('seq', 'mp')), may hold values from -0.375 to 0.375
- out_coef: float32 [1024, 16], P(('seq', 'mp')), may hold values from -4 to 4
- decay_rate: float32 [1024, 16], P(('seq', 'mp')), may hold values from 6.1035156e-05 to 0.04
- skip_gain: float32 [1024], P(('seq', 'mp')), may hold values from 0.5 to 1.5
- qkv_weight: bfloat16 [3, 1024, 1024], P(None, None, 'mp'), may hold values from -0.1875 to 0.1875
- out_weight: bfloat16 [1024, 1024], P('mp'), may hold values from -0.75 to 0.75
- norm2_gain: float32 [1024], replicated, may hold values from 0.5 to 1.5
- norm2_bias: float32 [1024], replicated, may hold values from -3 to 3
- up_weight: bfloat16 [1024, 4096], P(None, 'mp'), may hold values from -0.1875 to 0.1875
- up_bias: float32 [4096], P('mp'), may hold values from -3 to 3
- down_weight: bfloat16 [4096, 1024], P('mp'), may hold values from -0.1875 to 0.1875
- down_bias: float32 [1024], replicated, may hold values from -3 to 3
- cotangent: float32 [8192, 1024], P('seq'), may hold values from -6 to 6
Outputs:
- result: float32 [8192, 1024], P('seq')
- grad_tokens: float32 [8192, 1024], P('seq')
- grad_norm1_gain: float32 [1024], replicated
- grad_norm1_bias: float32 [1024], replicated
- grad_in_coef: float32 [1024, 16], P(('seq', 'mp'))
- grad_out_coef: float32 [1024, 16], P(('seq', 'mp'))
- grad_decay_rate: float32 [1024, 16], P(('seq', 'mp'))
- grad_skip_gain: float32 [1024], P(('seq', 'mp'))
- grad_qkv_weight: float32 [3, 1024, 1024], P(None, None, 'mp')
- grad_out_weight: float32 [1024, 1024], P('mp')
- grad_norm2_gain: float32 [1024], replicated
- grad_norm2_bias: float32 [1024], replicated
- grad_up_weight: float32 [1024, 4096], P(None, 'mp')
- grad_up_bias: float32 [4096], P('mp')
- grad_down_weight: float32 [4096, 1024], P('mp')
- grad_down_bias: float32 [1024], replicated
All inputs are finite; a program needn't handle non-finite values.
Results may differ from a plain program's by a relative error of at most 0.002.
Values sent between devices are 32-bit elements; how exact they have to be, the bound alone decides.
No kernel may reach another device: no remote copies, remote signals or barrier semaphores. Data moves between devices by JAX's collectives and lax.ppermute only.
A program may use at most 192 MiB of HBM per device.

v0:
```python
import math

import jax
import jax.numpy as jnp
from jax import lax
from jax.sharding import PartitionSpec as P

HDIM = 128
BLOCK = 512
CTX = 128
LEN = 4096


epsilon = 1e-05


def from_behind(block, axis, distance):
    devices = range(lax.axis_size(axis))
    route = [(i - distance, i) for i in devices if i - distance in devices]
    return lax.ppermute(block, axis, route)


def product(form, left, right):
    return jnp.einsum(form, left, right, precision=lax.Precision.HIGHEST)


def layer_norm(value, gain, bias):
    center = value - jnp.mean(value, axis=-1, keepdims=True)
    spread = jnp.mean(center * center, axis=-1, keepdims=True)
    return center * lax.rsqrt(spread + epsilon) * gain + bias


def angle_table(count_rows, count_cols, modulus):
    left = jnp.arange(count_rows, dtype=jnp.int32)[:, None]
    right = jnp.arange(count_cols, dtype=jnp.int32)[None, :]
    phase = left * right % modulus
    angle = phase.astype(jnp.float32) * (2.0 * math.pi / modulus)
    return (jnp.cos(angle), jnp.sin(angle))


def forward_dft(signal, tables):
    cos_one, sin_one, cos_twid, sin_twid, cos_two, sin_two = tables
    first_re = product("...ab,ak->...kb", signal, cos_one)
    first_im = -product("...ab,ak->...kb", signal, sin_one)
    twid_re = first_re * cos_twid + first_im * sin_twid
    twid_im = first_im * cos_twid - first_re * sin_twid
    spec_re = product("...kb,bm->...km", twid_re, cos_two) + product(
        "...kb,bm->...km", twid_im, sin_two
    )
    spec_im = product("...kb,bm->...km", twid_im, cos_two) - product(
        "...kb,bm->...km", twid_re, sin_two
    )
    return (spec_re, spec_im)


def inverse_dft(spec_re, spec_im, tables, total):
    cos_one, sin_one, cos_twid, sin_twid, cos_two, sin_two = tables
    back_re = product("...km,mb->...kb", spec_re, cos_two) - product(
        "...km,mb->...kb", spec_im, sin_two
    )
    back_im = product("...km,mb->...kb", spec_re, sin_two) + product(
        "...km,mb->...kb", spec_im, cos_two
    )
    turn_re = back_re * cos_twid - back_im * sin_twid
    turn_im = back_re * sin_twid + back_im * cos_twid
    real_part = product("...kb,ka->...ab", turn_re, cos_one) - product(
        "...kb,ka->...ab", turn_im, sin_one
    )
    return real_part / total


def causal_conv(signal, kernel):
    channels, windows, length = signal.shape
    total = 2 * length
    bits = total.bit_length() - 1
    cols_count = 1 << bits - bits // 2
    rows_count = total // cols_count
    cos_one, sin_one = angle_table(rows_count, rows_count, rows_count)
    cos_twid, sin_twid = angle_table(rows_count, cols_count, total)
    cos_two, sin_two = angle_table(cols_count, cols_count, cols_count)
    tables = (cos_one, sin_one, cos_twid, sin_twid, cos_two, sin_two)
    padded = jnp.concatenate([signal, jnp.zeros_like(signal)], -1).reshape(
        channels, windows, rows_count, cols_count
    )
    kern_pad = jnp.concatenate([kernel, jnp.zeros_like(kernel)], -1).reshape(
        channels, 1, rows_count, cols_count
    )
    sig_re, sig_im = forward_dft(padded, tables)
    ker_re, ker_im = forward_dft(kern_pad, tables)
    prod_re = sig_re * ker_re - sig_im * ker_im
    prod_im = sig_re * ker_im + sig_im * ker_re
    whole = inverse_dft(prod_re, prod_im, tables, total).reshape(channels, windows, total)
    return whole[:, :, :length]


def ssm_local(time_rows, in_coef, out_coef, decay_rate, skip_gain, window_state):
    channels = time_rows.shape[0]
    windows = time_rows.shape[1] // LEN
    signal = time_rows.reshape(channels, windows, LEN)
    steps_t = jnp.arange(LEN).astype(jnp.float32)
    fading = jnp.exp(-decay_rate[:, :, None] * steps_t)
    kernel = product("cn,cnt->ct", in_coef * out_coef, fading)
    shifted = fading * jnp.exp(-decay_rate)[:, :, None]
    start = jnp.einsum(
        "cn,scn,cnt->cst", out_coef, window_state, shifted, precision=lax.Precision.HIGHEST
    )
    conv = causal_conv(signal, kernel)
    return (conv + skip_gain[:, None, None] * signal + start).reshape(channels, windows * LEN)


def attend_local(normed, context, qkv, out_w, ctx_ok):
    rows_here, model_width = normed.shape
    inner = qkv.shape[2]
    blocks = rows_here // BLOCK
    heads_here = inner // HDIM
    highest = lax.Precision.HIGHEST
    query = jnp.dot(normed, qkv[0], precision=highest).reshape(blocks, BLOCK, heads_here, HDIM)
    key_self = jnp.dot(normed, qkv[1], precision=highest).reshape(blocks, BLOCK, heads_here, HDIM)
    value_self = jnp.dot(normed, qkv[2], precision=highest).reshape(blocks, BLOCK, heads_here, HDIM)
    key_ctx = product("dbc,de->bce", context, qkv[1]).reshape(blocks, CTX, heads_here, HDIM)
    value_ctx = product("dbc,de->bce", context, qkv[2]).reshape(blocks, CTX, heads_here, HDIM)
    keys = jnp.concatenate([key_ctx, key_self], 1)
    values = jnp.concatenate([value_ctx, value_self], 1)
    scores = product("bqhe,bkhe->bhqk", query, keys) * HDIM ** (-0.5)
    rows_q = jnp.arange(BLOCK)[:, None]
    cols_k = jnp.arange(CTX + BLOCK)[None, :]
    allowed = jnp.where(
        cols_k < CTX, ctx_ok[:, None, None, None], (cols_k - CTX <= rows_q)[None, None]
    )
    scores = jnp.where(allowed, scores, -1e30)
    probs = jax.nn.softmax(scores, axis=-1)
    heads = product("bhqk,bkhe->bqhe", probs, values).reshape(rows_here, inner)
    return jnp.dot(heads, out_w, precision=highest)


def feed_local(normed2, up_w, up_b, down_w):
    highest = lax.Precision.HIGHEST
    hidden = jax.nn.gelu(jnp.dot(normed2, up_w, precision=highest) + up_b, approximate=False)
    return jnp.dot(hidden, down_w, precision=highest)


def sum_feed_grads(grad_up, grad_up_bias, grad_down, grad_down_bias):
    return lax.psum((grad_up, grad_up_bias, grad_down, grad_down_bias), "seq")


def per_device(
    tokens,
    window_state,
    norm1_gain,
    norm1_bias,
    in_coef,
    out_coef,
    decay_rate,
    skip_gain,
    qkv_weight,
    out_weight,
    norm2_gain,
    norm2_bias,
    up_weight,
    up_bias,
    down_weight,
    down_bias,
    cotangent,
):
    count_seq = lax.axis_size("seq")
    count_mp = lax.axis_size("mp")
    place_seq = lax.axis_index("seq")
    place_mp = lax.axis_index("mp")
    rows_here, model_width = tokens.shape
    blocks_here = rows_here // BLOCK
    channels = in_coef.shape[0]
    qkv_full = qkv_weight.astype(jnp.float32)
    out_full = out_weight.astype(jnp.float32)
    up_full = up_weight.astype(jnp.float32)
    down_full = down_weight.astype(jnp.float32)
    normed, norm1_pull = jax.vjp(layer_norm, tokens, norm1_gain, norm1_bias)
    grouped = normed.reshape(rows_here, count_seq, count_mp, channels)
    own_half = lax.dynamic_index_in_dim(grouped, place_mp, axis=2, keepdims=False)
    outgoing = jnp.transpose(own_half, (1, 2, 0)).reshape(count_seq * channels, rows_here)
    time_in = lax.all_to_all(outgoing, "seq", split_axis=0, concat_axis=1, tiled=True)

    def ssm_piece(time_rows, coef_in, coef_out, rates, skips):
        return ssm_local(time_rows, coef_in, coef_out, rates, skips, window_state)

    time_out, ssm_pull = jax.vjp(ssm_piece, time_in, in_coef, out_coef, decay_rate, skip_gain)
    returned = lax.all_to_all(time_out, "seq", split_axis=1, concat_axis=0, tiled=True)
    width_back = returned.shape[1]
    halves = lax.all_gather(
        returned.reshape(count_seq, 1, channels, width_back), "mp", axis=1, tiled=True
    )
    joined = halves.reshape(model_width, width_back)
    tail = from_behind(joined[:, rows_here - CTX :], "seq", 1)
    extended = jnp.concatenate([tail, joined], 1)
    context = extended[:, :rows_here].reshape(model_width, blocks_here, BLOCK)[:, :, :CTX]
    block_start = (place_seq * rows_here + jnp.arange(blocks_here) * BLOCK) % LEN
    ctx_ok = block_start > 0

    def attend_piece(normed_in, context_in, qkv_in, out_in):
        return attend_local(normed_in, context_in, qkv_in, out_in, ctx_ok)

    attn_part = attend_piece(normed, context, qkv_full, out_full)
    mixed = tokens + lax.psum(attn_part, "mp")
    normed2, norm2_pull = jax.vjp(layer_norm, mixed, norm2_gain, norm2_bias)
    feed_part = feed_local(normed2, up_full, up_bias, down_full)
    result = mixed + lax.psum(feed_part, "mp") + down_bias
    grad_down_bias = jnp.sum(cotangent, axis=0)
    unused_feed, feed_pull = jax.vjp(feed_local, normed2, up_full, up_bias, down_full)
    grad_normed2_part, grad_up, grad_up_bias, grad_down = feed_pull(cotangent)
    grad_normed2 = lax.psum(grad_normed2_part, "mp")
    grad_mixed_norm, grad_gain2, grad_bias2 = norm2_pull(grad_normed2)
    grad_mixed = cotangent + grad_mixed_norm
    unused_attn, attend_pull = jax.vjp(attend_piece, normed, context, qkv_full, out_full)
    grad_normed_part, grad_context, grad_qkv, grad_out = attend_pull(grad_mixed)
    spread_rows = jnp.pad(grad_context, ((0, 0), (0, 0), (0, BLOCK - CTX))).reshape(
        model_width, rows_here
    )
    grad_extended = jnp.concatenate([spread_rows, jnp.zeros((model_width, CTX), jnp.float32)], 1)
    grad_tail = from_behind(grad_extended[:, :CTX], "seq", -1)
    grad_joined = grad_extended[:, CTX:] + jnp.pad(grad_tail, ((0, 0), (rows_here - CTX, 0)))
    width_grad = grad_joined.shape[1]
    grad_half = lax.psum_scatter(
        grad_joined.reshape(count_seq, count_mp, channels, width_grad),
        "mp",
        scatter_dimension=1,
        tiled=True,
    )
    grad_time = lax.all_to_all(
        grad_half.reshape(count_seq * channels, width_grad),
        "seq",
        split_axis=0,
        concat_axis=1,
        tiled=True,
    )
    grad_time_in, grad_in_coef, grad_out_coef, grad_decay, grad_skip = ssm_pull(grad_time)
    grad_back = lax.all_to_all(grad_time_in, "seq", split_axis=1, concat_axis=0, tiled=True)
    selector = (jnp.arange(count_mp) == place_mp).astype(jnp.float32)
    placed = grad_back.reshape(count_seq, 1, channels, rows_here) * selector[None, :, None, None]
    placed_rows = jnp.transpose(placed.reshape(model_width, rows_here))
    grad_normed = lax.psum(grad_normed_part + placed_rows, "mp")
    grad_tokens_norm, grad_gain1, grad_bias1 = norm1_pull(grad_normed)
    grad_tokens = grad_mixed + grad_tokens_norm
    feed_sums = sum_feed_grads(grad_up, grad_up_bias, grad_down, grad_down_bias)
    rest_sums = lax.psum(
        (grad_gain1, grad_bias1, grad_qkv, grad_out, grad_gain2, grad_bias2), "seq"
    )
    return (
        result,
        grad_tokens,
        rest_sums[0],
        rest_sums[1],
        grad_in_coef,
        grad_out_coef,
        grad_decay,
        grad_skip,
        rest_sums[2],
        rest_sums[3],
        rest_sums[4],
        rest_sums[5],
        feed_sums[0],
        feed_sums[1],
        feed_sums[2],
        feed_sums[3],
    )


def solution(mesh):
    placed = (
        P("seq", None),
        P(None, ("seq", "mp"), None),
        P(),
        P(),
        P(("seq", "mp"), None),
        P(("seq", "mp"), None),
        P(("seq", "mp"), None),
        P(("seq", "mp")),
        P(None, None, "mp"),
        P("mp", None),
        P(),
        P(),
        P(None, "mp"),
        P("mp"),
        P("mp", None),
        P(),
        P("seq", None),
    )
    return jax.shard_map(
        per_device,
        mesh=mesh,
        in_specs=placed,
        out_specs=(
            P("seq", None),
            P("seq", None),
            P(),
            P(),
            P(("seq", "mp"), None),
            P(("seq", "mp"), None),
            P(("seq", "mp"), None),
            P(("seq", "mp")),
            P(None, None, "mp"),
            P("mp", None),
            P(),
            P(),
            P(None, "mp"),
            P("mp"),
            P("mp", None),
            P(),
        ),
        check_vma=False,
    )
```

profile of v0, /device:TPU:0, one launch (start us, length us, event | category | flops | bytes accessed | tf_op | source)
XLA Modules:
  0.0 1192.9 jit_solution(4121227456708853096)
XLA Ops:
  15.8 7.4 all-to-all-start
  23.6 5.3 fusion.2
  39.0 7.2 all-to-all-done
  93.2 7.8 fusion.8
  105.9 31.6 %all_to_all.61 = f32[32,16,512]{2,0,1:T(8,128)} all-to-all(f32[32,16,512]{2,0,1:T(8,128)S(1)} %copy.94), channel_id=1, replica_groups=mesh['seq'=16,'mp'=2] {'seq'}, dimensions={1} | all-to-all | bytes 2097152 | tf_op jit(solution)/shard_map/all_to_all | solution.py:186
  155.1 16.1 %all-gather.3.cloned.1.call-done = f32[16,64,512]{2,1,0:T(8,128)} async-done(((f32[16,32,512]{2,1,0:T(8,128)}), f32[16,64,512]{2,1,0:T(8,128)}) %all-gather.3.cloned.1.call-update) | async-done | bytes 2097168 | tf_op jit(solution)/shard_map/all_gather | solution.py:188
  184.1 5.5 fusion.7
  192.0 6.4 fusion.28
  202.8 67.9 %all-reduce.21.cloned.1.call-done = f32[512,1024]{1,0:T(8,128)} async-done(((f32[512,1024]{1,0:T(8,128)}), f32[512,1024]{1,0:T(8,128)}) %all-reduce.21.cloned.1.call-update) | async-done | bytes 2097168 | tf_op jit(solution)/shard_map/psum | solution.py:202
  274.6 7.2 fusion.78
  281.9 19.5 %fusion.441 = (f32[2048]{0:T(1024)}, f32[512,2048]{1,0:T(8,128)S(1)}, f32[512,2048]{1,0:T(8,128)}) fusion(f32[512,2048]{1,0:T(8,128)S(1)} %fusion.78, f32[2048]{0:T(1024)S(1)} %copy-done.116, f32[512,1024]{1,0:T(8,128)S(1)} %copy-done.48, bf16[2048,1024]{1,0:T(8,128)(2,1)S(1)} %copy-done.125), kind=kOutput, calls=%fused_computation.500 | convolution fusion | flops 12961445888 | bytes 18890752 | tf_op jit(solution)/shard_map/transpose(jvp())/dot_general | solution.py:139
  303.4 8.0 fusion.450
  312.5 62.0 %all-reduce.23.cloned.1.call-done = f32[512,1024]{1,0:T(8,128)} async-done(((f32[512,1024]{1,0:T(8,128)}), f32[512,1024]{1,0:T(8,128)}) %all-reduce.23.cloned.1.call-update) | async-done | bytes 2097168 | tf_op jit(solution)/shard_map/psum | solution.py:209
  392.5 8.2 multiply_reduce_fusion.2
  416.8 68.0 %all-reduce.25.cloned.1.call-done = f32[16,2,32,512]{3,2,1,0:T(8,128)} async-done(((f32[16,2,32,512]{3,2,1,0:T(8,128)}), f32[16,2,32,512]{3,2,1,0:T(8,128)}) %all-reduce.25.cloned.1.call-update) | async-done | bytes 2097168
  486.8 30.3 %all_to_all.62 = f32[16,32,512]{2,1,0:T(8,128)S(1)} all-to-all(f32[16,32,512]{2,1,0:T(8,128)S(1)} %dynamic-slice_bitcast_fusion), channel_id=1, replica_groups=mesh['seq'=16,'mp'=2] {'seq'}, dimensions={0} | all-to-all | bytes 2097152 | tf_op jit(solution)/shard_map/all_to_all | solution.py:227
  536.6 5.0 multiply_reduce_fusion.4
  562.6 5.0 all-to-all-start.3
  567.8 12.2 %fusion.106 = f32[512,1024]{1,0:T(8,128)} fusion(bf16[2048,1024]{1,0:T(8,128)(2,1)} %param.31, f32[512,2048]{1,0:T(8,128)} %get-tuple-element.58, f32[512,2048]{1,0:T(8,128)} %copy-done.63, f32[2048]{0:T(1024)S(1)} %copy-done.117), kind=kOutput, calls=%fused_computation.157 | convolution fusion | flops 12888047616 | bytes 14688256 | tf_op jit(solution)/shard_map/dot_general | solution.py:139
  592.0 5.6 fusion.109
  602.3 8.1 bitcast_add_fusion
  612.0 17.8 %fusion.77 = f32[1024,2048]{1,0:T(8,128)} fusion(f32[512,2048]{1,0:T(8,128)} %copy-done.129, f32[512,1024]{1,0:T(8,128)S(1)} %copy-done.19, f32[1024]{0:T(1024)S(1)} %copy-done.127, f32[1024]{0:T(1024)S(1)} %copy-done.115, f32[512]{0:T(512)S(1)} %copy-done.99, f32[512]{0:T(512)S(1)} %copy-done.96), kind=kOutput, calls=%fused_computation.127 | convolution fusion | flops 12886999040 | bytes 14692352 | tf_op jit(solution)/shard_map/transpose(jvp())/dot_general | solution.py:138
  629.9 16.2 %fusion.105 = f32[2048,1024]{1,0:T(8,128)} fusion(f32[512,1024]{1,0:T(8,128)S(1)} %copy-done.50, f32[512,2048]{1,0:T(8,128)S(1)} %copy-done.65, f32[512,2048]{1,0:T(8,128)S(1)} %copy-done.64, f32[2048]{0:T(1024)S(1)} %copy-done.117), kind=kOutput, calls=%fused_computation.156 | convolution fusion | flops 12888047616 | bytes 18882560 | tf_op jit(solution)/shard_map/transpose(jvp())/dot_general | solution.py:139
  649.9 6.9 convolution_bitcast_fusion
  656.8 7.1 convolution_bitcast_fusion.1
  663.8 6.9 convolution_bitcast_fusion.2
  680.9 11.0 fusion.3
  700.9 11.1 fusion
  712.1 10.6 multiply_reduce_fusion.1
  728.6 65.8 %all-reduce.12 = (f32[1024]{0:T(1024)}, f32[1024]{0:T(1024)}, f32[1024]{0:T(1024)}, f32[1024]{0:T(1024)}, f32[2048]{0:T(1024)}, /*index=5*/f32[1024]{0:T(1024)}) all-reduce(f32[1024]{0:T(1024)S(1)} %get-tuple-element.36, f32[1024]{0:T(1024)S(1)} %get-tuple-element.43, ...), channel_id=1, replica_groups=mesh['seq'=16,'mp'=2] {'seq'}, use_global_device_ids=true, to_apply=%region_17.18 | all-reduce | flops 7168 | bytes 57344 | tf_op jit(solution)/shard_map/psum | solution.py:243
  801.7 366.3 %all-reduce.27.cloned.1.call-done = (f32[3,1024,512]{2,1,0:T(8,128)}, f32[512,1024]{1,0:T(8,128)}, f32[1024,2048]{1,0:T(8,128)}, f32[2048,1024]{1,0:T(8,128)}) async-done(((f32[3,1024,512]{2,1,0:T(8,128)}, f32[512,1024]{1,0:T(8,128)}, f32[1024,2048]{1,0:T(8,128)}, f32[2048,1024]{1,0:T(8,128)}), (f32[3,1024,512]{2,1,0:T(8,128)}, f32[512,1024]{1,0:T(8,128)}, f32[1024,2048]{1,0:T(8,128)}, ...) | async-done | bytes 25165840 | tf_op jit(solution)/shard_map/psum | solution.py:243
  1168.0 6.9 copy.162
  (441 shorter events, 255.5 us)
Async XLA Ops:
  7.2 192.2 %copy-start = (bf16[512,1024]{1,0:T(8,128)(2,1)S(1)}, bf16[512,1024]{1,0:T(8,128)(2,1)}, u32[]{:S(2)}) copy-start(bf16[512,1024]{1,0:T(8,128)(2,1)} %param.26) | copy-start | bytes 3145732
  11.4 166.0 %copy-start.2 = (f32[512,1024]{1,0:T(8,128)}, f32[512,1024]{1,0:T(8,128)S(1)}, u32[]{:S(2)}) copy-start(f32[512,1024]{1,0:T(8,128)S(1)} %multiply_add_fusion.6) | copy-start | bytes 6291460
  15.8 30.4 %all-to-all-start = ((f32[16,32,512]{2,1,0:T(8,128)}), f32[16,32,512]{2,1,0:T(8,128)}, u32[]{:S(2)}, u32[]{:S(2)}) async-start(f32[16,32,512]{2,1,0:T(8,128)} %dynamic-slice_bitcast_fusion.1), calls=%async_computation | async-start | bytes 2097152 | tf_op jit(solution)/shard_map/all_to_all | solution.py:180
  23.2 147.9 %all-gather.3.cloned.1.call-start = ((), (), s32[]{:S(2)}) async-start(), calls=%async_computation.6 | async-start | bytes 3145728 | tf_op jit(solution)/shard_map/all_gather | solution.py:188
  23.3 69.9 %copy-start.109 = (f32[4096]{0:T(1024)}, f32[4096]{0:T(1024)S(1)}, u32[]{:S(2)}) copy-start(f32[4096]{0:T(1024)S(1)} %iota_convert_fusion) | copy-start | bytes 49156
  23.4 69.8 %copy-start.90 = (f32[2,32,16]{2,0,1:T(2,128)}, f32[2,32,16]{2,0,1:T(2,128)S(1)}, u32[]{:S(2)}) copy-start(f32[2,32,16]{2,0,1:T(2,128)S(1)} %copy.93) | copy-start | bytes 12292
  23.5 69.7 %copy-start.105 = (f32[32,16]{1,0:T(8,128)}, f32[32,16]{1,0:T(8,128)S(1)}, u32[]{:S(2)}) copy-start(f32[32,16]{1,0:T(8,128)S(1)} %get-tuple-element.72) | copy-start | bytes 6148
  23.5 69.7 %copy-start.107 = (f32[32,16]{1,0:T(8,128)}, f32[32,16]{1,0:T(8,128)S(1)}, u32[]{:S(2)}) copy-start(f32[32,16]{1,0:T(8,128)S(1)} %get-tuple-element.73) | copy-start | bytes 6148
  137.6 133.1 %all-reduce.21.cloned.1.call-start = ((), (), s32[]{:S(2)}) async-start(), calls=%async_computation.4 | async-start | bytes 4194304 | tf_op jit(solution)/shard_map/psum | solution.py:202
  175.2 4.1 collective-permute-start
  202.5 68.1 %copy-start.11 = (f32[512,1024]{1,0:T(8,128)S(1)}, f32[512,1024]{1,0:T(8,128)}, u32[]{:S(2)}) copy-start(f32[512,1024]{1,0:T(8,128)} %param.17) | copy-start | bytes 6291460
  202.6 172.0 %all-reduce.23.cloned.1.call-start = ((), (), s32[]{:S(2)}) async-start(), calls=%async_computation.5 | async-start | bytes 4194304 | tf_op jit(solution)/shard_map/psum | solution.py:209
  281.9 19.5 %copy-start.63 = (f32[512,2048]{1,0:T(8,128)}, f32[512,2048]{1,0:T(8,128)S(1)}, u32[]{:S(2)}) copy-start(f32[512,2048]{1,0:T(8,128)S(1)} %fusion.78) | copy-start | bytes 12582916
  311.4 63.1 %copy-start.18 = (f32[512,1024]{1,0:T(8,128)S(1)}, f32[512,1024]{1,0:T(8,128)}, u32[]{:S(2)}) copy-start(f32[512,1024]{1,0:T(8,128)} %copy-done.17) | copy-start | bytes 6291460
  311.5 173.4 %all-reduce.25.cloned.1.call-start = ((), (), s32[]{:S(2)}) async-start(), calls=%async_computation.7 | async-start | bytes 4194304
  409.8 3.8 collective-permute-start.1
  562.6 35.0 %all-to-all-start.3 = ((f32[32,16,512]{2,0,1:T(8,128)}), f32[32,16,512]{2,0,1:T(8,128)S(1)}, u32[]{:S(2)}, u32[]{:S(2)}) async-start(f32[32,16,512]{2,0,1:T(8,128)} %copy.107), calls=%async_computation.3 | async-start | bytes 2097152 | tf_op jit(solution)/shard_map/all_to_all | solution.py:235
  567.6 158.5 %all-reduce.29.cloned.1.call-start = ((), (), s32[]{:S(2)}) async-start(), calls=%async_computation.9 | async-start | bytes 8388608 | tf_op jit(solution)/shard_map/psum | solution.py:205
  567.8 12.2 %copy-start.74 = (f32[1,640,4,128]{1,3,2,0:T(8,128)S(1)}, f32[1,640,4,128]{1,3,2,0:T(8,128)}, u32[]{:S(2)}) copy-start(f32[1,640,4,128]{1,3,2,0:T(8,128)} %copy-done.73) | copy-start | bytes 3932164
  567.8 12.3 %copy-start.56 = (f32[1,640,4,128]{1,3,2,0:T(8,128)S(1)}, f32[1,640,4,128]{1,3,2,0:T(8,128)}, u32[]{:S(2)}) copy-start(f32[1,640,4,128]{1,3,2,0:T(8,128)} %copy-done.55) | copy-start | bytes 3932164
  580.1 11.8 slice-start.4
  610.5 557.5 %all-reduce.27.cloned.1.call-start = ((), (), s32[]{:S(2)}) async-start(), calls=%async_computation.8 | async-start | bytes 50331648 | tf_op jit(solution)/shard_map/psum | solution.py:243
  612.0 17.8 %copy-start.50 = (f32[512,1024]{1,0:T(8,128)S(1)}, f32[512,1024]{1,0:T(8,128)}, u32[]{:S(2)}) copy-start(f32[512,1024]{1,0:T(8,128)} %param.33) | copy-start | bytes 6291460
  612.0 17.8 %copy-start.64 = (f32[512,2048]{1,0:T(8,128)S(1)}, f32[512,2048]{1,0:T(8,128)}, u32[]{:S(2)}) copy-start(f32[512,2048]{1,0:T(8,128)} %copy-done.63) | copy-start | bytes 12582916
  612.0 17.8 %copy-start.65 = (f32[512,2048]{1,0:T(8,128)S(1)}, f32[512,2048]{1,0:T(8,128)}, u32[]{:S(2)}) copy-start(f32[512,2048]{1,0:T(8,128)} %get-tuple-element.58) | copy-start | bytes 12582916
  629.9 16.2 %copy-start.53 = (f32[1024,1,512]{0,2,1:T(8,128)S(1)}, f32[1024,1,512]{0,2,1:T(8,128)}, u32[]{:S(2)}) copy-start(f32[1024,1,512]{0,2,1:T(8,128)} %copy-done.52) | copy-start | bytes 6291460
  680.9 11.1 copy-start.28
  680.9 11.1 copy-start.29
  700.9 11.2 copy-start.91
  712.1 11.4 copy-start.83
  712.1 11.4 copy-start.31
  726.2 68.2 %copy-start.101 = (f32[512]{0:T(512)S(1)}, f32[512]{0:T(512)}, u32[]{:S(2)}) copy-start(f32[512]{0:T(512)} %copy-done.100) | copy-start | bytes 6148
  (116 other events, 427.6 us)
Sparse Core Ops, SparseCore 0:
  137.7 33.4 all-gather.2
  202.7 67.9 all-reduce.20
  311.6 62.9 all-reduce.22
  415.7 69.0 all-reduce.24
  610.6 108.5 all-reduce.28
  724.5 443.4 all-reduce.26
where the time goes:
time: 1200 us; the launch traced here: 1190 us
  waiting for transfers between devices  590 us (49%)
  matrix products  308 us (26%)
  blocking collectives  128 us (11%)
  local copies, waits for them, and re-layouts  99.9 us (8%)
  other arithmetic  34.4 us (3%)
  starting transfers between devices  16.5 us (1%)
  between operations  16.5 us (1%)
    psum x1, waiting for transfers between devices, per_device(): lax.psum((grad_gain1, grad_bias1, grad_qkv, grad_out, grad_gain2, grad_bi...  366 us
    dot_general x50, matrix products, product(): return jnp.einsum(form, left, right, precision=lax.Precision.HIGHEST)  140 us
    unnamed x7, waiting for transfers between devices  68.1 us
    psum x1, waiting for transfers between devices, per_device(): mixed = tokens + lax.psum(attn_part, 'mp')  67.9 us
    psum x1, blocking collectives, per_device(): lax.psum((grad_gain1, grad_bias1, grad_qkv, grad_out, grad_gain2, grad_bi...  65.8 us
    psum x1, waiting for transfers between devices, per_device(): grad_normed2 = lax.psum(grad_normed2_part, 'mp')  62 us
    dot_general x3, matrix products, feed_local(): return jnp.dot(hidden, down_w, precision=highest)  47.9 us
    unnamed x287, local copies, waits for them, and re-layouts  37.9 us
  transfers between devices with their start and end apart: 10, of which 7 were waited for; matrix products, arithmetic and copies ran while one was open for 15% of the time, Pallas kernels for 0%

commit v1 on v0

v1 whole, which is shorter than its diff:
```python
import functools
import math

import jax
import jax.numpy as jnp
from jax import lax
from jax.experimental import pallas as pl
from jax.experimental.pallas import tpu as pltpu
from jax.sharding import PartitionSpec as P

HDIM = 128
BLOCK = 512
CTX = 128
LEN = 4096
EPS = 1e-05
HIGH = lax.Precision.HIGH


def mm(left, right, dims=((1,), (0,))):
    return lax.dot_general(
        left, right, (dims, ((), ())), precision=HIGH, preferred_element_type=jnp.float32
    )


def norm_parts(value):
    center = value - jnp.mean(value, axis=-1, keepdims=True)
    spread = jnp.mean(center * center, axis=-1, keepdims=True)
    rate = lax.rsqrt(spread + EPS)
    return center * rate, rate


def norm_back(grad, unit, rate, gain):
    scaled = grad * gain
    inner = jnp.mean(scaled * unit, axis=-1, keepdims=True)
    return rate * (scaled - jnp.mean(scaled, axis=-1, keepdims=True) - unit * inner)


def swap_bit(value, axis, bit):
    size = lax.axis_size(axis)
    return lax.ppermute(value, axis, [(i, i ^ (1 << bit)) for i in range(size)])


def bits_of(count):
    return count.bit_length() - 1


def shift_to(value, axis, distance):
    size = lax.axis_size(axis)
    route = [(i, i + distance) for i in range(size) if 0 <= i + distance < size]
    return lax.ppermute(value, axis, route)


def gather_all(piece):
    rows = piece.shape[0]
    mp_size, seq_size = lax.axis_size("mp"), lax.axis_size("seq")
    me = lax.axis_index("seq") * mp_size + lax.axis_index("mp")
    block, low = piece, 0
    for bit in range(bits_of(mp_size * seq_size)):
        axis, own = ("mp", bit) if bit < bits_of(mp_size) else ("seq", bit - bits_of(mp_size))
        other = swap_bit(block, axis, own)
        upper = (me >> bit) & 1
        block = jnp.where(
            upper == 1, jnp.concatenate([other, block], 0), jnp.concatenate([block, other], 0)
        )
    return block


def scatter_sum(whole):
    mp_size, seq_size = lax.axis_size("mp"), lax.axis_size("seq")
    me = lax.axis_index("seq") * mp_size + lax.axis_index("mp")
    block = whole
    for bit in reversed(range(bits_of(mp_size * seq_size))):
        axis, own = ("mp", bit) if bit < bits_of(mp_size) else ("seq", bit - bits_of(mp_size))
        half = block.reshape(2, block.shape[0] // 2, block.shape[1])
        upper = (me >> bit) & 1
        keep = lax.dynamic_index_in_dim(half, upper, 0, keepdims=False)
        give = lax.dynamic_index_in_dim(half, 1 - upper, 0, keepdims=False)
        block = keep + swap_bit(give, axis, own)
    return block


def sum_seq_small(value):
    for bit in range(bits_of(lax.axis_size("seq"))):
        value = value + swap_bit(value, "seq", bit)
    return value


def chip_order(count):
    if count <= 2:
        return list(range(count))
    return list(range(0, count, 2)) + list(range(count - 1 - count % 2, 0, -2))


def ring_route(count):
    order = chip_order(count)
    route = []
    for i in range(count):
        here, there = order[i], order[(i + 1) % count]
        route.append((2 * here, 2 * there))
        route.append((2 * there + 1, 2 * here + 1))
    return route


def pick(value, index):
    return lax.dynamic_index_in_dim(value, index, 0, keepdims=False)


def ring_sum(streams):
    count = lax.axis_size("seq") // 2
    order = chip_order(count)
    places = [0] * count
    for i, chip in enumerate(order):
        places[chip] = i
    me = lax.axis_index("seq")
    core = me % 2
    here = jnp.array(places, jnp.int32)[me // 2]
    place = jnp.where(core == 0, here, (count - here) % count)
    mirror = (count - place) % count
    route = ring_route(count)
    halves = []
    for value in streams:
        rows, cols = value.shape
        split = value.reshape(2, rows // 2, cols)
        mine = pick(split, core) + swap_bit(pick(split, 1 - core), "seq", 0)
        halves.append(mine.reshape(count, rows // 2 // count, cols))
    held = [pick(half, place) for half in halves]
    for step in range(count - 1):
        got = [lax.ppermute(part, "seq", route) for part in held]
        spot = (place + 2 * count - 1 - step) % count
        held = [new + pick(half, spot) for new, half in zip(got, halves)]
    outs = [jnp.zeros((2, count) + part.shape, part.dtype) for part in held]

    def put(whole, part, which, spot):
        return lax.dynamic_update_slice(whole, part[None, None], (which, spot % count, 0, 0))

    for step in range(count):
        spot, far = place + 1 - step + count, mirror + 1 - step + count
        outs = [put(whole, part, core, spot) for whole, part in zip(outs, held)]
        others = [swap_bit(part, "seq", 0) for part in held]
        outs = [put(whole, part, 1 - core, far) for whole, part in zip(outs, others)]
        if step < count - 1:
            held = [lax.ppermute(part, "seq", route) for part in held]
    return [whole.reshape(value.shape) for whole, value in zip(outs, streams)]


def summary_kernel(x_ref, fade_ref, h_ref, p_ref):
    fade = fade_ref[...]
    states = fade.shape[0]

    def octet(i, carry):
        h, p = carry
        tile = x_ref[pl.ds(pl.multiple_of(i * 8, 8), 8), :]
        for r in range(8):
            row = jnp.broadcast_to(tile[r : r + 1, :], fade.shape)
            p = fade * (p + h)
            h = fade * h + row
        return h, p

    zero = jnp.zeros(fade.shape, jnp.float32)
    h, p = lax.fori_loop(0, x_ref.shape[0] // 8, octet, (zero, zero))
    h_ref[...] = h
    p_ref[...] = p


def tail_kernel(x_ref, fade_ref, gate_ref, skip_ref, first_ref, y_ref):
    fade, gate, skip = fade_ref[...], gate_ref[...], skip_ref[...]

    def octet(i, u):
        base = pl.multiple_of(i * 8, 8)
        tile = x_ref[pl.ds(base, 8), :]
        rows = []
        for r in range(8):
            row = tile[r : r + 1, :]
            u = fade * u + gate * jnp.broadcast_to(row, fade.shape)
            rows.append(jnp.sum(u, axis=0, keepdims=True) + skip * row)
        y_ref[pl.ds(base, 8), :] = jnp.concatenate(rows, 0)
        return u

    lax.fori_loop(0, x_ref.shape[0] // 8, octet, first_ref[...])


def tail_back_kernel(
    x_ref, d_ref, fade_ref, gate_ref, skip_ref, q_ref, r_ref, dh_ref, dp_ref, dskip_ref, dx_ref
):
    fade, gate, skip = fade_ref[...], gate_ref[...], skip_ref[...]
    octets = x_ref.shape[0] // 8
    zero = jnp.zeros(fade.shape, jnp.float32)

    def forward(i, carry):
        h, p, dh, dp = carry
        base = pl.multiple_of(i * 8, 8)
        tile, grads = x_ref[pl.ds(base, 8), :], d_ref[pl.ds(base, 8), :]
        for r in range(8):
            p = fade * (p + h)
            h = fade * h + jnp.broadcast_to(tile[r : r + 1, :], fade.shape)
            grad = jnp.broadcast_to(grads[r : r + 1, :], fade.shape)
            dh = dh + grad * h
            dp = dp + grad * p
        return h, p, dh, dp

    _, _, dh, dp = lax.fori_loop(0, octets, forward, (zero, zero, zero, zero))
    dh_ref[...] = dh
    dp_ref[...] = dp
    dskip_ref[...] = jnp.sum(x_ref[...] * d_ref[...], axis=0, keepdims=True)

    def backward(k, carry):
        q, r_sum = carry
        base = pl.multiple_of((octets - 1 - k) * 8, 8)
        grads = d_ref[pl.ds(base, 8), :]
        rows = [None] * 8
        for r in reversed(range(8)):
            r_sum = fade * (r_sum + q)
            grad = grads[r : r + 1, :]
            q = fade * q + jnp.broadcast_to(grad, fade.shape)
            rows[r] = jnp.sum(gate * q, axis=0, keepdims=True) + skip * grad
        dx_ref[pl.ds(base, 8), :] = jnp.concatenate(rows, 0)
        return q, r_sum

    q, r_sum = lax.fori_loop(0, octets, backward, (zero, zero))
    q_ref[...] = q
    r_ref[...] = r_sum


def spread_kernel(first_ref, fade_ref, y_ref):
    fade = fade_ref[...]
    octets = y_ref.shape[0] // 8

    def octet(k, v):
        base = pl.multiple_of((octets - 1 - k) * 8, 8)
        rows = [None] * 8
        for r in reversed(range(8)):
            v = fade * v
            rows[r] = jnp.sum(v, axis=0, keepdims=True)
        y_ref[pl.ds(base, 8), :] = jnp.concatenate(rows, 0)
        return v

    lax.fori_loop(0, octets, octet, first_ref[...])


def by_channels(kernel, ins, outs, flops):
    width = ins[0].shape[1]
    cut = 512 if width % 512 == 0 else width

    def spec(rows):
        return pl.BlockSpec((rows, cut), lambda i: (0, i))

    moved = sum(a.size for a in ins) + sum(r * width for r in outs)
    return pl.pallas_call(
        kernel,
        grid=(width // cut,),
        in_specs=[spec(a.shape[0]) for a in ins],
        out_specs=[spec(r) for r in outs],
        out_shape=[jax.ShapeDtypeStruct((r, width), jnp.float32) for r in outs],
        cost_estimate=pl.CostEstimate(flops=flops, bytes_accessed=4 * moved, transcendentals=0),
    )(*ins)


def attend(query, keys, values, allowed):
    rows, inner = query.shape
    heads = inner // HDIM
    outs, kept = [], []
    for head in range(heads):
        cols = slice(head * HDIM, (head + 1) * HDIM)
        scores = mm(query[:, cols], keys[:, cols], ((1,), (1,))) * HDIM ** (-0.5)
        scores = jnp.where(allowed, scores, -1e30)
        top = jnp.max(scores, axis=-1, keepdims=True)
        weight = jnp.exp(scores - top)
        probs = weight / jnp.sum(weight, axis=-1, keepdims=True)
        outs.append(mm(probs, values[:, cols]))
        kept.append(probs)
    return jnp.concatenate(outs, 1), kept


def attend_back(grad, query, keys, values, outs, kept):
    heads = len(kept)
    dq, dk, dv = [], [], []
    for head in range(heads):
        cols = slice(head * HDIM, (head + 1) * HDIM)
        probs, g = kept[head], grad[:, cols]
        dprobs = mm(g, values[:, cols], ((1,), (1,)))
        inner = jnp.sum(g * outs[:, cols], axis=-1, keepdims=True)
        dscores = probs * (dprobs - inner) * HDIM ** (-0.5)
        dq.append(mm(dscores, keys[:, cols]))
        dk.append(mm(dscores, query[:, cols], ((0,), (0,))))
        dv.append(mm(probs, g, ((0,), (0,))))
    return jnp.concatenate(dq, 1), jnp.concatenate(dk, 1), jnp.concatenate(dv, 1)


def per_device(
    tokens,
    window_state,
    norm1_gain,
    norm1_bias,
    in_coef,
    out_coef,
    decay_rate,
    skip_gain,
    qkv_weight,
    out_weight,
    norm2_gain,
    norm2_bias,
    up_weight,
    up_bias,
    down_weight,
    down_bias,
    cotangent,
):
    place_seq = lax.axis_index("seq")
    rows, width = tokens.shape
    channels, states = in_coef.shape
    windows = window_state.shape[0]
    per_window = LEN // rows
    block = place_seq % per_window
    window = place_seq // per_window
    has_ctx = block > 0

    qkv = qkv_weight.astype(jnp.float32)
    out_own = out_weight.astype(jnp.float32)
    up = up_weight.astype(jnp.float32)
    down = down_weight.astype(jnp.float32)

    packed = jnp.concatenate(
        [decay_rate, in_coef, out_coef, skip_gain[:, None]] + [window_state[w] for w in range(windows)],
        1,
    )
    used = packed.shape[1]
    packed = jnp.pad(packed, ((0, 0), (0, -used % 128)))
    coefs = jnp.transpose(gather_all(packed))
    decay = coefs[:states]
    c_in = coefs[states : 2 * states]
    c_out = coefs[2 * states : 3 * states]
    skip = coefs[3 * states : 3 * states + 1]
    carried = lax.dynamic_slice_in_dim(coefs, 3 * states + 1 + window * states, states, 0)
    fade = jnp.exp(-decay)

    tail_tokens = shift_to(tokens[rows - CTX :], "seq", 1)

    unit1, rate1 = norm_parts(tokens)
    normed = unit1 * norm1_gain + norm1_bias
    tail_unit, _ = norm_parts(tail_tokens)
    tail = jnp.where(has_ctx, tail_unit * norm1_gain + norm1_bias, 0.0)
    segment = jnp.concatenate([tail, normed[: rows - CTX]], 0)

    sum_h, sum_p = by_channels(summary_kernel, [segment, fade], [states, states], 5 * segment.size * states)
    length = float(rows)
    before = jnp.zeros((2, states, width), jnp.float32)
    total = jnp.stack([sum_h, sum_p])

    def shifted(pair, steps):
        gone = jnp.exp(-decay * steps)
        return jnp.stack([gone * pair[0], gone * (pair[1] + steps * pair[0])])

    for bit in range(bits_of(per_window)):
        other = swap_bit(total, "seq", bit)
        upper = ((block >> bit) & 1) == 1
        behind = (block & ((1 << bit) - 1)).astype(jnp.float32) * length
        before = jnp.where(upper, shifted(other, behind) + before, before)
        left = jnp.where(upper, other, total)
        right = jnp.where(upper, total, other)
        total = shifted(left, length * (1 << bit)) + right
    past_h, past_p = before[0], before[1]
    start_t = jnp.maximum(block * rows - CTX, 0).astype(jnp.float32)
    gate = c_in * c_out
    first = c_out * (c_in * past_h + carried * jnp.exp(-decay * start_t))
    (context,) = by_channels(
        tail_kernel, [tail, fade, gate, skip, first], [CTX], 5 * CTX * width * states
    )

    query = mm(normed, qkv[0])
    key_self = mm(normed, qkv[1])
    value_self = mm(normed, qkv[2])
    key_ctx = mm(context, qkv[1])
    value_ctx = mm(context, qkv[2])
    keys = jnp.concatenate([key_ctx, key_self], 0)
    values = jnp.concatenate([value_ctx, value_self], 0)
    rows_q = jnp.arange(rows)[:, None]
    cols_k = jnp.arange(CTX + rows)[None, :]
    allowed = jnp.where(cols_k < CTX, has_ctx, cols_k - CTX <= rows_q)
    heads, kept = attend(query, keys, values, allowed)
    attn_part = mm(heads, out_own)
    mixed = tokens + (attn_part + swap_bit(attn_part, "mp", 0))

    unit2, rate2 = norm_parts(mixed)
    normed2 = unit2 * norm2_gain + norm2_bias
    pre = mm(normed2, up) + up_bias
    cdf = 0.5 * lax.erfc(pre * (-(0.5**0.5)))
    hidden = pre * cdf
    slope = cdf + pre * (jnp.exp(-0.5 * pre * pre) * (1.0 / math.sqrt(2.0 * math.pi)))
    grad_pre = mm(cotangent, down, ((1,), (1,))) * slope
    grad_down = mm(hidden, cotangent, ((0,), (0,)))
    grad_normed2_part = mm(grad_pre, up, ((1,), (1,)))
    grad_up = mm(normed2, grad_pre, ((0,), (0,)))
    grad_up_bias = jnp.sum(grad_pre, axis=0)
    grad_down_bias = jnp.sum(cotangent, axis=0)
    feed_part = mm(hidden, down)
    result = mixed + (feed_part + swap_bit(feed_part, "mp", 0)) + down_bias
    grad_up_sum, grad_down_sum = ring_sum([grad_up, grad_down])

    grad_normed2 = grad_normed2_part + swap_bit(grad_normed2_part, "mp", 0)
    grad_gain2 = jnp.sum(grad_normed2 * unit2, axis=0)
    grad_bias2 = jnp.sum(grad_normed2, axis=0)
    grad_mixed = cotangent + norm_back(grad_normed2, unit2, rate2, norm2_gain)

    grad_heads = mm(grad_mixed, out_own, ((1,), (1,)))
    grad_out_t = mm(grad_mixed, heads, ((0,), (0,)))
    dq, dk, dv = attend_back(grad_heads, query, keys, values, heads, kept)
    grad_context = mm(dk[:CTX], qkv[1], ((1,), (1,))) + mm(dv[:CTX], qkv[2], ((1,), (1,)))
    grad_context = jnp.where(has_ctx, grad_context, 0.0)
    grad_normed_part = (
        mm(dq, qkv[0], ((1,), (1,)))
        + mm(dk[CTX:], qkv[1], ((1,), (1,)))
        + mm(dv[CTX:], qkv[2], ((1,), (1,)))
    )
    grad_q = mm(normed, dq, ((0,), (0,)))
    seen = jnp.concatenate([context, normed], 0)
    grad_k = mm(seen, dk, ((0,), (0,)))
    grad_v = mm(seen, dv, ((0,), (0,)))
    (attn_sum,) = ring_sum([jnp.concatenate([grad_q, grad_k, grad_v, grad_out_t], 1)])
    inner = grad_q.shape[1]
    grad_qkv_sum = jnp.stack([attn_sum[:, i * inner : (i + 1) * inner] for i in range(3)])
    grad_out_sum = jnp.transpose(attn_sum[:, 3 * inner :])

    sum_q, sum_r, part_h, part_p, part_skip, grad_tail = by_channels(
        tail_back_kernel,
        [tail, grad_context, fade, gate, skip],
        [states, states, states, states, 1, CTX],
        20 * CTX * width * states,
    )
    along_h = fade * past_h * sum_q + part_h
    along_p = fade * (past_h * (sum_r + sum_q) + past_p * sum_q) + part_p
    faded = jnp.exp(-decay * (start_t + 1.0))
    part_in = c_out * along_h
    part_out = c_in * along_h + carried * faded * sum_q
    part_decay = -gate * along_p - c_out * carried * faded * ((start_t + 1.0) * sum_q + sum_r)
    stacked = jnp.concatenate([part_in, part_out, part_decay, part_skip], 0)
    stacked = jnp.pad(stacked, ((0, -stacked.shape[0] % 128), (0, 0)))
    own = scatter_sum(jnp.transpose(stacked))
    grad_in = own[:, :states]
    grad_out_coef = own[:, states : 2 * states]
    grad_decay = own[:, 2 * states : 3 * states]
    grad_skip = own[:, 3 * states]

    after = jnp.zeros((states, width), jnp.float32)
    total_q = sum_q
    for bit in range(bits_of(per_window)):
        other = swap_bit(total_q, "seq", bit)
        upper = ((block >> bit) & 1) == 1
        ahead = ((1 << bit) - 1 - (block & ((1 << bit) - 1))).astype(jnp.float32) * length
        after = jnp.where(upper, after, after + jnp.exp(-decay * ahead) * other)
        left = jnp.where(upper, other, total_q)
        right = jnp.where(upper, total_q, other)
        total_q = left + jnp.exp(-decay * (length * (1 << bit))) * right
    (grad_segment,) = by_channels(
        spread_kernel, [gate * after, fade], [rows], 4 * rows * width * states
    )
    to_last = jnp.where(has_ctx, grad_segment[:CTX] + grad_tail, 0.0)
    from_next = shift_to(to_last, "seq", -1)
    grad_states = jnp.concatenate([grad_segment[CTX:], from_next], 0)

    grad_normed_half = grad_normed_part + grad_states
    grad_normed = grad_normed_half + swap_bit(grad_normed_half, "mp", 0)
    grad_gain1 = jnp.sum(grad_normed * unit1, axis=0)
    grad_bias1 = jnp.sum(grad_normed, axis=0)
    grad_tokens = grad_mixed + norm_back(grad_normed, unit1, rate1, norm1_gain)

    early = sum_seq_small(
        jnp.concatenate([grad_gain2, grad_bias2, grad_down_bias, grad_up_bias]).reshape(-1, width)
    )
    late = sum_seq_small(jnp.stack([grad_gain1, grad_bias1]))
    return (
        result,
        grad_tokens,
        late[0],
        late[1],
        grad_in,
        grad_out_coef,
        grad_decay,
        grad_skip,
        grad_qkv_sum,
        grad_out_sum,
        early[0],
        early[1],
        grad_up_sum,
        early[3:].reshape(-1),
        grad_down_sum,
        early[2],
    )


def solution(mesh):
    owner = P(("seq", "mp"), None)
    return jax.shard_map(
        per_device,
        mesh=mesh,
        in_specs=(
            P("seq", None),
            P(None, ("seq", "mp"), None),
            P(),
            P(),
            owner,
            owner,
            owner,
            P(("seq", "mp")),
            P(None, None, "mp"),
            P("mp", None),
            P(),
            P(),
            P(None, "mp"),
            P("mp"),
            P("mp", None),
            P(),
            P("seq", None),
        ),
        out_specs=(
            P("seq", None),
            P("seq", None),
            P(),
            P(),
            owner,
            owner,
            owner,
            P(("seq", "mp")),
            P(None, None, "mp"),
            P("mp", None),
            P(),
            P(),
            P(None, "mp"),
            P("mp"),
            P("mp", None),
            P(),
        ),
        check_vma=False,
    )
```

time: 1200 us -> 743 us (0.62)
  waiting for transfers between devices: 590 us -> 329 us
  matrix products: 308 us -> 119 us
  blocking collectives: 128 us -> 0 us
  starting transfers between devices: 16.5 us -> 95.2 us
  other arithmetic: 34.4 us -> 72 us
  Pallas kernels: 0 us -> 26.7 us
    psum x4 -> x0, waiting for transfers between devices: 496 us -> none  [the longest x1 366 us: per_device(): lax.psum((grad_gain1, grad_bias1, grad_qkv, grad_out, grad_gain2, grad_bi...]
    ppermute x2 -> x99, waiting for transfers between devices: 2.51 us -> 329 us  [the longest x55 154 us: swap_bit(): return lax.ppermute(value, axis, [(i, i ^ 1 << bit) for i in range(size)])]
    dot_general x71 -> x46, matrix products: 308 us -> 119 us  [mm(): lax.dot_general(left, right, (dims, ((), ())), precision=HIGH, preferred_...]
    ppermute x2 -> x99, starting transfers between devices: 3.28 us -> 95.2 us  [the longest x21 34.3 us: ring_sum(): got = [lax.ppermute(part, 'seq', route) for part in held]]
    unnamed x7 -> x0, waiting for transfers between devices: 68.1 us -> none
    psum x1 -> x0, blocking collectives: 65.8 us -> none  [per_device(): lax.psum((grad_gain1, grad_bias1, grad_qkv, grad_out, grad_gain2, grad_bi...]
    all_to_all x2 -> x0, blocking collectives: 61.9 us -> none  [the longest x1 31.6 us: per_device(): lax.all_to_all(time_out, 'seq', split_axis=1, concat_axis=0, tiled=True)]
    dynamic_slice x0 -> x8, local copies, waits for them, and re-layouts: none -> 35.3 us  [the longest x3 33.8 us: pick(): return lax.dynamic_index_in_dim(value, index, 0, keepdims=False)]
  transfers between devices with their start and end apart: 10 -> 99, of which waited for: 7 -> 57; matrix products, arithmetic and copies ran while one was open for 15% -> 26% of each run, Pallas kernels for 0% -> 2%
where the time goes in v1:
time: 743 us; the launch traced here: 736 us
  waiting for transfers between devices  329 us (44%)
  matrix products  119 us (16%)
  starting transfers between devices  95.2 us (13%)
  local copies, waits for them, and re-layouts  88.3 us (12%)
  other arithmetic  72 us (10%)
  Pallas kernels  26.7 us (4%)
    ppermute x55, waiting for transfers between devices, swap_bit(): return lax.ppermute(value, axis, [(i, i ^ 1 << bit) for i in range(size)])  154 us
    dot_general x46, matrix products, mm(): lax.dot_general(left, right, (dims, ((), ())), precision=HIGH, preferred_...  119 us
    ppermute x21, waiting for transfers between devices, ring_sum(): held = [lax.ppermute(part, 'seq', route) for part in held]  105 us
    ppermute x21, waiting for transfers between devices, ring_sum(): got = [lax.ppermute(part, 'seq', route) for part in held]  69.5 us
    ppermute x21, starting transfers between devices, ring_sum(): got = [lax.ppermute(part, 'seq', route) for part in held]  34.3 us
    ppermute x55, starting transfers between devices, swap_bit(): return lax.ppermute(value, axis, [(i, i ^ 1 << bit) for i in range(size)])  34.2 us
    dynamic_slice x3, local copies, waits for them, and re-layouts, pick(): return lax.dynamic_index_in_dim(value, index, 0, keepdims=False)  33.8 us
    pallas_call x4, Pallas kernels, by_channels(): pl.pallas_call(kernel, grid=(width // cut,), in_specs=[spec(a.shape[0]) f...  26.7 us
  transfers between devices with their start and end apart: 99, of which 57 were waited for; matrix products, arithmetic and copies ran while one was open for 26% of the time, Pallas kernels for 2%

profile of v1, /device:TPU:0, one launch (start us, length us, event | category | flops | bytes accessed | tf_op | source)
XLA Modules:
  0.0 735.7 jit_solution(12993502470634151058)
XLA Ops:
  31.9 7.0 collective-permute-done.5
  46.4 6.5 shard_map.306
  77.9 4.6 shard_map.307
  104.7 42.7 %collective-permute-done.9 = f32[512,1024]{1,0:T(8,128)} collective-permute-done((f32[512,1024]{1,0:T(8,128)}, f32[512,1024]{1,0:T(8,128)}, u32[]{:S(2)}, u32[]{:S(2)}) %collective-permute-start.9) | collective-permute-done | bytes 2097184 | tf_op jit(solution)/shard_map/ppermute | solution.py:40
  151.0 12.9 %fusion.1 = (f32[512,2048]{1,0:T(8,128)S(1)}, f32[512,2048]{1,0:T(8,128)S(1)}) fusion(f32[2048]{0:T(1024)S(1)} %copy-done.58, bf16[1024,2048]{1,0:T(8,128)(2,1)S(1)} %copy-done.73, f32[512,1024]{1,0:T(8,128)S(1)} %get-tuple-element.149, f32[1024]{0:T(1024)S(1)} %copy-done.74, f32[1024]{0:T(1024)S(1)} %copy-done.70, f32[512]{0:T(512)S(1)} %add_rsqrt_fusion, ...), kind=kOutput, calls=%fused_computation.5 | convolution fusion | flops 6510608384 | bytes 14700544 | tf_op jit(solution)/shard_map/dot_general | solution.py:20
  163.9 6.8 fusion.196
  170.7 9.3 %fusion.198 = f32[512,1024]{1,0:T(8,128)} fusion(f32[512,2048]{1,0:T(8,128)} %get-tuple-element.203, bf16[1024,2048]{1,0:T(8,128)(2,1)} %param.31), kind=kOutput, calls=%fused_computation.422 | convolution fusion | flops 6442450944 | bytes 10485760 | tf_op jit(solution)/shard_map/dot_general | solution.py:20
  186.7 8.1 %fusion.15 = f32[1024,2048]{1,0:T(8,128)S(1)} fusion(f32[512,2048]{1,0:T(8,128)S(1)} %copy-done.38, f32[512,1024]{1,0:T(8,128)S(1)} %get-tuple-element.149, f32[1024]{0:T(1024)S(1)} %copy-done.74, f32[1024]{0:T(1024)S(1)} %copy-done.70, f32[512]{0:T(512)S(1)} %add_rsqrt_fusion, f32[512]{0:T(512)S(1)} %broadcast_multiply_fusion.4), kind=kOutput, calls=%fused_computation.59 | convolution fusion | flops 6444548096 | bytes 14692352 | tf_op jit(solution)/shard_map/dot_general | solution.py:20
  199.4 7.6 %fusion.17 = f32[2048,1024]{1,0:T(8,128)S(1)} fusion(f32[512,1024]{1,0:T(8,128)S(1)} %copy-done.21, f32[512,2048]{1,0:T(8,128)S(1)} %get-tuple-element.200, f32[512,2048]{1,0:T(8,128)S(1)} %get-tuple-element.201, f32[2048]{0:T(1024)S(1)} %copy-done.58), kind=kOutput, calls=%fused_computation.63 | convolution fusion | flops 6444548096 | bytes 18882560 | tf_op jit(solution)/shard_map/dot_general | solution.py:20
  212.0 16.9 %collective-permute-done.11 = f32[512,1024]{1,0:T(8,128)} collective-permute-done((f32[512,1024]{1,0:T(8,128)}, f32[512,1024]{1,0:T(8,128)}, u32[]{:S(2)}, u32[]{:S(2)}) %collective-permute-start.11) | collective-permute-done | bytes 2097184 | tf_op jit(solution)/shard_map/ppermute | solution.py:40
  232.3 38.4 %collective-permute-done.10 = f32[512,1024]{1,0:T(8,128)S(1)} collective-permute-done((f32[512,1024]{1,0:T(8,128)S(1)}, f32[512,1024]{1,0:T(8,128)S(1)}, u32[]{:S(2)}, u32[]{:S(2)}) %collective-permute-start.10) | collective-permute-done | bytes 2097184 | tf_op jit(solution)/shard_map/ppermute | solution.py:40
  313.3 7.6 %shard_map.308 = (f32[16,1024]{1,0:T(8,128)}, f32[16,1024]{1,0:T(8,128)}, f32[16,1024]{1,0:T(8,128)}, f32[16,1024]{1,0:T(8,128)}, f32[1,1024]{1,0:T(1,128)}, /*index=5*/f32[128,1024]{1,0:T(8,128)}) custom-call(f32[128,1024]{1,0:T(8,128)} %copy-done.29, f32[128,1024]{1,0:T(8,128)} %fusion.32.d_ref, f32[16,1024]{1,0:T(8,128)} %fusion.186.fade_ref, ...), custom_call_target="tpu_custom_call" | custom-call | flops 41943040 | bytes 1974272 | tf_op jit(solution)/shard_map/pallas_call | solution.py:248
  321.1 5.4 fusion.42
  334.2 6.0 pad_maximum_fusion
  340.3 11.7 %reshape.165 = f32[2,512,2048]{1,0,2:T(2,128)} reshape(f32[1024,2048]{0,1:T(8,128)} %pad_maximum_fusion) | data formatting | bytes 16777216 | tf_op jit(solution)/shard_map/reshape | solution.py:123
  353.7 12.1 %constant_dynamic-slice_fusion.1 = (f32[1,512,2048]{1,0,2:T(1,128)}, f32[1,512,2048]{1,0,2:T(1,128)}) fusion(f32[2,512,2048]{1,0,2:T(2,128)} %reshape.165, s32[]{:T(128)S(6)} %select_n.721, s32[]{:T(128)S(6)} %select_n.722), kind=kLoop, calls=%fused_computation.366 | loop fusion | bytes 16777224 | tf_op jit(solution)/shard_map/jit(dynamic_index_in_dim)/dynamic_slice | solution.py:105
  365.8 10.9 %copy.76 = f32[1,512,2048]{2,1,0:T(8,128)} copy(f32[1,512,2048]{1,0,2:T(1,128)} %get-tuple-element.155) | data formatting | bytes 8388608 | tf_op jit(solution)/shard_map/jit(dynamic_index_in_dim)/dynamic_slice | solution.py:105
  376.6 10.9 %copy.75 = f32[1,512,2048]{2,1,0:T(8,128)} copy(f32[1,512,2048]{1,0,2:T(1,128)} %get-tuple-element.154) | data formatting | bytes 8388608 | tf_op jit(solution)/shard_map/jit(dynamic_index_in_dim)/dynamic_slice | solution.py:105
  405.0 7.9 %shard_map.309 = f32[512,1024]{1,0:T(8,128)} custom-call(f32[16,1024]{1,0:T(8,128)} %fusion.128.first_ref, f32[16,1024]{1,0:T(8,128)} %fusion.186.fade_ref), custom_call_target="tpu_custom_call" | custom-call | flops 33554432 | bytes 2228224 | tf_op jit(solution)/shard_map/pallas_call | solution.py:248
  419.8 5.9 maximum_add_fusion
  434.3 6.4 collective-permute-start.54
  450.0 19.8 %collective-permute-done.16 = f32[512,1024]{1,0:T(8,128)} collective-permute-done((f32[512,1024]{1,0:T(8,128)}, f32[512,1024]{1,0:T(8,128)}, u32[]{:S(2)}, u32[]{:S(2)}) %collective-permute-start.16) | collective-permute-done | bytes 2097184 | tf_op jit(solution)/shard_map/ppermute | solution.py:40
  473.1 4.6 collective-permute-start.17
  477.8 5.3 collective-permute-start.78
  484.0 6.6 collective-permute-done.18
  617.0 4.6 collective-permute-done.89
  683.4 5.6 collective-permute-done.97
  689.3 5.4 collective-permute-done.41
  695.9 7.9 %collective-permute-done.43 = f32[64,2048]{1,0:T(8,128)S(1)} collective-permute-done((f32[64,2048]{1,0:T(8,128)S(1)}, f32[64,2048]{1,0:T(8,128)S(1)}, u32[]{:S(2)}, u32[]{:S(2)}) %collective-permute-start.43) | collective-permute-done | bytes 524320 | tf_op jit(solution)/shard_map/ppermute | solution.py:142
  705.0 8.0 %collective-permute-done.45 = f32[64,2048]{1,0:T(8,128)S(1)} collective-permute-done((f32[64,2048]{1,0:T(8,128)S(1)}, f32[64,2048]{1,0:T(8,128)S(1)}, u32[]{:S(2)}, u32[]{:S(2)}) %collective-permute-start.45) | collective-permute-done | bytes 524320 | tf_op jit(solution)/shard_map/ppermute | solution.py:142
  714.3 7.9 %collective-permute-done.47 = f32[64,2048]{1,0:T(8,128)S(1)} collective-permute-done((f32[64,2048]{1,0:T(8,128)S(1)}, f32[64,2048]{1,0:T(8,128)S(1)}, u32[]{:S(2)}, u32[]{:S(2)}) %collective-permute-start.47) | collective-permute-done | bytes 524320 | tf_op jit(solution)/shard_map/ppermute | solution.py:142
  728.9 6.4 pad_maximum_fusion.1
  (557 shorter events, 403.1 us)
Async XLA Ops:
  2.7 37.6 %collective-permute-start = (f32[128,1024]{1,0:T(8,128)}, f32[128,1024]{1,0:T(8,128)}, u32[]{:S(2)}, u32[]{:S(2)}) collective-permute-start(f32[128,1024]{1,0:T(8,128)} %slice.203), channel_id=1, source_target_pairs={{0,2},{2,4},{4,6},{6,8},{8,10},{10,12},{12,14},{14,16},{16,18},{18... | collective-permute-start | bytes 1572872 | tf_op jit(solution)/shard_map/ppermute | solution.py:50
  100.7 46.7 %collective-permute-start.9 = (f32[512,1024]{1,0:T(8,128)}, f32[512,1024]{1,0:T(8,128)}, u32[]{:S(2)}, u32[]{:S(2)}) collective-permute-start(f32[512,1024]{1,0:T(8,128)} %fusion.81), channel_id=1, source_target_pairs={{0,1},{1,0},{2,3},{3,2},{4,5},{5,4},{6,7},{7,6},{8,9},{9,8},{10,11... | collective-permute-start | bytes 6291464 | tf_op jit(solution)/shard_map/ppermute | solution.py:40
  180.0 48.9 %collective-permute-start.11 = (f32[512,1024]{1,0:T(8,128)}, f32[512,1024]{1,0:T(8,128)}, u32[]{:S(2)}, u32[]{:S(2)}) collective-permute-start(f32[512,1024]{1,0:T(8,128)} %fusion.198), channel_id=1, source_target_pairs={{0,1},{1,0},{2,3},{3,2},{4,5},{5,4},{6,7},{7,6},{8,9},{9,8},{10,11... | collective-permute-start | bytes 6291464 | tf_op jit(solution)/shard_map/ppermute | solution.py:40
  186.1 84.5 %collective-permute-start.10 = (f32[512,1024]{1,0:T(8,128)S(1)}, f32[512,1024]{1,0:T(8,128)S(1)}, u32[]{:S(2)}, u32[]{:S(2)}) collective-permute-start(f32[512,1024]{1,0:T(8,128)S(1)} %fusion.18), channel_id=1, source_target_pairs={{0,1},{1,0},{2,3},{3,2},{4,5},{5,4},{6,7},{7,6},{8,9},{9,8},{10,11... | collective-permute-start | bytes 6291464 | tf_op jit(solution)/shard_map/ppermute | solution.py:40
  199.4 230.6 %collective-permute-start.53 = (f32[512,2048]{1,0:T(8,128)}, f32[512,2048]{1,0:T(8,128)}, u32[]{:S(2)}, u32[]{:S(2)}) collective-permute-start(f32[512,2048]{1,0:T(8,128)} %dynamic-slice_bitcast_fusion.1), channel_id=1, source_target_pairs={{0,2},{2,0},{4,6},{6,4},{8,10},{10,8},{12,14},{14,12},{16,18},{18,... | collective-permute-start | bytes 12582920 | tf_op jit(solution)/shard_map/ppermute | solution.py:40
  211.5 229.2 %collective-permute-start.76 = (f32[1024,1024]{1,0:T(8,128)}, f32[1024,1024]{1,0:T(8,128)}, u32[]{:S(2)}, u32[]{:S(2)}) collective-permute-start(f32[1024,1024]{1,0:T(8,128)} %dynamic-slice_bitcast_fusion), channel_id=1, source_target_pairs={{0,2},{2,0},{4,6},{6,4},{8,10},{10,8},{12,14},{14,12},{16,18},{18,... | collective-permute-start | bytes 12582920 | tf_op jit(solution)/shard_map/ppermute | solution.py:40
  321.1 67.3 %collective-permute-start.12 = (f32[16,1024]{1,0:T(8,128)}, f32[16,1024]{1,0:T(8,128)}, u32[]{:S(2)}, u32[]{:S(2)}) collective-permute-start(f32[16,1024]{1,0:T(8,128)} %get-tuple-element.26), channel_id=1, source_target_pairs={{0,2},{2,0},{4,6},{6,4},{8,10},{10,8},{12,14},{14,12},{16,18},{18,... | collective-permute-start | bytes 196616 | tf_op jit(solution)/shard_map/ppermute | solution.py:40
  330.6 65.2 %collective-permute-start.21 = (f32[512,128]{0,1:T(8,128)S(1)}, f32[512,128]{0,1:T(8,128)S(1)}, u32[]{:S(2)}, u32[]{:S(2)}) collective-permute-start(f32[512,128]{0,1:T(8,128)S(1)} %bitcast.479), channel_id=1, source_target_pairs={{0,16},{2,18},{4,20},{6,22},{8,24},{10,26},{12,28},{14,30},{16,0},... | collective-permute-start | bytes 786440 | tf_op jit(solution)/shard_map/ppermute | solution.py:40
  333.5 18.5 %collective-permute-start.50 = (f32[5,1024]{1,0:T(8,128)S(1)}, f32[5,1024]{1,0:T(8,128)S(1)}, u32[]{:S(2)}, u32[]{:S(2)}) collective-permute-start(f32[5,1024]{1,0:T(8,128)S(1)} %add.1207), channel_id=1, source_target_pairs={{0,4},{2,6},{4,0},{6,2},{8,12},{10,14},{12,8},{14,10},{16,20},{18,... | collective-permute-start | bytes 61448 | tf_op jit(solution)/shard_map/ppermute | solution.py:40
  352.6 34.9 %collective-permute-start.51 = (f32[5,1024]{1,0:T(8,128)}, f32[5,1024]{1,0:T(8,128)}, u32[]{:S(2)}, u32[]{:S(2)}) collective-permute-start(f32[5,1024]{1,0:T(8,128)} %add.1208), channel_id=1, source_target_pairs={{0,8},{2,10},{4,12},{6,14},{8,0},{10,2},{12,4},{14,6},{16,24},{18,... | collective-permute-start | bytes 61448 | tf_op jit(solution)/shard_map/ppermute | solution.py:40
  387.5 122.8 %collective-permute-start.26 = (f32[512,2048]{1,0:T(8,128)}, f32[512,2048]{1,0:T(8,128)}, u32[]{:S(2)}, u32[]{:S(2)}) collective-permute-start(f32[512,2048]{1,0:T(8,128)} %bitcast.464), channel_id=1, source_target_pairs={{0,2},{2,0},{4,6},{6,4},{8,10},{10,8},{12,14},{14,12},{16,18},{18,... | collective-permute-start | bytes 12582920 | tf_op jit(solution)/shard_map/ppermute | solution.py:40
  425.7 44.1 %collective-permute-start.16 = (f32[512,1024]{1,0:T(8,128)}, f32[512,1024]{1,0:T(8,128)}, u32[]{:S(2)}, u32[]{:S(2)}) collective-permute-start(f32[512,1024]{1,0:T(8,128)} %maximum_add_fusion), channel_id=1, source_target_pairs={{0,1},{1,0},{2,3},{3,2},{4,5},{5,4},{6,7},{7,6},{8,9},{9,8},{10,11... | collective-permute-start | bytes 6291464 | tf_op jit(solution)/shard_map/ppermute | solution.py:40
  445.2 32.5 %collective-permute-start.77 = (f32[128,1024]{1,0:T(8,128)S(1)}, f32[128,1024]{1,0:T(8,128)S(1)}, u32[]{:S(2)}, u32[]{:S(2)}) collective-permute-start(f32[128,1024]{1,0:T(8,128)S(1)} %dynamic-slice_bitcast_fusion.2), channel_id=1, source_target_pairs={{0,8},{10,2},{8,16},{18,10},{16,24},{26,18},{24,28},{30,26},{28,20... | collective-permute-start | bytes 1572872 | tf_op jit(solution)/shard_map/ppermute | solution.py:128
  447.5 46.9 %collective-permute-start.55 = (f32[64,2048]{1,0:T(8,128)S(1)}, f32[64,2048]{1,0:T(8,128)S(1)}, u32[]{:S(2)}, u32[]{:S(2)}) collective-permute-start(f32[64,2048]{1,0:T(8,128)S(1)} %bitcast_add_fusion.16), channel_id=1, source_target_pairs={{0,8},{10,2},{8,16},{18,10},{16,24},{26,18},{24,28},{30,26},{28,20... | collective-permute-start | bytes 1572872 | tf_op jit(solution)/shard_map/ppermute | solution.py:128
  531.8 16.8 %collective-permute-start.59 = (f32[64,2048]{1,0:T(8,128)S(1)}, f32[64,2048]{1,0:T(8,128)S(1)}, u32[]{:S(2)}, u32[]{:S(2)}) collective-permute-start(f32[64,2048]{1,0:T(8,128)S(1)} %bitcast_add_fusion.12), channel_id=1, source_target_pairs={{0,8},{10,2},{8,16},{18,10},{16,24},{26,18},{24,28},{30,26},{28,20... | collective-permute-start | bytes 1572872 | tf_op jit(solution)/shard_map/ppermute | solution.py:128
  548.7 16.8 %collective-permute-start.60 = (f32[64,2048]{1,0:T(8,128)S(1)}, f32[64,2048]{1,0:T(8,128)S(1)}, u32[]{:S(2)}, u32[]{:S(2)}) collective-permute-start(f32[64,2048]{1,0:T(8,128)S(1)} %bitcast_add_fusion.11), channel_id=1, source_target_pairs={{0,8},{10,2},{8,16},{18,10},{16,24},{26,18},{24,28},{30,26},{28,20... | collective-permute-start | bytes 1572872 | tf_op jit(solution)/shard_map/ppermute | solution.py:128
  559.9 16.8 %collective-permute-start.30 = (f32[64,2048]{1,0:T(8,128)S(1)}, f32[64,2048]{1,0:T(8,128)S(1)}, u32[]{:S(2)}, u32[]{:S(2)}) collective-permute-start(f32[64,2048]{1,0:T(8,128)S(1)} %bitcast_add_fusion.21), channel_id=1, source_target_pairs={{0,8},{10,2},{8,16},{18,10},{16,24},{26,18},{24,28},{30,26},{28,20... | collective-permute-start | bytes 1572872 | tf_op jit(solution)/shard_map/ppermute | solution.py:128
  576.8 16.8 %collective-permute-start.31 = (f32[64,2048]{1,0:T(8,128)S(1)}, f32[64,2048]{1,0:T(8,128)S(1)}, u32[]{:S(2)}, u32[]{:S(2)}) collective-permute-start(f32[64,2048]{1,0:T(8,128)S(1)} %bitcast_add_fusion.20), channel_id=1, source_target_pairs={{0,8},{10,2},{8,16},{18,10},{16,24},{26,18},{24,28},{30,26},{28,20... | collective-permute-start | bytes 1572872 | tf_op jit(solution)/shard_map/ppermute | solution.py:128
  582.3 16.9 %collective-permute-start.63 = (f32[64,2048]{1,0:T(8,128)S(1)}, f32[64,2048]{1,0:T(8,128)S(1)}, u32[]{:S(2)}, u32[]{:S(2)}) collective-permute-start(f32[64,2048]{1,0:T(8,128)S(1)} %collective-permute-done.62), channel_id=1, source_target_pairs={{0,2},{2,0},{4,6},{6,4},{8,10},{10,8},{12,14},{14,12},{16,18},{18,... | collective-permute-start | bytes 1572872 | tf_op jit(solution)/shard_map/ppermute | solution.py:40
  582.3 16.8 %collective-permute-start.64 = (f32[64,2048]{1,0:T(8,128)S(1)}, f32[64,2048]{1,0:T(8,128)S(1)}, u32[]{:S(2)}, u32[]{:S(2)}) collective-permute-start(f32[64,2048]{1,0:T(8,128)S(1)} %collective-permute-done.62), channel_id=1, source_target_pairs={{0,8},{10,2},{8,16},{18,10},{16,24},{26,18},{24,28},{30,26},{28,20... | collective-permute-start | bytes 1572872 | tf_op jit(solution)/shard_map/ppermute | solution.py:142
  587.9 17.0 %collective-permute-start.86 = (f32[128,1024]{1,0:T(8,128)S(1)}, f32[128,1024]{1,0:T(8,128)S(1)}, u32[]{:S(2)}, u32[]{:S(2)}) collective-permute-start(f32[128,1024]{1,0:T(8,128)S(1)} %collective-permute-done.85), channel_id=1, source_target_pairs={{0,2},{2,0},{4,6},{6,4},{8,10},{10,8},{12,14},{14,12},{16,18},{18,... | collective-permute-start | bytes 1572872 | tf_op jit(solution)/shard_map/ppermute | solution.py:40
  593.6 16.8 %collective-permute-start.32 = (f32[64,2048]{1,0:T(8,128)S(1)}, f32[64,2048]{1,0:T(8,128)S(1)}, u32[]{:S(2)}, u32[]{:S(2)}) collective-permute-start(f32[64,2048]{1,0:T(8,128)S(1)} %bitcast_add_fusion.19), channel_id=1, source_target_pairs={{0,8},{10,2},{8,16},{18,10},{16,24},{26,18},{24,28},{30,26},{28,20... | collective-permute-start | bytes 1572872 | tf_op jit(solution)/shard_map/ppermute | solution.py:128
  599.2 16.9 %collective-permute-start.65 = (f32[64,2048]{1,0:T(8,128)S(1)}, f32[64,2048]{1,0:T(8,128)S(1)}, u32[]{:S(2)}, u32[]{:S(2)}) collective-permute-start(f32[64,2048]{1,0:T(8,128)S(1)} %collective-permute-done.64), channel_id=1, source_target_pairs={{0,2},{2,0},{4,6},{6,4},{8,10},{10,8},{12,14},{14,12},{16,18},{18,... | collective-permute-start | bytes 1572872 | tf_op jit(solution)/shard_map/ppermute | solution.py:40
  599.2 16.8 %collective-permute-start.66 = (f32[64,2048]{1,0:T(8,128)S(1)}, f32[64,2048]{1,0:T(8,128)S(1)}, u32[]{:S(2)}, u32[]{:S(2)}) collective-permute-start(f32[64,2048]{1,0:T(8,128)S(1)} %collective-permute-done.64), channel_id=1, source_target_pairs={{0,8},{10,2},{8,16},{18,10},{16,24},{26,18},{24,28},{30,26},{28,20... | collective-permute-start | bytes 1572872 | tf_op jit(solution)/shard_map/ppermute | solution.py:142
  604.8 17.0 %collective-permute-start.88 = (f32[128,1024]{1,0:T(8,128)S(1)}, f32[128,1024]{1,0:T(8,128)S(1)}, u32[]{:S(2)}, u32[]{:S(2)}) collective-permute-start(f32[128,1024]{1,0:T(8,128)S(1)} %collective-permute-done.87), channel_id=1, source_target_pairs={{0,2},{2,0},{4,6},{6,4},{8,10},{10,8},{12,14},{14,12},{16,18},{18,... | collective-permute-start | bytes 1572872 | tf_op jit(solution)/shard_map/ppermute | solution.py:40
  610.5 16.8 %collective-permute-start.33 = (f32[64,2048]{1,0:T(8,128)S(1)}, f32[64,2048]{1,0:T(8,128)S(1)}, u32[]{:S(2)}, u32[]{:S(2)}) collective-permute-start(f32[64,2048]{1,0:T(8,128)S(1)} %bitcast_add_fusion.18), channel_id=1, source_target_pairs={{0,8},{10,2},{8,16},{18,10},{16,24},{26,18},{24,28},{30,26},{28,20... | collective-permute-start | bytes 1572872 | tf_op jit(solution)/shard_map/ppermute | solution.py:128
  616.0 16.8 %collective-permute-start.68 = (f32[64,2048]{1,0:T(8,128)S(1)}, f32[64,2048]{1,0:T(8,128)S(1)}, u32[]{:S(2)}, u32[]{:S(2)}) collective-permute-start(f32[64,2048]{1,0:T(8,128)S(1)} %collective-permute-done.66), channel_id=1, source_target_pairs={{0,8},{10,2},{8,16},{18,10},{16,24},{26,18},{24,28},{30,26},{28,20... | collective-permute-start | bytes 1572872 | tf_op jit(solution)/shard_map/ppermute | solution.py:142
  632.9 16.8 %collective-permute-start.70 = (f32[64,2048]{1,0:T(8,128)S(1)}, f32[64,2048]{1,0:T(8,128)S(1)}, u32[]{:S(2)}, u32[]{:S(2)}) collective-permute-start(f32[64,2048]{1,0:T(8,128)S(1)} %collective-permute-done.68), channel_id=1, source_target_pairs={{0,8},{10,2},{8,16},{18,10},{16,24},{26,18},{24,28},{30,26},{28,20... | collective-permute-start | bytes 1572872 | tf_op jit(solution)/shard_map/ppermute | solution.py:142
  649.8 16.8 %collective-permute-start.72 = (f32[64,2048]{1,0:T(8,128)S(1)}, f32[64,2048]{1,0:T(8,128)S(1)}, u32[]{:S(2)}, u32[]{:S(2)}) collective-permute-start(f32[64,2048]{1,0:T(8,128)S(1)} %collective-permute-done.70), channel_id=1, source_target_pairs={{0,8},{10,2},{8,16},{18,10},{16,24},{26,18},{24,28},{30,26},{28,20... | collective-permute-start | bytes 1572872 | tf_op jit(solution)/shard_map/ppermute | solution.py:142
  666.6 16.8 %collective-permute-start.74 = (f32[64,2048]{1,0:T(8,128)S(1)}, f32[64,2048]{1,0:T(8,128)S(1)}, u32[]{:S(2)}, u32[]{:S(2)}) collective-permute-start(f32[64,2048]{1,0:T(8,128)S(1)} %collective-permute-done.72), channel_id=1, source_target_pairs={{0,8},{10,2},{8,16},{18,10},{16,24},{26,18},{24,28},{30,26},{28,20... | collective-permute-start | bytes 1572872 | tf_op jit(solution)/shard_map/ppermute | solution.py:142
  672.2 16.9 %collective-permute-start.96 = (f32[128,1024]{1,0:T(8,128)S(1)}, f32[128,1024]{1,0:T(8,128)S(1)}, u32[]{:S(2)}, u32[]{:S(2)}) collective-permute-start(f32[128,1024]{1,0:T(8,128)S(1)} %collective-permute-done.95), channel_id=1, source_target_pairs={{0,2},{2,0},{4,6},{6,4},{8,10},{10,8},{12,14},{14,12},{16,18},{18,... | collective-permute-start | bytes 1572872 | tf_op jit(solution)/shard_map/ppermute | solution.py:40
  677.8 17.8 %collective-permute-start.40 = (f32[64,2048]{1,0:T(8,128)S(1)}, f32[64,2048]{1,0:T(8,128)S(1)}, u32[]{:S(2)}, u32[]{:S(2)}) collective-permute-start(f32[64,2048]{1,0:T(8,128)S(1)} %collective-permute-done.39), channel_id=1, source_target_pairs={{0,2},{2,0},{4,6},{6,4},{8,10},{10,8},{12,14},{14,12},{16,18},{18,... | collective-permute-start | bytes 1572872 | tf_op jit(solution)/shard_map/ppermute | solution.py:40
  (145 other events, 1354.9 us)

commit v2 on v1

v2 whole, which is shorter than its diff:
```python
import functools
import math

import jax
import jax.numpy as jnp
from jax import lax
from jax.experimental import pallas as pl
from jax.experimental.pallas import tpu as pltpu
from jax.sharding import PartitionSpec as P

HDIM = 128
BLOCK = 512
CTX = 128
LEN = 4096
EPS = 1e-05
HIGH = lax.Precision.HIGH


def mm(left, right, dims=((1,), (0,))):
    return lax.dot_general(
        left, right, (dims, ((), ())), precision=HIGH, preferred_element_type=jnp.float32
    )


def norm_parts(value):
    center = value - jnp.mean(value, axis=-1, keepdims=True)
    spread = jnp.mean(center * center, axis=-1, keepdims=True)
    rate = lax.rsqrt(spread + EPS)
    return center * rate, rate


def norm_back(grad, unit, rate, gain):
    scaled = grad * gain
    inner = jnp.mean(scaled * unit, axis=-1, keepdims=True)
    return rate * (scaled - jnp.mean(scaled, axis=-1, keepdims=True) - unit * inner)


def swap_bit(value, axis, bit):
    size = lax.axis_size(axis)
    return lax.ppermute(value, axis, [(i, i ^ (1 << bit)) for i in range(size)])


def bits_of(count):
    return count.bit_length() - 1


def shift_to(value, axis, distance):
    size = lax.axis_size(axis)
    route = [(i, i + distance) for i in range(size) if 0 <= i + distance < size]
    return lax.ppermute(value, axis, route)


def after(value, *others):
    return lax.optimization_barrier((value,) + others)[0]


def gather_all(piece):
    rows = piece.shape[0]
    mp_size, seq_size = lax.axis_size("mp"), lax.axis_size("seq")
    me = lax.axis_index("seq") * mp_size + lax.axis_index("mp")
    block, low = piece, 0
    for bit in range(bits_of(mp_size * seq_size)):
        axis, own = ("mp", bit) if bit < bits_of(mp_size) else ("seq", bit - bits_of(mp_size))
        other = swap_bit(block, axis, own)
        upper = (me >> bit) & 1
        block = jnp.where(
            upper == 1, jnp.concatenate([other, block], 0), jnp.concatenate([block, other], 0)
        )
    return block


def scatter_sum(whole):
    mp_size, seq_size = lax.axis_size("mp"), lax.axis_size("seq")
    me = lax.axis_index("seq") * mp_size + lax.axis_index("mp")
    block = whole
    for bit in reversed(range(bits_of(mp_size * seq_size))):
        axis, own = ("mp", bit) if bit < bits_of(mp_size) else ("seq", bit - bits_of(mp_size))
        half = block.reshape(2, block.shape[0] // 2, block.shape[1])
        upper = (me >> bit) & 1
        keep = lax.dynamic_index_in_dim(half, upper, 0, keepdims=False)
        give = lax.dynamic_index_in_dim(half, 1 - upper, 0, keepdims=False)
        block = keep + swap_bit(give, axis, own)
    return block


def sum_seq_small(value):
    for bit in range(bits_of(lax.axis_size("seq"))):
        value = value + swap_bit(value, "seq", bit)
    return value


def trade_chips(value, distance):
    size = lax.axis_size("seq")
    return lax.ppermute(value, "seq", [(i, i ^ (2 * distance)) for i in range(size)])


def chip_order(count):
    if count <= 2:
        return list(range(count))
    return list(range(0, count, 2)) + list(range(count - 1 - count % 2, 0, -2))


def ring_route(count):
    order = chip_order(count)
    route = []
    for i in range(count):
        here, there = order[i], order[(i + 1) % count]
        route.append((2 * here, 2 * there))
        route.append((2 * there + 1, 2 * here + 1))
    return route


def ring_spot():
    count = lax.axis_size("seq") // 2
    places = [0] * count
    for i, chip in enumerate(chip_order(count)):
        places[chip] = i
    me = lax.axis_index("seq")
    here = jnp.array(places, jnp.int32)[me // 2]
    return jnp.where(me % 2 == 0, here, (count - here) % count)


def unset(shape):
    return pl.pallas_call(
        lambda out: None,
        out_shape=jax.ShapeDtypeStruct(shape, jnp.float32),
        out_specs=pl.BlockSpec(memory_space=pl.ANY),
    )()


def ring_reduce(parts, gate=()):
    count = lax.axis_size("seq") // 2
    place, route = ring_spot(), ring_route(count)
    rows = parts[0].shape[0] // count

    def chunk(spot):
        cut = [lax.dynamic_slice_in_dim(p, spot * rows, rows, 0) for p in parts]
        return cut[0] if len(cut) == 1 else jnp.concatenate(cut, 1)

    held = chunk(place)
    if gate:
        held = after(held, *gate)
    for step in range(count - 1):
        got = lax.ppermute(held, "seq", route)
        held = got + chunk((place + 2 * count - 1 - step) % count)
    return held


def ring_spread(held, outs, split):
    count = lax.axis_size("seq") // 2
    place, route = ring_spot(), ring_route(count)
    core = lax.axis_index("seq") % 2
    mirror = (count - place) % count
    rows = held.shape[0]

    def put(outs, part, which, spot):
        row = which * (count * rows) + spot % count * rows
        new = []
        for out, (low, high, lead) in zip(outs, split):
            cut = part[:, low:high]
            if lead is None:
                new.append(lax.dynamic_update_slice(out, cut, (row, 0)))
            else:
                new.append(lax.dynamic_update_slice(out, cut[None], (lead, row, 0)))
        return new

    for step in range(count):
        spot, far = place + 1 - step + count, mirror + 1 - step + count
        other = swap_bit(held, "seq", 0)
        outs = put(outs, held, core, spot)
        outs = put(outs, other, 1 - core, far)
        if step < count - 1:
            held = lax.ppermute(held, "seq", route)
    return outs, held


def chip_sum(left, right, first=None):
    core = lax.axis_index("seq") % 2

    def half(which):
        total = None
        for l, r in zip(left, right):
            cut = lax.dynamic_slice_in_dim(l, which * (l.shape[1] // 2), l.shape[1] // 2, 1)
            part = mm(cut, r, ((0,), (0,)))
            total = part if total is None else total + part
        return total

    give = half(1 - core)
    got = swap_bit(give, "seq", 0)
    return half(core) + got


def rows8(shape):
    return lax.broadcasted_iota(jnp.int32, shape, 0).astype(jnp.float32)


def octets_of(decay_ref):
    states, lanes = decay_ref.shape
    rates = [jnp.broadcast_to(decay_ref[n : n + 1, :], (8, lanes)) for n in range(states)]
    return rates, [jnp.exp(-8.0 * rate) for rate in rates]


def summary_kernel(tail_ref, x_ref, decay_ref, h_ref):
    states, lanes = decay_ref.shape
    rates, jump = octets_of(decay_ref)

    def run(ref):
        def step(i, acc):
            tile = ref[pl.ds(pl.multiple_of(i * 8, 8), 8), :]
            return tuple(j * a + tile for j, a in zip(jump, acc))

        return step

    acc = (tail_ref[:8, :] * 0.0,) * states
    acc = lax.fori_loop(0, tail_ref.shape[0] // 8, run(tail_ref), acc)
    acc = lax.fori_loop(0, (x_ref.shape[0] - tail_ref.shape[0]) // 8, run(x_ref), acc)
    left = 7.0 - rows8((8, lanes))
    for n in range(states):
        h_ref[n : n + 1, :] = jnp.sum(acc[n] * jnp.exp(-rates[n] * left), axis=0, keepdims=True)


def moment_kernel(tail_ref, x_ref, decay_ref, p_ref):
    states, lanes = decay_ref.shape
    rates, jump = octets_of(decay_ref)

    def run(ref):
        def step(i, carry):
            acc, lag = carry
            tile = ref[pl.ds(pl.multiple_of(i * 8, 8), 8), :]
            lag = tuple(j * (b + a) for j, a, b in zip(jump, acc, lag))
            acc = tuple(j * a + tile for j, a in zip(jump, acc))
            return acc, lag

        return step

    zeros = (tail_ref[:8, :] * 0.0,) * states
    carry = lax.fori_loop(0, tail_ref.shape[0] // 8, run(tail_ref), (zeros, zeros))
    acc, lag = lax.fori_loop(0, (x_ref.shape[0] - tail_ref.shape[0]) // 8, run(x_ref), carry)
    left = 7.0 - rows8((8, lanes))
    for n in range(states):
        total = (8.0 * lag[n] + left * acc[n]) * jnp.exp(-rates[n] * left)
        p_ref[n : n + 1, :] = jnp.sum(total, axis=0, keepdims=True)


def carry_kernel(near_ref, first_ref, decay_ref, y_ref):
    states, lanes = decay_ref.shape
    rates, jump = octets_of(decay_ref)
    ahead = rows8((8, lanes)) + 1.0
    start = tuple(
        jnp.broadcast_to(first_ref[n : n + 1, :], (8, lanes)) * jnp.exp(-rates[n] * ahead)
        for n in range(states)
    )

    def step(i, modes):
        base = pl.multiple_of(i * 8, 8)
        y_ref[pl.ds(base, 8), :] = near_ref[pl.ds(base, 8), :] + sum(modes)
        return tuple(j * m for j, m in zip(jump, modes))

    lax.fori_loop(0, y_ref.shape[0] // 8, step, start)


def spread_kernel(first_ref, decay_ref, y_ref):
    states, lanes = decay_ref.shape
    rates, jump = octets_of(decay_ref)
    ahead = 8.0 - rows8((8, lanes))
    count = y_ref.shape[0] // 8
    start = tuple(
        jnp.broadcast_to(first_ref[n : n + 1, :], (8, lanes)) * jnp.exp(-rates[n] * ahead)
        for n in range(states)
    )

    def step(i, modes):
        y_ref[pl.ds(pl.multiple_of((count - 1 - i) * 8, 8), 8), :] = sum(modes)
        return tuple(j * m for j, m in zip(jump, modes))

    lax.fori_loop(0, count, step, start)


def near_kernel(x_ref, fade_ref, gate_ref, skip_ref, y_ref):
    fade, gate, skip = fade_ref[...], gate_ref[...], skip_ref[...]

    def octet(i, u):
        base = pl.multiple_of(i * 8, 8)
        tile = x_ref[pl.ds(base, 8), :]
        rows = []
        for r in range(8):
            row = tile[r : r + 1, :]
            u = fade * u + gate * jnp.broadcast_to(row, fade.shape)
            rows.append(jnp.sum(u, axis=0, keepdims=True) + skip * row)
        y_ref[pl.ds(base, 8), :] = jnp.concatenate(rows, 0)
        return u

    lax.fori_loop(0, x_ref.shape[0] // 8, octet, jnp.zeros(fade.shape, jnp.float32))


def tail_back_kernel(
    x_ref, d_ref, fade_ref, gate_ref, skip_ref, q_ref, r_ref, dh_ref, dp_ref, dskip_ref, dx_ref
):
    fade, gate, skip = fade_ref[...], gate_ref[...], skip_ref[...]
    octets = x_ref.shape[0] // 8
    zero = jnp.zeros(fade.shape, jnp.float32)

    def forward(i, carry):
        h, p, dh, dp = carry
        base = pl.multiple_of(i * 8, 8)
        tile, grads = x_ref[pl.ds(base, 8), :], d_ref[pl.ds(base, 8), :]
        for r in range(8):
            p = fade * (p + h)
            h = fade * h + jnp.broadcast_to(tile[r : r + 1, :], fade.shape)
            grad = jnp.broadcast_to(grads[r : r + 1, :], fade.shape)
            dh = dh + grad * h
            dp = dp + grad * p
        return h, p, dh, dp

    _, _, dh, dp = lax.fori_loop(0, octets, forward, (zero, zero, zero, zero))
    dh_ref[...] = dh
    dp_ref[...] = dp
    dskip_ref[...] = jnp.sum(x_ref[...] * d_ref[...], axis=0, keepdims=True)

    def backward(k, carry):
        q, r_sum = carry
        base = pl.multiple_of((octets - 1 - k) * 8, 8)
        grads = d_ref[pl.ds(base, 8), :]
        rows = [None] * 8
        for r in reversed(range(8)):
            r_sum = fade * (r_sum + q)
            grad = grads[r : r + 1, :]
            q = fade * q + jnp.broadcast_to(grad, fade.shape)
            rows[r] = jnp.sum(gate * q, axis=0, keepdims=True) + skip * grad
        dx_ref[pl.ds(base, 8), :] = jnp.concatenate(rows, 0)
        return q, r_sum

    q, r_sum = lax.fori_loop(0, octets, backward, (zero, zero))
    q_ref[...] = q
    r_ref[...] = r_sum


def by_channels(kernel, ins, outs, flops, cut=512):
    width = ins[0].shape[1]
    cut = cut if width % cut == 0 else width

    def spec(rows):
        return pl.BlockSpec((rows, cut), lambda i: (0, i))

    moved = sum(a.size for a in ins) + sum(r * width for r in outs)
    return pl.pallas_call(
        kernel,
        grid=(width // cut,),
        in_specs=[spec(a.shape[0]) for a in ins],
        out_specs=[spec(r) for r in outs],
        out_shape=[jax.ShapeDtypeStruct((r, width), jnp.float32) for r in outs],
        cost_estimate=pl.CostEstimate(flops=flops, bytes_accessed=4 * moved, transcendentals=0),
    )(*ins)


def cut(value):
    top = value.astype(jnp.bfloat16)
    return top, (value - top.astype(jnp.float32)).astype(jnp.bfloat16)


def dot3(left, right, dims):
    def one(a, b):
        return lax.dot_general(a, b, (dims, ((), ())), preferred_element_type=jnp.float32)

    return one(left[0], right[1]) + one(left[1], right[0]) + one(left[0], right[0])


NT = ((1,), (1,))
NN = ((1,), (0,))
TN = ((0,), (0,))
TILE = 256
SCALE = HDIM ** (-0.5)


def causal(shape, first_row):
    row = lax.broadcasted_iota(jnp.int32, shape, 0) + first_row
    return lax.broadcasted_iota(jnp.int32, shape, 1) <= row


def self_kernel(q_ref, k_ref, v_ref, acc_ref, top_ref, sum_ref):
    rows = q_ref.shape[0]
    k, v = cut(k_ref[...]), cut(v_ref[...])
    for first in range(0, rows, TILE):
        span = slice(first, first + TILE)
        seen = first + TILE
        q = cut(q_ref[span, :] * SCALE)
        scores = dot3(q, (k[0][:seen], k[1][:seen]), NT)
        scores = jnp.where(causal(scores.shape, first), scores, -1e30)
        top = jnp.max(scores, axis=1, keepdims=True)
        weight = jnp.exp(scores - top)
        acc_ref[span, :] = dot3(cut(weight), (v[0][:seen], v[1][:seen]), NN)
        top_ref[span, :] = jnp.broadcast_to(top, (TILE, HDIM))
        sum_ref[span, :] = jnp.broadcast_to(jnp.sum(weight, axis=1, keepdims=True), (TILE, HDIM))


def ctx_kernel(ok_ref, q_ref, k_ref, v_ref, acc_ref, top_ref, sum_ref, out_ref, log_ref):
    ok = ok_ref[0] > 0
    q = cut(q_ref[...] * SCALE)
    scores = dot3(q, cut(k_ref[...]), NT)
    scores = jnp.where(ok, scores, -1e30)
    top = jnp.maximum(top_ref[...], jnp.max(scores, axis=1, keepdims=True))
    weight = jnp.where(ok, jnp.exp(scores - top[:, :1]), 0.0)
    ease = jnp.exp(top_ref[...] - top)
    total = sum_ref[...] * ease + jnp.sum(weight, axis=1, keepdims=True)
    out_ref[...] = (acc_ref[...] * ease + dot3(cut(weight), cut(v_ref[...]), NN)) / total
    log_ref[...] = top + jnp.log(total)


def back_kernel(
    ok_ref, q_ref, k_ref, v_ref, kc_ref, vc_ref, o0_ref, o1_ref, l0_ref, l1_ref, g0_ref, g1_ref,
    dq_ref, dk_ref, dv_ref, dkc_ref, dvc_ref,
):
    ok = ok_ref[0] > 0
    rows = q_ref.shape[0]
    tiles = (rows + TILE - 1) // TILE
    k, v, kc, vc = cut(k_ref[...]), cut(v_ref[...]), cut(kc_ref[...]), cut(vc_ref[...])
    for tile in reversed(range(tiles)):
        first = tile * TILE
        seen = first + TILE
        o, log, g = (
            (o0_ref, l0_ref, g0_ref) if first < rows // 2 else (o1_ref, l1_ref, g1_ref)
        )
        local = slice(first % (rows // 2), first % (rows // 2) + TILE)
        grad = g[local, :]
        q = cut(q_ref[first:seen, :] * SCALE)
        grad2 = cut(grad)
        inner = jnp.sum(grad * o[local, :], axis=1, keepdims=True)
        mark = log[local, :][:, :1]
        ks, vs = (k[0][:seen], k[1][:seen]), (v[0][:seen], v[1][:seen])
        probs = dot3(q, ks, NT)
        probs = jnp.where(causal(probs.shape, first), jnp.exp(probs - mark), 0.0)
        probs_c = jnp.where(ok, jnp.exp(dot3(q, kc, NT) - mark), 0.0)
        ds = cut(probs * (dot3(grad2, vs, NT) - inner))
        ds_c = cut(probs_c * (dot3(grad2, vc, NT) - inner))
        probs, probs_c = cut(probs), cut(probs_c)
        dq_ref[first:seen, :] = (dot3(ds, ks, NN) + dot3(ds_c, kc, NN)) * SCALE
        dk, dv = dot3(ds, q, TN), dot3(probs, grad2, TN)
        dkc, dvc = dot3(ds_c, q, TN), dot3(probs_c, grad2, TN)
        if tile == tiles - 1:
            dk_ref[...], dv_ref[...], dkc_ref[...], dvc_ref[...] = dk, dv, dkc, dvc
        else:
            dk_ref[:seen, :] += dk
            dv_ref[:seen, :] += dv
            dkc_ref[...] += dkc
            dvc_ref[...] += dvc


def by_heads(kernel, ins, outs, scalars=(), firsts=None, flops=0):
    heads = ins[0][0].shape[1] // HDIM
    specs = [pl.BlockSpec(memory_space=pltpu.SMEM) for _ in scalars]
    for _, rows, at in ins:
        specs.append(pl.BlockSpec((rows, HDIM), lambda h, at=at: (at, h)))
    moved = sum(r * HDIM * heads for _, r, _ in ins) + sum(outs) * HDIM * heads
    return pl.pallas_call(
        kernel,
        grid=(heads,),
        in_specs=specs,
        out_specs=[pl.BlockSpec((r, HDIM), lambda h: (0, h)) for r in outs],
        out_shape=[jax.ShapeDtypeStruct((r, heads * HDIM), jnp.float32) for r in outs],
        cost_estimate=pl.CostEstimate(flops=flops, bytes_accessed=4 * moved, transcendentals=0),
        compiler_params=pltpu.CompilerParams(vmem_limit_bytes=40 << 20),
    )(*scalars, *[a for a, _, _ in ins])


def per_device(
    tokens,
    window_state,
    norm1_gain,
    norm1_bias,
    in_coef,
    out_coef,
    decay_rate,
    skip_gain,
    qkv_weight,
    out_weight,
    norm2_gain,
    norm2_bias,
    up_weight,
    up_bias,
    down_weight,
    down_bias,
    cotangent,
):
    place_seq = lax.axis_index("seq")
    core = place_seq % 2
    rows, width = tokens.shape
    states = in_coef.shape[1]
    windows = window_state.shape[0]
    per_window = LEN // rows
    block = place_seq % per_window
    window = place_seq // per_window
    has_ctx = block > 0
    ok = has_ctx.astype(jnp.int32).reshape(1)
    half = rows // 2

    qkv = qkv_weight.astype(jnp.float32)
    out_own = out_weight.astype(jnp.float32)
    up = up_weight.astype(jnp.float32)
    down = down_weight.astype(jnp.float32)

    decay = jnp.transpose(gather_all(decay_rate))
    packed = jnp.concatenate(
        [in_coef, out_coef, skip_gain[:, None]] + [window_state[w] for w in range(windows)], 1
    )
    coefs = jnp.transpose(gather_all(packed))
    c_in = coefs[:states]
    c_out = coefs[states : 2 * states]
    skip = coefs[2 * states : 2 * states + 1]
    carried = lax.dynamic_slice_in_dim(coefs, 2 * states + 1 + window * states, states, 0)
    gate = c_in * c_out
    fade = jnp.exp(-decay)

    tail_tokens = shift_to(tokens[rows - CTX :], "seq", 1)

    inner = out_own.shape[0]
    sent = lax.dynamic_slice_in_dim(out_own, core * (inner // 2), inner // 2, 0)
    across = swap_bit(sent, "mp", 0)
    beside = swap_bit(across, "seq", 0)
    out_far = jnp.where(
        core == 0, jnp.concatenate([across, beside], 0), jnp.concatenate([beside, across], 0)
    )

    unit1, rate1 = norm_parts(tokens)
    normed = unit1 * norm1_gain + norm1_bias
    tail_unit, _ = norm_parts(tail_tokens)
    tail = jnp.where(has_ctx, tail_unit * norm1_gain + norm1_bias, 0.0)

    length = float(rows)
    chips = per_window // 2
    chip = block // 2
    (sum_h,) = by_channels(summary_kernel, [tail, normed, decay], [states], 2 * rows * width * states, 128)

    def faded(steps):
        return jnp.exp(-decay * steps)

    def pair_order(value):
        other = swap_bit(value, "seq", 0)
        return jnp.where(core == 0, value, other), jnp.where(core == 0, other, value)

    first_h, second_h = pair_order(sum_h)
    both_h = faded(length) * first_h + second_h
    far_h = [trade_chips(both_h, d) for d in range(1, chips)]
    past_h = jnp.zeros_like(sum_h)
    for d in range(1, chips):
        there = chip ^ d
        gap = jnp.maximum(chip - 1 - there, 0).astype(jnp.float32) * (2.0 * length)
        past_h = past_h + jnp.where(there < chip, faded(gap) * far_h[d - 1], 0.0)
    past_h = jnp.where(core == 0, past_h, faded(length) * past_h + first_h)

    start_t = jnp.maximum(block * rows - CTX, 0).astype(jnp.float32)
    first = c_out * (c_in * past_h + carried * faded(start_t))
    (near,) = by_channels(near_kernel, [tail, fade, gate, skip], [CTX], 5 * CTX * width * states)
    (context,) = by_channels(carry_kernel, [near, first, decay], [CTX], 2 * CTX * width * states, 128)

    query = mm(normed, qkv[0])
    key = mm(normed, qkv[1])
    value = mm(normed, qkv[2])
    acc, top, total = by_heads(
        self_kernel, [(a, rows, 0) for a in (query, key, value)], [rows] * 3,
        flops=2 * 6 * rows * rows * inner,
    )
    grad_hidden = mm(cotangent, down, NT)
    context = after(context, acc, grad_hidden)
    key_ctx = mm(context, qkv[1])
    value_ctx = mm(context, qkv[2])
    heads, logs, far = [], [], []
    for part in range(2):
        o, l = by_heads(
            ctx_kernel,
            [(query, half, part), (key_ctx, CTX, 0), (value_ctx, CTX, 0)]
            + [(a, half, part) for a in (acc, top, total)],
            [half, half],
            scalars=(ok,),
            flops=2 * 6 * half * CTX * inner,
        )
        if part:
            o = after(o, heads[0])
        heads.append(o)
        logs.append(l)
        far.append(swap_bit(o, "mp", 0))

    unit2, rate2, mixed, normed2, hidden, slope = [], [], [], [], [], []
    for part in range(2):
        span = slice(part * half, (part + 1) * half)
        m = tokens[span] + (mm(heads[part], out_own) + mm(far[part], out_far))
        u, r = norm_parts(m)
        n = u * norm2_gain + norm2_bias
        pre = mm(n, up) + up_bias
        cdf = 0.5 + 0.5 * lax.erf(pre * (0.5**0.5))
        bell = jnp.exp(-0.5 * pre * pre) * (1.0 / math.sqrt(2.0 * math.pi))
        mixed.append(m)
        unit2.append(u)
        rate2.append(r)
        normed2.append(n)
        hidden.append(pre * cdf)
        slope.append(grad_hidden[span] * (cdf + pre * bell))
    cots = [cotangent[:half], cotangent[half:]]
    down_half = chip_sum(hidden, cots)
    grad_pre = [after(s, down_half) for s in slope]
    part2 = [mm(g, up, NT) for g in grad_pre]
    sums2 = [p + swap_bit(p, "mp", 0) for p in part2]
    up_half = chip_sum(normed2, [after(g, part2[1]) for g in grad_pre])
    feed = jnp.concatenate([mm(after(h, up_half), down) for h in hidden], 0)
    result = jnp.concatenate(mixed, 0) + (feed + swap_bit(after(feed, *sums2), "mp", 0)) + down_bias
    grad_up_bias = jnp.sum(grad_pre[0], axis=0) + jnp.sum(grad_pre[1], axis=0)
    grad_down_bias = jnp.sum(cotangent, axis=0)

    held_down = ring_reduce([down_half])
    held_up = ring_reduce([up_half])
    (grad_down,), last_down = ring_spread(held_down, [unset(down.shape)], [(0, width, None)])
    (grad_up,), last_up = ring_spread(held_up, [unset(up.shape)], [(0, up.shape[1], None)])

    grad_mixed, grad_heads = [], []
    gain2, bias2 = 0.0, 0.0
    for part in range(2):
        g = sums2[part]
        gain2 = gain2 + jnp.sum(g * unit2[part], axis=0)
        bias2 = bias2 + jnp.sum(g, axis=0)
        grad_mixed.append(cots[part] + norm_back(g, unit2[part], rate2[part], norm2_gain))
        grad_heads.append(mm(grad_mixed[part], out_own, NT))

    dq, dk, dv, dk_ctx, dv_ctx = by_heads(
        back_kernel,
        [(query, rows, 0), (key, rows, 0), (value, rows, 0), (key_ctx, CTX, 0), (value_ctx, CTX, 0)]
        + [(a, half, 0) for a in heads + logs + grad_heads],
        [rows, rows, rows, CTX, CTX],
        scalars=(ok,),
        flops=2 * 15 * rows * (rows + CTX) * inner,
    )
    dkv = jnp.concatenate([dk, dv], 1)
    dkv_ctx = jnp.concatenate([dk_ctx, dv_ctx], 1)
    q_half = chip_sum([normed], [dq])
    kv_half = chip_sum([context, normed], [dkv_ctx, dkv])
    out_half = chip_sum(grad_mixed, heads)
    grad_context = mm(dk_ctx, qkv[1], NT) + mm(dv_ctx, qkv[2], NT)
    grad_context = jnp.where(has_ctx, grad_context, 0.0)
    grad_normed_part = mm(dq, qkv[0], NT) + mm(dk, qkv[1], NT) + mm(dv, qkv[2], NT)

    gates = (last_down, last_up)
    held_qo = ring_reduce([q_half, out_half], gates)
    held_kv = ring_reduce([kv_half], gates)
    grad_qkv = unset((3, width, inner))
    (grad_qkv, grad_out_t), _ = ring_spread(
        held_qo, [grad_qkv, unset((width, inner))], [(0, inner, 0), (inner, 2 * inner, None)]
    )
    (key_out, value_out), _ = ring_spread(
        held_kv, [unset((width, inner)), unset((width, inner))], [(0, inner, None), (inner, 2 * inner, None)]
    )
    grad_qkv = lax.dynamic_update_slice(grad_qkv, key_out[None], (1, 0, 0))
    grad_qkv = lax.dynamic_update_slice(grad_qkv, value_out[None], (2, 0, 0))
    grad_out = jnp.transpose(grad_out_t)

    (sum_p,) = by_channels(moment_kernel, [tail, after(normed, dq), decay], [states], 4 * rows * width * states, 128)
    first_p, second_p = pair_order(sum_p)
    both_p = faded(length) * (first_p + length * first_h) + second_p
    past_p = jnp.zeros_like(sum_p)
    for d in range(1, chips):
        there = chip ^ d
        gap = jnp.maximum(chip - 1 - there, 0).astype(jnp.float32) * (2.0 * length)
        moved = faded(gap) * (trade_chips(both_p, d) + gap * far_h[d - 1])
        past_p = past_p + jnp.where(there < chip, moved, 0.0)
    chip_h = jnp.zeros_like(sum_p)
    for d in range(1, chips):
        there = chip ^ d
        gap = jnp.maximum(chip - 1 - there, 0).astype(jnp.float32) * (2.0 * length)
        chip_h = chip_h + jnp.where(there < chip, faded(gap) * far_h[d - 1], 0.0)
    past_p = jnp.where(core == 0, past_p, faded(length) * (past_p + length * chip_h) + first_p)

    sum_q, sum_r, part_h, part_p, part_skip, grad_tail = by_channels(
        tail_back_kernel,
        [tail, grad_context, fade, gate, skip],
        [states, states, states, states, 1, CTX],
        20 * CTX * width * states,
    )
    along_h = fade * past_h * sum_q + part_h
    along_p = fade * (past_h * (sum_r + sum_q) + past_p * sum_q) + part_p
    gone = faded(start_t + 1.0)
    part_in = c_out * along_h
    part_out = c_in * along_h + carried * gone * sum_q
    part_decay = -gate * along_p - c_out * carried * gone * ((start_t + 1.0) * sum_q + sum_r)
    stacked = jnp.concatenate([part_in, part_out, part_decay, part_skip], 0)
    stacked = jnp.pad(stacked, ((0, -stacked.shape[0] % 128), (0, 0)))
    own = scatter_sum(jnp.transpose(stacked))
    grad_in = own[:, :states]
    grad_out_coef = own[:, states : 2 * states]
    grad_decay = own[:, 2 * states : 3 * states]
    grad_skip = own[:, 3 * states]

    first_q, second_q = pair_order(sum_q)
    both_q = first_q + faded(length) * second_q
    later = jnp.zeros_like(sum_q)
    for d in range(1, chips):
        there = chip ^ d
        gap = jnp.maximum(there - 1 - chip, 0).astype(jnp.float32) * (2.0 * length)
        later = later + jnp.where(there > chip, faded(gap) * trade_chips(both_q, d), 0.0)
    later = jnp.where(core == 1, later, second_q + faded(length) * later)
    (grad_segment,) = by_channels(
        spread_kernel, [gate * later, decay], [rows], 2 * rows * width * states, 128
    )
    to_last = jnp.where(has_ctx, grad_segment[:CTX] + grad_tail, 0.0)
    from_next = shift_to(to_last, "seq", -1)
    grad_states = jnp.concatenate([grad_segment[CTX:], from_next], 0)

    grad_normed_half = grad_normed_part + grad_states
    grad_normed = grad_normed_half + swap_bit(grad_normed_half, "mp", 0)
    grad_gain1 = jnp.sum(grad_normed * unit1, axis=0)
    grad_bias1 = jnp.sum(grad_normed, axis=0)
    grad_tokens = jnp.concatenate(grad_mixed, 0) + norm_back(grad_normed, unit1, rate1, norm1_gain)

    small = sum_seq_small(
        jnp.concatenate(
            [gain2, bias2, grad_down_bias, grad_gain1, grad_bias1, grad_up_bias]
        ).reshape(-1, width)
    )
    return (
        result,
        grad_tokens,
        small[3],
        small[4],
        grad_in,
        grad_out_coef,
        grad_decay,
        grad_skip,
        grad_qkv,
        grad_out,
        small[0],
        small[1],
        grad_up,
        small[5:].reshape(-1),
        grad_down,
        small[2],
    )


def solution(mesh):
    owner = P(("seq", "mp"), None)
    return jax.shard_map(
        per_device,
        mesh=mesh,
        in_specs=(
            P("seq", None),
            P(None, ("seq", "mp"), None),
            P(),
            P(),
            owner,
            owner,
            owner,
            P(("seq", "mp")),
            P(None, None, "mp"),
            P("mp", None),
            P(),
            P(),
            P(None, "mp"),
            P("mp"),
            P("mp", None),
            P(),
            P("seq", None),
        ),
        out_specs=(
            P("seq", None),
            P("seq", None),
            P(),
            P(),
            owner,
            owner,
            owner,
            P(("seq", "mp")),
            P(None, None, "mp"),
            P("mp", None),
            P(),
            P(),
            P(None, "mp"),
            P("mp"),
            P("mp", None),
            P(),
        ),
        check_vma=False,
    )
```

time: 743 us -> 628 us (0.85)
  waiting for transfers between devices: 329 us -> 178 us
  Pallas kernels: 26.7 us -> 71.8 us
  starting transfers between devices: 95.2 us -> 133 us
  other arithmetic: 72 us -> 47.6 us
  local copies, waits for them, and re-layouts: 88.3 us -> 64.3 us
    ppermute x42 -> x65, waiting for transfers between devices: 175 us -> 94.7 us  [the longest x28 44.5 us: ring_reduce(): got = lax.ppermute(held, 'seq', route)]
    ppermute x55 -> x67, waiting for transfers between devices: 154 us -> 83.8 us  [swap_bit(): return lax.ppermute(value, axis, [(i, i ^ 1 << bit) for i in range(size)])]
    ppermute x42 -> x65, starting transfers between devices: 56.4 us -> 96.2 us  [the longest x28 44.5 us: ring_spread(): held = lax.ppermute(held, 'seq', route)]
    dynamic_slice x4 -> x6, local copies, waits for them, and re-layouts: 34.4 us -> 4.41 us  [the longest x5 3.83 us: chunk(): cut = [lax.dynamic_slice_in_dim(p, spot * rows, rows, 0) for p in parts]]
    dynamic_update_slice x45 -> x80, local copies, waits for them, and re-layouts: 2 us -> 29.2 us  [the longest x62 14 us: put(): new.append(lax.dynamic_update_slice(out, cut, (row, 0)))]
    pallas_call x0 -> x10, Pallas kernels: none -> 24.7 us  [the longest x4 24.7 us: by_heads(): pl.pallas_call(kernel, grid=(heads,), in_specs=specs, out_specs=[pl.Block...]
    pallas_call x4 -> x6, Pallas kernels: 26.7 us -> 47 us  [by_channels(): pl.pallas_call(kernel, grid=(width // cut,), in_specs=[spec(a.shape[0]) f...]
    reshape x2 -> x1, local copies, waits for them, and re-layouts: 11.7 us -> 1.38 us  [per_device(): small = sum_seq_small(jnp.concatenate([gain2, bias2, grad_down_bias, grad...]
  transfers between devices with their start and end apart: 99 -> 134, of which waited for: 57 -> 62; matrix products, arithmetic and copies ran while one was open for 26% -> 30% of each run, Pallas kernels for 2% -> 12%
where the time goes in v2:
time: 628 us; the launch traced here: 617 us
  waiting for transfers between devices  178 us (28%)
  starting transfers between devices  133 us (21%)
  matrix products  116 us (18%)
  Pallas kernels  71.8 us (11%)
  local copies, waits for them, and re-layouts  64.3 us (10%)
  other arithmetic  47.6 us (8%)
    dot_general x41, matrix products, mm(): lax.dot_general(left, right, (dims, ((), ())), precision=HIGH, preferred_...  116 us
    ppermute x67, waiting for transfers between devices, swap_bit(): return lax.ppermute(value, axis, [(i, i ^ 1 << bit) for i in range(size)])  83.8 us
    pallas_call x6, Pallas kernels, by_channels(): pl.pallas_call(kernel, grid=(width // cut,), in_specs=[spec(a.shape[0]) f...  47 us
    ppermute x28, waiting for transfers between devices, ring_reduce(): got = lax.ppermute(held, 'seq', route)  44.5 us
    ppermute x28, starting transfers between devices, ring_spread(): held = lax.ppermute(held, 'seq', route)  44.5 us
    ppermute x28, waiting for transfers between devices, ring_spread(): held = lax.ppermute(held, 'seq', route)  44.4 us
    ppermute x28, starting transfers between devices, ring_reduce(): got = lax.ppermute(held, 'seq', route)  42.5 us
    ppermute x67, starting transfers between devices, swap_bit(): return lax.ppermute(value, axis, [(i, i ^ 1 << bit) for i in range(size)])  34.3 us
  transfers between devices with their start and end apart: 134, of which 62 were waited for; matrix products, arithmetic and copies ran while one was open for 30% of the time, Pallas kernels for 12%

profile of v2, /device:TPU:0, one launch (start us, length us, event | category | flops | bytes accessed | tf_op | source)
XLA Modules:
  0.0 616.7 jit_solution(2899310134980269747)
XLA Ops:
  20.5 6.1 fusion.167
  26.6 6.1 shard_map.363
  55.6 7.6 %shard_map.361 = f32[16,1024]{1,0:T(8,128)} custom-call(f32[128,1024]{1,0:T(8,128)} %add_select_fusion.x_ref.tail_ref, f32[512,1024]{1,0:T(8,128)} %copy-done.18, f32[16,1024]{1,0:T(8,128)} %get-tuple-element.194.decay_ref), custom_call_target="tpu_custom_call" | custom-call | flops 16777216 | bytes 2752512 | tf_op jit(solution)/shard_map/pallas_call | solution.py:346
  70.4 4.4 shard_map.360.near_ref
  75.6 6.0 shard_map.362
  96.5 18.4 %collective-permute-done.18 = f32[256,512]{1,0:T(8,128)S(1)} collective-permute-done((f32[256,512]{1,0:T(8,128)S(1)}, f32[256,512]{1,0:T(8,128)S(1)}, u32[]{:S(2)}, u32[]{:S(2)}) %collective-permute-start.18) | collective-permute-done | bytes 524320 | tf_op jit(solution)/shard_map/ppermute | solution.py:40
  127.0 5.6 fusion.9
  134.7 4.0 convolution_add_fusion.3
  147.1 4.5 add_add_fusion.1
  164.3 4.0 convolution_add_fusion
  172.3 5.6 fusion.74
  181.0 25.9 %collective-permute-done.21 = f32[256,1024]{1,0:T(8,128)} collective-permute-done((f32[256,1024]{1,0:T(8,128)}, f32[256,1024]{1,0:T(8,128)}, u32[]{:S(2)}, u32[]{:S(2)}) %collective-permute-start.21) | collective-permute-done | bytes 1048608 | tf_op jit(solution)/shard_map/ppermute | solution.py:40
  207.0 3.9 multiply_reduce_fusion.4
  214.2 12.3 %shard_map.366 = (f32[512,512]{1,0:T(8,128)S(1)}, f32[512,512]{1,0:T(8,128)S(1)}, f32[512,512]{1,0:T(8,128)S(1)}, f32[128,512]{1,0:T(8,128)S(1)}, f32[128,512]{1,0:T(8,128)S(1)}) custom-call(s32[1]{0:T(128)} %bitcast.ok_ref, f32[512,512]{1,0:T(8,128)S(1)} %fusion.31.q_ref, f32[512,512]{1,0:T(8,128)S(1)} %copy-done.13, f32[512,512]{1,0:T(8,128)S(1)} %copy-done.11, ...), custom_call_target="tpu_custom_call" | custom-call | flops 5033164800 | bytes 10485760 | tf_op jit(solution)/shard_map/pallas_call | solution.py:454
  244.3 11.3 %shard_map.369 = f32[16,1024]{1,0:T(8,128)} custom-call(f32[128,1024]{1,0:T(8,128)} %add_select_fusion.x_ref.tail_ref, f32[512,1024]{1,0:T(8,128)} %copy-done.18, f32[16,1024]{1,0:T(8,128)} %get-tuple-element.194.decay_ref), custom_call_target="tpu_custom_call" | custom-call | flops 33554432 | bytes 2752512 | tf_op jit(solution)/shard_map/pallas_call | solution.py:346
  258.9 7.6 %shard_map.367 = (f32[16,1024]{1,0:T(8,128)}, f32[16,1024]{1,0:T(8,128)}, f32[16,1024]{1,0:T(8,128)}, f32[16,1024]{1,0:T(8,128)}, f32[1,1024]{1,0:T(1,128)}, /*index=5*/f32[128,1024]{1,0:T(8,128)}) custom-call(f32[128,1024]{1,0:T(8,128)} %add_select_fusion.x_ref.tail_ref, f32[128,1024]{1,0:T(8,128)} %fusion.14.d_ref, ...), custom_call_target="tpu_custom_call" | custom-call | flops 41943040 | bytes 1974272 | tf_op jit(solution)/shard_map/pallas_call | solution.py:346
  286.5 12.6 %collective-permute-done.38 = f32[512,128]{0,1:T(8,128)S(1)} collective-permute-done((f32[512,128]{0,1:T(8,128)S(1)}, f32[512,128]{0,1:T(8,128)S(1)}, u32[]{:S(2)}, u32[]{:S(2)}) %collective-permute-start.38) | collective-permute-done | bytes 262176 | tf_op jit(solution)/shard_map/ppermute | solution.py:40
  310.9 10.1 %shard_map.368 = f32[512,1024]{1,0:T(8,128)} custom-call(f32[16,1024]{1,0:T(8,128)} %select_multiply_fusion.first_ref, f32[16,1024]{1,0:T(8,128)} %get-tuple-element.194.decay_ref), custom_call_target="tpu_custom_call" | custom-call | flops 16777216 | bytes 2228224 | tf_op jit(solution)/shard_map/pallas_call | solution.py:346
  334.3 6.5 %collective-permute-start.48 = (f32[128,1024]{1,0:T(8,128)}, f32[128,1024]{1,0:T(8,128)S(1)}, u32[]{:S(2)}, u32[]{:S(2)}) collective-permute-start(f32[128,1024]{1,0:T(8,128)} %dynamic-slice_add_fusion.11), channel_id=1, source_target_pairs={{0,8},{10,2},{8,16},{18,10},{16,24},{26,18},{24,28},{30,26},{28,20... | collective-permute-start | bytes 1572872 | tf_op jit(solution)/shard_map/ppermute | solution.py:144
  340.8 4.6 maximum_add_fusion.2
  350.3 4.4 add_add_fusion
  359.6 4.6 collective-permute-done.59
  370.9 4.6 collective-permute-done.60
  376.5 4.2 add_add_fusion.2
  383.1 3.6 collective-permute-done.61
  387.7 6.0 collective-permute-done.29
  413.2 5.0 fusion.172
  465.2 8.5 %collective-permute-done.23 = f32[512,1024]{1,0:T(8,128)S(1)} collective-permute-done((f32[512,1024]{1,0:T(8,128)S(1)}, f32[512,1024]{1,0:T(8,128)S(1)}, u32[]{:S(2)}, u32[]{:S(2)}) %collective-permute-start.23) | collective-permute-done | bytes 2097184 | tf_op jit(solution)/shard_map/ppermute | solution.py:40
  478.2 4.7 collective-permute-done.69
  485.3 6.7 %collective-permute-done.70 = f32[64,2048]{1,0:T(8,128)S(1)} collective-permute-done((f32[64,2048]{1,0:T(8,128)S(1)}, f32[64,2048]{1,0:T(8,128)S(1)}, u32[]{:S(2)}, u32[]{:S(2)}) %collective-permute-start.70) | collective-permute-done | bytes 524320 | tf_op jit(solution)/shard_map/ppermute | solution.py:173
  493.9 7.4 %collective-permute-done.71 = f32[64,2048]{1,0:T(8,128)S(1)} collective-permute-done((f32[64,2048]{1,0:T(8,128)S(1)}, f32[64,2048]{1,0:T(8,128)S(1)}, u32[]{:S(2)}, u32[]{:S(2)}) %collective-permute-start.71) | collective-permute-done | bytes 524320 | tf_op jit(solution)/shard_map/ppermute | solution.py:173
  503.1 7.3 %collective-permute-done.72 = f32[64,2048]{1,0:T(8,128)S(1)} collective-permute-done((f32[64,2048]{1,0:T(8,128)S(1)}, f32[64,2048]{1,0:T(8,128)S(1)}, u32[]{:S(2)}, u32[]{:S(2)}) %collective-permute-start.72) | collective-permute-done | bytes 524320 | tf_op jit(solution)/shard_map/ppermute | solution.py:173
  (774 shorter events, 377.2 us)
Async XLA Ops:
  0.7 34.1 %collective-permute-start.1 = (f32[32,16]{0,1:T(8,128)}, f32[32,16]{0,1:T(8,128)S(1)}, u32[]{:S(2)}, u32[]{:S(2)}) collective-permute-start(f32[32,16]{0,1:T(8,128)} %param.31), channel_id=1, source_target_pairs={{0,1},{1,0},{2,3},{3,2},{4,5},{5,4},{6,7},{7,6},{8,9},{9,8},{10,11... | collective-permute-start | bytes 6152 | tf_op jit(solution)/shard_map/ppermute | solution.py:40
  6.6 32.5 %collective-permute-start.6 = (f32[32,65]{0,1:T(8,128)S(1)}, f32[32,65]{0,1:T(8,128)S(1)}, u32[]{:S(2)}, u32[]{:S(2)}) collective-permute-start(f32[32,65]{0,1:T(8,128)S(1)} %concatenate.127), channel_id=1, source_target_pairs={{0,1},{1,0},{2,3},{3,2},{4,5},{5,4},{6,7},{7,6},{8,9},{9,8},{10,11... | collective-permute-start | bytes 24968 | tf_op jit(solution)/shard_map/ppermute | solution.py:40
  7.9 46.4 %collective-permute-start = (f32[128,1024]{1,0:T(8,128)S(1)}, f32[128,1024]{1,0:T(8,128)S(1)}, u32[]{:S(2)}, u32[]{:S(2)}) collective-permute-start(f32[128,1024]{1,0:T(8,128)S(1)} %slice.282), channel_id=1, source_target_pairs={{0,2},{2,4},{4,6},{6,8},{8,10},{10,12},{12,14},{14,16},{16,18},{18... | collective-permute-start | bytes 1572872 | tf_op jit(solution)/shard_map/ppermute | solution.py:50
  11.6 70.1 %collective-permute-start.16 = (f32[256,1024]{1,0:T(8,128)}, f32[256,1024]{1,0:T(8,128)}, u32[]{:S(2)}, u32[]{:S(2)}) collective-permute-start(f32[256,1024]{1,0:T(8,128)} %dynamic-slice_convert_fusion), channel_id=1, source_target_pairs={{0,1},{1,0},{2,3},{3,2},{4,5},{5,4},{6,7},{7,6},{8,9},{9,8},{10,11... | collective-permute-start | bytes 3145736 | tf_op jit(solution)/shard_map/ppermute | solution.py:40
  81.6 33.2 %collective-permute-start.17 = (f32[256,1024]{1,0:T(8,128)}, f32[256,1024]{1,0:T(8,128)S(1)}, u32[]{:S(2)}, u32[]{:S(2)}) collective-permute-start(f32[256,1024]{1,0:T(8,128)} %collective-permute-done.16), channel_id=1, source_target_pairs={{0,2},{2,0},{4,6},{6,4},{8,10},{10,8},{12,14},{14,12},{16,18},{18,... | collective-permute-start | bytes 3145736 | tf_op jit(solution)/shard_map/ppermute | solution.py:40
  89.4 28.7 %collective-permute-start.15 = (f32[256,512]{1,0:T(8,128)S(1)}, f32[256,512]{1,0:T(8,128)S(1)}, u32[]{:S(2)}, u32[]{:S(2)}) collective-permute-start(f32[256,512]{1,0:T(8,128)S(1)} %get-tuple-element.50.o0_ref), channel_id=1, source_target_pairs={{0,1},{1,0},{2,3},{3,2},{4,5},{5,4},{6,7},{7,6},{8,9},{9,8},{10,11... | collective-permute-start | bytes 1572872 | tf_op jit(solution)/shard_map/ppermute | solution.py:40
  93.4 21.4 %collective-permute-start.18 = (f32[256,512]{1,0:T(8,128)S(1)}, f32[256,512]{1,0:T(8,128)S(1)}, u32[]{:S(2)}, u32[]{:S(2)}) collective-permute-start(f32[256,512]{1,0:T(8,128)S(1)} %get-tuple-element.52.o1_ref), channel_id=1, source_target_pairs={{0,1},{1,0},{2,3},{3,2},{4,5},{5,4},{6,7},{7,6},{8,9},{9,8},{10,11... | collective-permute-start | bytes 1572872 | tf_op jit(solution)/shard_map/ppermute | solution.py:40
  158.6 48.4 %collective-permute-start.22 = (f32[256,1024]{1,0:T(8,128)}, f32[256,1024]{1,0:T(8,128)}, u32[]{:S(2)}, u32[]{:S(2)}) collective-permute-start(f32[256,1024]{1,0:T(8,128)} %fusion.170), channel_id=1, source_target_pairs={{0,1},{1,0},{2,3},{3,2},{4,5},{5,4},{6,7},{7,6},{8,9},{9,8},{10,11... | collective-permute-start | bytes 3145736 | tf_op jit(solution)/shard_map/ppermute | solution.py:40
  160.0 18.0 %collective-permute-start.45 = (f32[128,1024]{1,0:T(8,128)}, f32[128,1024]{1,0:T(8,128)}, u32[]{:S(2)}, u32[]{:S(2)}) collective-permute-start(f32[128,1024]{1,0:T(8,128)} %constant_dynamic-slice_fusion.16), channel_id=1, source_target_pairs={{0,8},{10,2},{8,16},{18,10},{16,24},{26,18},{24,28},{30,26},{28,20... | collective-permute-start | bytes 1572872 | tf_op jit(solution)/shard_map/ppermute | solution.py:144
  160.8 46.1 %collective-permute-start.21 = (f32[256,1024]{1,0:T(8,128)}, f32[256,1024]{1,0:T(8,128)}, u32[]{:S(2)}, u32[]{:S(2)}) collective-permute-start(f32[256,1024]{1,0:T(8,128)} %fusion.173), channel_id=1, source_target_pairs={{0,1},{1,0},{2,3},{3,2},{4,5},{5,4},{6,7},{7,6},{8,9},{9,8},{10,11... | collective-permute-start | bytes 3145736 | tf_op jit(solution)/shard_map/ppermute | solution.py:40
  172.3 178.0 %collective-permute-start.20 = (f32[512,2048]{1,0:T(8,128)}, f32[512,2048]{1,0:T(8,128)}, u32[]{:S(2)}, u32[]{:S(2)}) collective-permute-start(f32[512,2048]{1,0:T(8,128)} %convolution_add_fusion), channel_id=1, source_target_pairs={{0,2},{2,0},{4,6},{6,4},{8,10},{10,8},{12,14},{14,12},{16,18},{18,... | collective-permute-start | bytes 12582920 | tf_op jit(solution)/shard_map/ppermute | solution.py:40
  180.1 119.6 %collective-permute-start.46 = (f32[128,1024]{1,0:T(8,128)}, f32[128,1024]{1,0:T(8,128)}, u32[]{:S(2)}, u32[]{:S(2)}) collective-permute-start(f32[128,1024]{1,0:T(8,128)} %dynamic-slice_add_fusion.13), channel_id=1, source_target_pairs={{0,8},{10,2},{8,16},{18,10},{16,24},{26,18},{24,28},{30,26},{28,20... | collective-permute-start | bytes 1572872 | tf_op jit(solution)/shard_map/ppermute | solution.py:144
  255.6 18.7 %collective-permute-start.34 = (f32[16,1024]{1,0:T(8,128)}, f32[16,1024]{1,0:T(8,128)}, u32[]{:S(2)}, u32[]{:S(2)}) collective-permute-start(f32[16,1024]{1,0:T(8,128)} %shard_map.369), channel_id=1, source_target_pairs={{0,2},{2,0},{4,6},{6,4},{8,10},{10,8},{12,14},{14,12},{16,18},{18,... | collective-permute-start | bytes 196616 | tf_op jit(solution)/shard_map/ppermute | solution.py:40
  281.7 63.8 %collective-permute-start.44 = (f32[512,512]{1,0:T(8,128)}, f32[512,512]{1,0:T(8,128)}, u32[]{:S(2)}, u32[]{:S(2)}) collective-permute-start(f32[512,512]{1,0:T(8,128)} %convolution_add_fusion.5), channel_id=1, source_target_pairs={{0,2},{2,0},{4,6},{6,4},{8,10},{10,8},{12,14},{14,12},{16,18},{18,... | collective-permute-start | bytes 3145736 | tf_op jit(solution)/shard_map/ppermute | solution.py:40
  283.6 15.5 %collective-permute-start.38 = (f32[512,128]{0,1:T(8,128)S(1)}, f32[512,128]{0,1:T(8,128)S(1)}, u32[]{:S(2)}, u32[]{:S(2)}) collective-permute-start(f32[512,128]{0,1:T(8,128)S(1)} %bitcast.352), channel_id=1, source_target_pairs={{0,16},{2,18},{4,20},{6,22},{8,24},{10,26},{12,28},{14,30},{16,0},... | collective-permute-start | bytes 786440 | tf_op jit(solution)/shard_map/ppermute | solution.py:40
  307.4 48.3 %collective-permute-start.43 = (f32[512,512]{1,0:T(8,128)}, f32[512,512]{1,0:T(8,128)}, u32[]{:S(2)}, u32[]{:S(2)}) collective-permute-start(f32[512,512]{1,0:T(8,128)} %fusion.43), channel_id=1, source_target_pairs={{0,2},{2,0},{4,6},{6,4},{8,10},{10,8},{12,14},{14,12},{16,18},{18,... | collective-permute-start | bytes 3145736 | tf_op jit(solution)/shard_map/ppermute | solution.py:40
  308.2 18.2 %collective-permute-start.47 = (f32[128,1024]{1,0:T(8,128)}, f32[128,1024]{1,0:T(8,128)}, u32[]{:S(2)}, u32[]{:S(2)}) collective-permute-start(f32[128,1024]{1,0:T(8,128)} %dynamic-slice_add_fusion.12), channel_id=1, source_target_pairs={{0,8},{10,2},{8,16},{18,10},{16,24},{26,18},{24,28},{30,26},{28,20... | collective-permute-start | bytes 1572872 | tf_op jit(solution)/shard_map/ppermute | solution.py:144
  325.9 50.6 %collective-permute-start.95 = (f32[512,1024]{1,0:T(8,128)}, f32[512,1024]{1,0:T(8,128)}, u32[]{:S(2)}, u32[]{:S(2)}) collective-permute-start(f32[512,1024]{1,0:T(8,128)} %convolution_add_fusion.4), channel_id=1, source_target_pairs={{0,2},{2,0},{4,6},{6,4},{8,10},{10,8},{12,14},{14,12},{16,18},{18,... | collective-permute-start | bytes 6291464 | tf_op jit(solution)/shard_map/ppermute | solution.py:40
  334.3 14.3 %collective-permute-start.48 = (f32[128,1024]{1,0:T(8,128)}, f32[128,1024]{1,0:T(8,128)S(1)}, u32[]{:S(2)}, u32[]{:S(2)}) collective-permute-start(f32[128,1024]{1,0:T(8,128)} %dynamic-slice_add_fusion.11), channel_id=1, source_target_pairs={{0,8},{10,2},{8,16},{18,10},{16,24},{26,18},{24,28},{30,26},{28,20... | collective-permute-start | bytes 1572872 | tf_op jit(solution)/shard_map/ppermute | solution.py:144
  345.4 48.3 %collective-permute-start.29 = (f32[512,1024]{1,0:T(8,128)S(1)}, f32[512,1024]{1,0:T(8,128)S(1)}, u32[]{:S(2)}, u32[]{:S(2)}) collective-permute-start(f32[512,1024]{1,0:T(8,128)S(1)} %maximum_add_fusion.2), channel_id=1, source_target_pairs={{0,1},{1,0},{2,3},{3,2},{4,5},{5,4},{6,7},{7,6},{8,9},{9,8},{10,11... | collective-permute-start | bytes 6291464 | tf_op jit(solution)/shard_map/ppermute | solution.py:40
  382.2 25.8 %collective-permute-start.52 = (f32[128,1024]{1,0:T(8,128)}, f32[128,1024]{1,0:T(8,128)}, u32[]{:S(2)}, u32[]{:S(2)}) collective-permute-start(f32[128,1024]{1,0:T(8,128)} %get-tuple-element.185), channel_id=1, source_target_pairs={{0,8},{10,2},{8,16},{18,10},{16,24},{26,18},{24,28},{30,26},{28,20... | collective-permute-start | bytes 1572872 | tf_op jit(solution)/shard_map/ppermute | solution.py:173
  402.1 41.1 %collective-permute-start.126 = (f32[128,1024]{1,0:T(8,128)}, f32[128,1024]{1,0:T(8,128)S(1)}, u32[]{:S(2)}, u32[]{:S(2)}) collective-permute-start(f32[128,1024]{1,0:T(8,128)} %get-tuple-element.185), channel_id=1, source_target_pairs={{0,2},{2,0},{4,6},{6,4},{8,10},{10,8},{12,14},{14,12},{16,18},{18,... | collective-permute-start | bytes 1572872 | tf_op jit(solution)/shard_map/ppermute | solution.py:40
  412.3 27.8 %collective-permute-start.33 = (f32[7,1024]{1,0:T(8,128)S(1)}, f32[7,1024]{1,0:T(8,128)S(1)}, u32[]{:S(2)}, u32[]{:S(2)}) collective-permute-start(f32[7,1024]{1,0:T(8,128)S(1)} %add.2061), channel_id=1, source_target_pairs={{0,16},{2,18},{4,20},{6,22},{8,24},{10,26},{12,28},{14,30},{16,0},... | collective-permute-start | bytes 86024 | tf_op jit(solution)/shard_map/ppermute | solution.py:40
  429.3 44.4 %collective-permute-start.23 = (f32[512,1024]{1,0:T(8,128)S(1)}, f32[512,1024]{1,0:T(8,128)S(1)}, u32[]{:S(2)}, u32[]{:S(2)}) collective-permute-start(f32[512,1024]{1,0:T(8,128)S(1)} %pad_maximum_fusion), channel_id=1, source_target_pairs={{0,1},{1,0},{2,3},{3,2},{4,5},{5,4},{6,7},{7,6},{8,9},{9,8},{10,11... | collective-permute-start | bytes 6291464 | tf_op jit(solution)/shard_map/ppermute | solution.py:40
  443.2 16.3 %collective-permute-start.128 = (f32[128,1024]{1,0:T(8,128)S(1)}, f32[128,1024]{1,0:T(8,128)S(1)}, u32[]{:S(2)}, u32[]{:S(2)}) collective-permute-start(f32[128,1024]{1,0:T(8,128)S(1)} %collective-permute-done.53), channel_id=1, source_target_pairs={{0,2},{2,0},{4,6},{6,4},{8,10},{10,8},{12,14},{14,12},{16,18},{18,... | collective-permute-start | bytes 1572872 | tf_op jit(solution)/shard_map/ppermute | solution.py:40
  456.9 16.7 %collective-permute-start.68 = (f32[64,2048]{1,0:T(8,128)S(1)}, f32[64,2048]{1,0:T(8,128)S(1)}, u32[]{:S(2)}, u32[]{:S(2)}) collective-permute-start(f32[64,2048]{1,0:T(8,128)S(1)} %collective-permute-done.67), channel_id=1, source_target_pairs={{0,8},{10,2},{8,16},{18,10},{16,24},{26,18},{24,28},{30,26},{28,20... | collective-permute-start | bytes 1572872 | tf_op jit(solution)/shard_map/ppermute | solution.py:173
  459.6 17.7 %collective-permute-start.130 = (f32[128,1024]{1,0:T(8,128)S(1)}, f32[128,1024]{1,0:T(8,128)S(1)}, u32[]{:S(2)}, u32[]{:S(2)}) collective-permute-start(f32[128,1024]{1,0:T(8,128)S(1)} %collective-permute-done.55), channel_id=1, source_target_pairs={{0,2},{2,0},{4,6},{6,4},{8,10},{10,8},{12,14},{14,12},{16,18},{18,... | collective-permute-start | bytes 1572872 | tf_op jit(solution)/shard_map/ppermute | solution.py:40
  462.6 14.8 %collective-permute-start.58 = (f32[128,1024]{1,0:T(8,128)S(1)}, f32[128,1024]{1,0:T(8,128)S(1)}, u32[]{:S(2)}, u32[]{:S(2)}) collective-permute-start(f32[128,1024]{1,0:T(8,128)S(1)} %collective-permute-done.57), channel_id=1, source_target_pairs={{0,8},{10,2},{8,16},{18,10},{16,24},{26,18},{24,28},{30,26},{28,20... | collective-permute-start | bytes 1572872 | tf_op jit(solution)/shard_map/ppermute | solution.py:173
  484.8 18.0 %collective-permute-start.120 = (f32[64,2048]{1,0:T(8,128)S(1)}, f32[64,2048]{1,0:T(8,128)S(1)}, u32[]{:S(2)}, u32[]{:S(2)}) collective-permute-start(f32[64,2048]{1,0:T(8,128)S(1)} %collective-permute-done.67), channel_id=1, source_target_pairs={{0,2},{2,0},{4,6},{6,4},{8,10},{10,8},{12,14},{14,12},{16,18},{18,... | collective-permute-start | bytes 1572872 | tf_op jit(solution)/shard_map/ppermute | solution.py:40
  512.0 15.7 %collective-permute-start.123 = (f32[64,2048]{1,0:T(8,128)S(1)}, f32[64,2048]{1,0:T(8,128)S(1)}, u32[]{:S(2)}, u32[]{:S(2)}) collective-permute-start(f32[64,2048]{1,0:T(8,128)S(1)} %collective-permute-done.70), channel_id=1, source_target_pairs={{0,2},{2,0},{4,6},{6,4},{8,10},{10,8},{12,14},{14,12},{16,18},{18,... | collective-permute-start | bytes 1572872 | tf_op jit(solution)/shard_map/ppermute | solution.py:40
  521.3 19.4 %collective-permute-start.124 = (f32[64,2048]{1,0:T(8,128)S(1)}, f32[64,2048]{1,0:T(8,128)S(1)}, u32[]{:S(2)}, u32[]{:S(2)}) collective-permute-start(f32[64,2048]{1,0:T(8,128)S(1)} %collective-permute-done.71), channel_id=1, source_target_pairs={{0,2},{2,0},{4,6},{6,4},{8,10},{10,8},{12,14},{14,12},{16,18},{18,... | collective-permute-start | bytes 1572872 | tf_op jit(solution)/shard_map/ppermute | solution.py:40
  534.3 19.4 %collective-permute-start.125 = (f32[64,2048]{1,0:T(8,128)S(1)}, f32[64,2048]{1,0:T(8,128)S(1)}, u32[]{:S(2)}, u32[]{:S(2)}) collective-permute-start(f32[64,2048]{1,0:T(8,128)S(1)} %collective-permute-done.72), channel_id=1, source_target_pairs={{0,2},{2,0},{4,6},{6,4},{8,10},{10,8},{12,14},{14,12},{16,18},{18,... | collective-permute-start | bytes 1572872 | tf_op jit(solution)/shard_map/ppermute | solution.py:40
  (238 other events, 2090.2 us)

commit v3 on v2

v3 whole, which is shorter than its diff:
```python
import functools
import math

import jax
import jax.numpy as jnp
from jax import lax
from jax.experimental import pallas as pl
from jax.experimental.pallas import tpu as pltpu
from jax.sharding import PartitionSpec as P

HDIM = 128
BLOCK = 512
CTX = 128
LEN = 4096
EPS = 1e-05
HIGH = lax.Precision.HIGH


def mm(left, right, dims=((1,), (0,))):
    return lax.dot_general(
        left, right, (dims, ((), ())), precision=HIGH, preferred_element_type=jnp.float32
    )


def norm_parts(value):
    center = value - jnp.mean(value, axis=-1, keepdims=True)
    spread = jnp.mean(center * center, axis=-1, keepdims=True)
    rate = lax.rsqrt(spread + EPS)
    return center * rate, rate


def norm_back(grad, unit, rate, gain):
    scaled = grad * gain
    inner = jnp.mean(scaled * unit, axis=-1, keepdims=True)
    return rate * (scaled - jnp.mean(scaled, axis=-1, keepdims=True) - unit * inner)


def swap_bit(value, axis, bit):
    size = lax.axis_size(axis)
    return lax.ppermute(value, axis, [(i, i ^ (1 << bit)) for i in range(size)])


def bits_of(count):
    return count.bit_length() - 1


def shift_in_window(value, distance, per_window):
    size = lax.axis_size("seq")
    route = [(i, i + distance) for i in range(size)]
    inside = [(a, b) for a, b in route if 0 <= b < size and a // per_window == b // per_window]
    return lax.ppermute(value, "seq", inside)


def after(value, *others):
    return lax.optimization_barrier((value,) + others)[0]


def gather_all(piece, gates=()):
    mp_size, seq_size = lax.axis_size("mp"), lax.axis_size("seq")
    me = lax.axis_index("seq") * mp_size + lax.axis_index("mp")
    block, seen = piece, []
    for bit in range(bits_of(mp_size * seq_size)):
        axis, own = ("mp", bit) if bit < bits_of(mp_size) else ("seq", bit - bits_of(mp_size))
        if gates:
            block = after(block, gates[bit])
        other = swap_bit(block, axis, own)
        upper = (me >> bit) & 1
        block = jnp.where(
            upper == 1, jnp.concatenate([other, block], 1), jnp.concatenate([block, other], 1)
        )
        seen.append(block)
    return block, seen


def trade_chips(value, distance):
    size = lax.axis_size("seq")
    return lax.ppermute(value, "seq", [(i, i ^ (2 * distance)) for i in range(size)])


def chip_order(count):
    if count <= 2:
        return list(range(count))
    return list(range(0, count, 2)) + list(range(count - 1 - count % 2, 0, -2))


def ring_route(count):
    order = chip_order(count)
    route = []
    for i in range(count):
        here, there = order[i], order[(i + 1) % count]
        route.append((2 * here, 2 * there))
        route.append((2 * there + 1, 2 * here + 1))
    return route


def ring_spot():
    count = lax.axis_size("seq") // 2
    places = [0] * count
    for i, chip in enumerate(chip_order(count)):
        places[chip] = i
    me = lax.axis_index("seq")
    here = jnp.array(places, jnp.int32)[me // 2]
    return jnp.where(me % 2 == 0, here, (count - here) % count)


def unset(shape):
    return pl.pallas_call(
        lambda out: None,
        out_shape=jax.ShapeDtypeStruct(shape, jnp.float32),
        out_specs=pl.BlockSpec(memory_space=pl.ANY),
    )()


def pick(value, index):
    return lax.dynamic_index_in_dim(value, index, 0, keepdims=False)


class Clock:
    def __init__(self):
        self.last = ()

    def hold(self, value):
        return after(value, *self.last) if self.last else value

    def set(self, *values):
        self.last = values


def assemble_kernel(count, cuts, where_ref, *refs):
    parts, outs, sems = refs[: 2 * count], refs[2 * count : -1], refs[-1]
    copies = []
    for n in range(2 * count):
        which, spot = where_ref[0, n], where_ref[1, n]
        for out, (low, high) in zip(outs, cuts):
            copies.append(
                pltpu.make_async_copy(
                    parts[n].at[low:high], out.at[:, which, spot], sems.at[len(copies)]
                )
            )
    for copy in copies:
        copy.start()
    for copy in copies:
        copy.wait()


class Ring:
    def __init__(self, pieces, outs):
        self.count = lax.axis_size("seq") // 2
        self.place, self.route = ring_spot(), ring_route(self.count)
        self.core = lax.axis_index("seq") % 2
        self.mirror = (self.count - self.place) % self.count
        self.rows, self.cols = pieces[0][0].shape[0] // self.count, pieces[0][0].shape[1]
        self.pieces = [
            [a.reshape(self.count, self.rows, self.cols) for a in addends] for addends in pieces
        ]
        self.outs = outs
        self.step, self.own, self.far = 0, [], []
        self.held = self.chunk(self.place)

    def chunk(self, spot):
        return jnp.stack([sum(pick(a, spot) for a in addends) for addends in self.pieces])

    def turn(self, clock):
        got = clock.hold(lax.ppermute(self.held, "seq", self.route))
        self.step += 1
        if self.step < self.count:
            got = got + self.chunk((self.place + 2 * self.count - self.step) % self.count)
        self.held = got
        if self.step >= self.count - 1:
            self.own.append(got)
            self.far.append(swap_bit(got, "seq", 0))
        clock.set(got)

    def results(self):
        count = self.count
        hops = jnp.arange(count, dtype=jnp.int32)
        spots = jnp.concatenate([self.place + 1 - hops, self.mirror + 1 - hops]) + count
        which = jnp.repeat(jnp.stack([self.core, 1 - self.core]), count)
        where = jnp.stack([which, spots % count]).astype(jnp.int32)
        cuts, low = [], 0
        for size in self.outs:
            cuts.append((low, low + size))
            low += size
        shapes = [(size, 2, count, self.rows, self.cols) for size in self.outs]
        outs = pl.pallas_call(
            functools.partial(assemble_kernel, count, cuts),
            in_specs=[pl.BlockSpec(memory_space=pltpu.SMEM)]
            + [pl.BlockSpec(memory_space=pltpu.VMEM)] * (2 * count),
            out_specs=[pl.BlockSpec(memory_space=pl.ANY)] * len(shapes),
            out_shape=[jax.ShapeDtypeStruct(shape, jnp.float32) for shape in shapes],
            scratch_shapes=[pltpu.SemaphoreType.DMA((2 * count * len(shapes),))],
            cost_estimate=pl.CostEstimate(
                flops=0, bytes_accessed=8 * sum(math.prod(a) for a in shapes), transcendentals=0
            ),
        )(where, *self.own, *self.far)
        return [out.reshape(out.shape[0], -1, self.cols) for out in outs]


def core_half(value, which):
    size = value.shape[1] // 2
    return lax.dynamic_slice_in_dim(value, which * size, size, 1)


def rows8(shape):
    return lax.broadcasted_iota(jnp.int32, shape, 0).astype(jnp.float32)


def tree(values):
    values = list(values)
    while len(values) > 1:
        values = [sum(values[i : i + 2]) for i in range(0, len(values), 2)]
    return values[0]


def groups(decay_ref):
    states, lanes = decay_ref.shape
    for low in range(0, lanes, 128):
        span = slice(low, low + 128)
        rates = [jnp.broadcast_to(decay_ref[n : n + 1, span], (8, 128)) for n in range(states)]
        yield span, rates, [jnp.exp(-8.0 * rate) for rate in rates]


UNROLL = 4


def over_rows(ref, count, span, body, carry):
    def step(i, carry):
        for k in range(UNROLL):
            base = pl.multiple_of((i * UNROLL + k) * 8, 8)
            carry = body(ref[pl.ds(base, 8), span], carry)
        return carry

    return lax.fori_loop(0, count // (8 * UNROLL), step, carry)


def summary_kernel(tail_ref, x_ref, decay_ref, h_ref):
    for span, rates, jump in groups(decay_ref):

        def body(tile, acc):
            return tuple(j * a + tile for j, a in zip(jump, acc))

        acc = (tail_ref[:8, span] * 0.0,) * len(rates)
        acc = over_rows(tail_ref, tail_ref.shape[0], span, body, acc)
        acc = over_rows(x_ref, x_ref.shape[0] - tail_ref.shape[0], span, body, acc)
        left = 7.0 - rows8((8, 128))
        for n, rate in enumerate(rates):
            h_ref[n : n + 1, span] = jnp.sum(acc[n] * jnp.exp(-rate * left), axis=0, keepdims=True)


def moment_kernel(tail_ref, x_ref, decay_ref, p_ref):
    for span, rates, jump in groups(decay_ref):

        def body(tile, carry):
            acc, lag = carry
            lag = tuple(j * (b + a) for j, a, b in zip(jump, acc, lag))
            return tuple(j * a + tile for j, a in zip(jump, acc)), lag

        zeros = (tail_ref[:8, span] * 0.0,) * len(rates)
        carry = over_rows(tail_ref, tail_ref.shape[0], span, body, (zeros, zeros))
        acc, lag = over_rows(x_ref, x_ref.shape[0] - tail_ref.shape[0], span, body, carry)
        left = 7.0 - rows8((8, 128))
        for n, rate in enumerate(rates):
            total = (8.0 * lag[n] + left * acc[n]) * jnp.exp(-rate * left)
            p_ref[n : n + 1, span] = jnp.sum(total, axis=0, keepdims=True)


def carry_kernel(near_ref, first_ref, decay_ref, y_ref):
    for span, rates, jump in groups(decay_ref):
        ahead = rows8((8, 128)) + 1.0
        modes = tuple(
            jnp.broadcast_to(first_ref[n : n + 1, span], (8, 128)) * jnp.exp(-rate * ahead)
            for n, rate in enumerate(rates)
        )

        def step(i, modes):
            for k in range(UNROLL):
                base = pl.multiple_of((i * UNROLL + k) * 8, 8)
                y_ref[pl.ds(base, 8), span] = near_ref[pl.ds(base, 8), span] + tree(modes)
                modes = tuple(j * m for j, m in zip(jump, modes))
            return modes

        lax.fori_loop(0, y_ref.shape[0] // (8 * UNROLL), step, modes)


def spread_kernel(first_ref, decay_ref, tail_ref, y_ref):
    for span, rates, jump in groups(decay_ref):
        ahead = 8.0 - rows8((8, 128))
        modes = tuple(
            jnp.broadcast_to(first_ref[n : n + 1, span], (8, 128)) * jnp.exp(-rate * ahead)
            for n, rate in enumerate(rates)
        )

        def run(ref, modes):
            count = ref.shape[0] // 8

            def step(i, modes):
                for k in range(UNROLL):
                    base = pl.multiple_of((count - 1 - i * UNROLL - k) * 8, 8)
                    ref[pl.ds(base, 8), span] = tree(modes)
                    modes = tuple(j * m for j, m in zip(jump, modes))
                return modes

            return lax.fori_loop(0, count // UNROLL, step, modes)

        run(tail_ref, run(y_ref, modes))


def near_kernel(x_ref, fade_ref, gate_ref, skip_ref, y_ref):
    fade, gate, skip = fade_ref[...], gate_ref[...], skip_ref[...]

    def octet(i, u):
        base = pl.multiple_of(i * 8, 8)
        tile = x_ref[pl.ds(base, 8), :]
        rows = []
        for r in range(8):
            row = tile[r : r + 1, :]
            u = fade * u + gate * jnp.broadcast_to(row, fade.shape)
            rows.append(jnp.sum(u, axis=0, keepdims=True) + skip * row)
        y_ref[pl.ds(base, 8), :] = jnp.concatenate(rows, 0)
        return u

    lax.fori_loop(0, x_ref.shape[0] // 8, octet, jnp.zeros(fade.shape, jnp.float32))


def tail_back_kernel(
    x_ref, d_ref, fade_ref, gate_ref, skip_ref, q_ref, r_ref, dh_ref, dp_ref, dskip_ref, dx_ref
):
    fade, gate, skip = fade_ref[...], gate_ref[...], skip_ref[...]
    octets = x_ref.shape[0] // 8
    zero = jnp.zeros(fade.shape, jnp.float32)

    def forward(i, carry):
        h, p, dh, dp = carry
        base = pl.multiple_of(i * 8, 8)
        tile, grads = x_ref[pl.ds(base, 8), :], d_ref[pl.ds(base, 8), :]
        for r in range(8):
            p = fade * (p + h)
            h = fade * h + jnp.broadcast_to(tile[r : r + 1, :], fade.shape)
            grad = jnp.broadcast_to(grads[r : r + 1, :], fade.shape)
            dh = dh + grad * h
            dp = dp + grad * p
        return h, p, dh, dp

    _, _, dh, dp = lax.fori_loop(0, octets, forward, (zero, zero, zero, zero))
    dh_ref[...] = dh
    dp_ref[...] = dp
    dskip_ref[...] = jnp.sum(x_ref[...] * d_ref[...], axis=0, keepdims=True)

    def backward(k, carry):
        q, r_sum = carry
        base = pl.multiple_of((octets - 1 - k) * 8, 8)
        grads = d_ref[pl.ds(base, 8), :]
        rows = [None] * 8
        for r in reversed(range(8)):
            r_sum = fade * (r_sum + q)
            grad = grads[r : r + 1, :]
            q = fade * q + jnp.broadcast_to(grad, fade.shape)
            rows[r] = jnp.sum(gate * q, axis=0, keepdims=True) + skip * grad
        dx_ref[pl.ds(base, 8), :] = jnp.concatenate(rows, 0)
        return q, r_sum

    q, r_sum = lax.fori_loop(0, octets, backward, (zero, zero))
    q_ref[...] = q
    r_ref[...] = r_sum


def by_channels(kernel, ins, outs, cut=512):
    width = ins[0].shape[1]
    cut = cut if width % cut == 0 else width

    def spec(rows):
        return pl.BlockSpec((rows, cut), lambda i: (0, i))

    return pl.pallas_call(
        kernel,
        grid=(width // cut,),
        in_specs=[spec(a.shape[0]) for a in ins],
        out_specs=[spec(r) for r in outs],
        out_shape=[jax.ShapeDtypeStruct((r, width), jnp.float32) for r in outs],
        cost_estimate=pl.CostEstimate(flops=0, bytes_accessed=COST, transcendentals=0),
    )(*ins)


def cut(value):
    top = value.astype(jnp.bfloat16)
    return top, (value - top.astype(jnp.float32)).astype(jnp.bfloat16)


def dot3(left, right, dims):
    def one(a, b):
        return lax.dot_general(a, b, (dims, ((), ())), preferred_element_type=jnp.float32)

    return one(left[0], right[1]) + one(left[1], right[0]) + one(left[0], right[0])


NT = ((1,), (1,))
NN = ((1,), (0,))
TN = ((0,), (0,))
TILE = 256
LATE = 4
COST = 1024
SCALE = HDIM ** (-0.5)


def causal(shape, first_row):
    row = lax.broadcasted_iota(jnp.int32, shape, 0) + first_row
    return lax.broadcasted_iota(jnp.int32, shape, 1) <= row


def self_kernel(q_ref, k_ref, v_ref, acc_ref, top_ref, sum_ref):
    rows = q_ref.shape[0]
    k, v = cut(k_ref[...]), cut(v_ref[...])
    for first in range(0, rows, TILE):
        span = slice(first, first + TILE)
        seen = first + TILE
        q = cut(q_ref[span, :] * SCALE)
        scores = dot3(q, (k[0][:seen], k[1][:seen]), NT)
        scores = jnp.where(causal(scores.shape, first), scores, -1e30)
        top = jnp.max(scores, axis=1, keepdims=True)
        weight = jnp.exp(scores - top)
        acc_ref[span, :] = dot3(cut(weight), (v[0][:seen], v[1][:seen]), NN)
        top_ref[span, :] = jnp.broadcast_to(top, (TILE, HDIM))
        sum_ref[span, :] = jnp.broadcast_to(jnp.sum(weight, axis=1, keepdims=True), (TILE, HDIM))


def ctx_kernel(ok_ref, q_ref, k_ref, v_ref, acc_ref, top_ref, sum_ref, out_ref, log_ref):
    ok = ok_ref[0] > 0
    q = cut(q_ref[...] * SCALE)
    scores = dot3(q, cut(k_ref[...]), NT)
    scores = jnp.where(ok, scores, -1e30)
    top = jnp.maximum(top_ref[...], jnp.max(scores, axis=1, keepdims=True))
    weight = jnp.where(ok, jnp.exp(scores - top[:, :1]), 0.0)
    ease = jnp.exp(top_ref[...] - top)
    total = sum_ref[...] * ease + jnp.sum(weight, axis=1, keepdims=True)
    out_ref[...] = (acc_ref[...] * ease + dot3(cut(weight), cut(v_ref[...]), NN)) / total
    log_ref[...] = top + jnp.log(total)


def back_kernel(ok_ref, q_ref, k_ref, v_ref, kc_ref, vc_ref, o_ref, l_ref, g_ref, d_ref):
    ok = ok_ref[0] > 0
    rows = q_ref.shape[0]
    k, v, kc, vc = cut(k_ref[...]), cut(v_ref[...]), cut(kc_ref[...]), cut(vc_ref[...])
    d_ref[0, :CTX, :] = jnp.zeros((CTX, HDIM), jnp.float32)
    for first in reversed(range(0, rows, TILE)):
        seen = first + TILE
        span = slice(first, seen)
        grad = g_ref[span, :]
        q = cut(q_ref[span, :] * SCALE)
        grad2 = cut(grad)
        inner = jnp.sum(grad * o_ref[span, :], axis=1, keepdims=True)
        mark = l_ref[span, :][:, :1]
        ks, vs = (k[0][:seen], k[1][:seen]), (v[0][:seen], v[1][:seen])
        probs = dot3(q, ks, NT)
        probs = jnp.where(causal(probs.shape, first), jnp.exp(probs - mark), 0.0)
        probs_c = jnp.where(ok, jnp.exp(dot3(q, kc, NT) - mark), 0.0)
        ds = cut(probs * (dot3(grad2, vs, NT) - inner))
        ds_c = cut(probs_c * (dot3(grad2, vc, NT) - inner))
        probs, probs_c = cut(probs), cut(probs_c)
        d_ref[0, CTX + first : CTX + seen, :] = (dot3(ds, ks, NN) + dot3(ds_c, kc, NN)) * SCALE
        for at, (own, ctx, other) in enumerate([(ds, ds_c, q), (probs, probs_c, grad2)]):
            near, back = dot3(own, other, TN), dot3(ctx, other, TN)
            if seen == rows:
                d_ref[1 + at, CTX:, :] = near
                d_ref[1 + at, :CTX, :] = back
            else:
                d_ref[1 + at, CTX : CTX + seen, :] += near
                d_ref[1 + at, :CTX, :] += back


def by_heads(kernel, ins, outs, scalars=()):
    heads = ins[0][0].shape[1] // HDIM
    specs = [pl.BlockSpec(memory_space=pltpu.SMEM) for _ in scalars]
    for _, rows, at in ins:
        specs.append(pl.BlockSpec((rows, HDIM), lambda h, at=at: (at, h)))
    return pl.pallas_call(
        kernel,
        grid=(heads,),
        in_specs=specs,
        out_specs=[
            pl.BlockSpec(lead + (HDIM,), lambda h, n=len(lead): (0,) * n + (h,)) for lead in outs
        ],
        out_shape=[jax.ShapeDtypeStruct(lead + (heads * HDIM,), jnp.float32) for lead in outs],
        cost_estimate=pl.CostEstimate(flops=0, bytes_accessed=COST, transcendentals=0),
        compiler_params=pltpu.CompilerParams(vmem_limit_bytes=40 << 20),
    )(*scalars, *[a for a, _, _ in ins])


def per_device(
    tokens,
    window_state,
    norm1_gain,
    norm1_bias,
    in_coef,
    out_coef,
    decay_rate,
    skip_gain,
    qkv_weight,
    out_weight,
    norm2_gain,
    norm2_bias,
    up_weight,
    up_bias,
    down_weight,
    down_bias,
    cotangent,
):
    place_seq = lax.axis_index("seq")
    core = place_seq % 2
    rows, width = tokens.shape
    states = in_coef.shape[1]
    windows = window_state.shape[0]
    per_window = LEN // rows
    block = place_seq % per_window
    window = place_seq // per_window
    has_ctx = block > 0
    ok = has_ctx.astype(jnp.int32).reshape(1)
    half = rows // 2

    qkv = qkv_weight.astype(jnp.float32)
    out_own = out_weight.astype(jnp.float32)
    up = up_weight.astype(jnp.float32)
    down = down_weight.astype(jnp.float32)

    packed = jnp.concatenate(
        [jnp.transpose(a) for a in (decay_rate, in_coef, out_coef)]
        + [jnp.transpose(window_state[w]) for w in range(windows)]
        + [skip_gain[None]],
        0,
    )
    coefs, rounds = gather_all(packed)
    decay, c_in, c_out = (coefs[i * states : (i + 1) * states] for i in range(3))
    carried = lax.dynamic_slice_in_dim(coefs, (3 + window) * states, states, 0)
    skip = coefs[(3 + windows) * states :]
    gate = c_in * c_out
    fade = jnp.exp(-decay)

    def faded(steps):
        return jnp.exp(-decay * steps)

    inner = out_own.shape[0]
    sent = lax.dynamic_slice_in_dim(out_own, core * (inner // 2), inner // 2, 0)
    across = swap_bit(after(sent, rounds[1]), "mp", 0)
    beside = swap_bit(across, "seq", 0)
    out_far = jnp.where(
        core == 0, jnp.concatenate([across, beside], 0), jnp.concatenate([beside, across], 0)
    )

    unit1, rate1 = norm_parts(tokens)
    normed = after(unit1 * norm1_gain + norm1_bias)
    tail = shift_in_window(normed[rows - CTX :], 1, per_window)
    query = mm(normed, qkv[0])
    key = mm(normed, qkv[1])
    value = mm(normed, qkv[2])
    acc, top, total = by_heads(
        self_kernel,
        [(after(query, rounds[1]), rows, 0), (key, rows, 0), (value, rows, 0)],
        [(rows,)] * 3,
    )

    length = float(rows)
    chips = per_window // 2
    chip = block // 2
    (sum_h,) = by_channels(
        summary_kernel,
        [tail, after(normed, acc), decay],
        [states],
    )

    def pair_order(value):
        other = swap_bit(value, "seq", 0)
        return jnp.where(core == 0, value, other), jnp.where(core == 0, other, value)

    first_h, second_h = pair_order(sum_h)
    both_h = faded(length) * first_h + second_h
    far_h = [trade_chips(both_h, d) for d in range(1, chips)]
    (near,) = by_channels(
        near_kernel, [after(tail, sum_h), fade, gate, skip], [CTX]
    )
    far_h = [after(h, near) for h in far_h]
    past_h = jnp.zeros_like(sum_h)
    for d in range(1, chips):
        there = chip ^ d
        gap = jnp.maximum(chip - 1 - there, 0).astype(jnp.float32) * (2.0 * length)
        past_h = past_h + jnp.where(there < chip, faded(gap) * far_h[d - 1], 0.0)
    chip_h = past_h
    past_h = jnp.where(core == 0, past_h, faded(length) * past_h + first_h)

    start_t = jnp.maximum(block * rows - CTX, 0).astype(jnp.float32)
    first = c_out * (c_in * past_h + carried * faded(start_t))

    (context,) = by_channels(
        carry_kernel, [near, first, decay], [CTX]
    )
    key_ctx = mm(context, qkv[1])
    value_ctx = mm(context, qkv[2])
    heads, logs, far = [], [], []
    for part in range(2):
        o, l = by_heads(
            ctx_kernel,
            [(query, half, part), (key_ctx, CTX, 0), (after(value_ctx, *heads), CTX, 0)]
            + [(a, half, part) for a in (acc, top, total)],
            [(half,)] * 2,
            scalars=(ok,),
        )
        heads.append(o)
        logs.append(l)
        far.append(swap_bit(o, "mp", 0))
    grad_hidden = mm(after(cotangent, *heads), down, NT)
    seen = jnp.concatenate([after(context, *heads), normed], 0)
    outs = jnp.concatenate(heads, 0)
    log = jnp.concatenate(logs, 0)

    hidden, grad_pre = unset((rows, up.shape[1])), unset((rows, up.shape[1]))
    normed2 = unset((rows, width))
    mixed, part2 = [], []
    for part in range(2):
        span = slice(part * half, (part + 1) * half)
        came = after(far[part], part2[0]) if part else after(far[0], seen, outs, log, grad_hidden)
        m = tokens[span] + (mm(heads[part], out_own) + mm(came, out_far))
        n = norm_parts(m)[0] * norm2_gain + norm2_bias
        pre = mm(n, up) + up_bias
        cdf = 0.5 + 0.5 * lax.erf(pre * (0.5**0.5))
        bell = jnp.exp(-0.5 * pre * pre) * (1.0 / math.sqrt(2.0 * math.pi))
        hidden = lax.dynamic_update_slice(hidden, pre * cdf, (part * half, 0))
        slope = grad_hidden[span] * (cdf + pre * bell)
        grad_pre = lax.dynamic_update_slice(grad_pre, slope, (part * half, 0))
        normed2 = lax.dynamic_update_slice(normed2, n, (part * half, 0))
        mixed.append(m)
        if part == 0:
            part2.append(mm(grad_pre[span], up, NT))

    clock = Clock()
    give = mm(core_half(after(hidden, part2[0]), 1 - core), cotangent, TN)
    keep = mm(core_half(after(hidden, give), core), cotangent, TN)
    down_ring = Ring([[keep, swap_bit(give, "seq", 0)]], (1,))
    clock.set(down_ring.held)
    part2.append(mm(clock.hold(grad_pre)[half:], up, NT))
    clock.set(part2[1])
    gots2 = [swap_bit(p, "mp", 0) for p in part2]
    down_ring.turn(clock)
    give = mm(core_half(clock.hold(normed2), 1 - core), grad_pre, TN)
    clock.set(give)
    down_ring.turn(clock)
    keep = mm(core_half(clock.hold(normed2), core), grad_pre, TN) + swap_bit(give, "seq", 0)
    up_ring = Ring([[keep]], (1,))
    clock.set(up_ring.held)
    hops = down_ring.count - 1
    down_ring.turn(clock)
    (sum_p,) = by_channels(moment_kernel, [tail, clock.hold(normed), decay], [states])
    clock.set(sum_p)
    up_ring.turn(clock)
    down_ring.turn(clock)

    grad2 = jnp.concatenate([p + clock.hold(g) for p, g in zip(part2, gots2)], 0)
    mixed = jnp.concatenate(mixed, 0)
    unit2, rate2 = norm_parts(after(mixed, grad2))
    gain2 = jnp.sum(grad2 * unit2, axis=0)
    bias2 = jnp.sum(grad2, axis=0)
    grad_mixed = cotangent + norm_back(grad2, unit2, rate2, norm2_gain)
    clock.set(grad_mixed, gain2, bias2)
    up_ring.turn(clock)
    down_ring.turn(clock)
    grad_heads = mm(clock.hold(grad_mixed), out_own, NT)
    clock.set(grad_heads)

    (grads,) = by_heads(
        back_kernel,
        [(query, rows, 0), (key, rows, 0), (value, rows, 0), (key_ctx, CTX, 0), (value_ctx, CTX, 0)]
        + [(a, rows, 0) for a in (outs, log, clock.hold(grad_heads))],
        [(3, CTX + rows)],
        scalars=(ok,),
    )
    clock.set(grads)
    up_ring.turn(clock)
    down_ring.turn(clock)
    gives = [mm(core_half(clock.hold(seen), 1 - core), grads[i], TN) for i in range(3)]
    gives.append(mm(core_half(clock.hold(grad_mixed), 1 - core), outs, TN))
    gots = [swap_bit(g, "seq", 0) for g in gives]
    clock.set(*gives)
    up_ring.turn(clock)
    down_ring.turn(clock)
    feed = mm(clock.hold(hidden), down)
    clock.set(feed)
    feed = lax.psum(feed, "mp")
    up_ring.turn(clock)
    down_ring.turn(clock)
    keeps = [mm(core_half(clock.hold(seen), core), grads[i], TN) + gots[i] for i in range(3)]
    keeps.append(mm(core_half(clock.hold(grad_mixed), core), outs, TN) + gots[3])
    attn_ring = Ring([[k] for k in keeps], (3, 1))
    clock.set(attn_ring.held)
    while up_ring.step < hops:
        up_ring.turn(clock)
        if down_ring.step < hops + 2:
            down_ring.turn(clock)

    left_down, left_up = 2 * hops - down_ring.step, 2 * hops - up_ring.step
    queue = [up_ring] * (left_up - left_down) + [down_ring, up_ring] * left_down

    def next_turn():
        if attn_ring.step < attn_ring.count * 2 - 2:
            attn_ring.turn(clock)
        if queue:
            queue.pop(0).turn(clock)

    held = clock.hold(grads)
    grad_seen = sum(mm(held[i], qkv[i], NT) for i in range(3))
    grad_context = jnp.where(has_ctx, grad_seen[:CTX], 0.0)
    clock.set(grad_seen)
    next_turn()

    sum_q, sum_r, part_h, part_p, part_skip, grad_tail = by_channels(
        tail_back_kernel,
        [tail, clock.hold(grad_context), fade, gate, skip],
        [states, states, states, states, 1, CTX],
    )
    clock.set(sum_q)
    next_turn()
    other = swap_bit(jnp.concatenate([sum_p, sum_q], 0), "seq", 0)
    other_p, other_q = other[:states], other[states:]
    first_p, second_p = jnp.where(core == 0, sum_p, other_p), jnp.where(core == 0, other_p, sum_p)
    first_q, second_q = jnp.where(core == 0, sum_q, other_q), jnp.where(core == 0, other_q, sum_q)
    both_p = faded(length) * (first_p + length * first_h) + second_p
    both_q = first_q + faded(length) * second_q
    both = jnp.concatenate([both_p, both_q], 0)
    clock.set(both)
    past_p = jnp.zeros_like(sum_p)
    later = jnp.zeros_like(sum_q)
    came = [trade_chips(both, d) for d in range(1, chips)]
    next_turn()
    for d in range(1, chips):
        there = chip ^ d
        gap = (jnp.maximum(jnp.abs(chip - there) - 1, 0)).astype(jnp.float32) * (2.0 * length)
        near_p, near_q = came[d - 1][:states], came[d - 1][states:]
        fading = faded(gap)
        past_p = past_p + jnp.where(there < chip, fading * (near_p + gap * far_h[d - 1]), 0.0)
        later = later + jnp.where(there > chip, fading * near_q, 0.0)
    past_p = jnp.where(core == 0, past_p, faded(length) * (past_p + length * chip_h) + first_p)
    later = jnp.where(core == 1, later, second_q + faded(length) * later)
    far_tail, grad_rows = by_channels(
        spread_kernel,
        [clock.hold(gate * later), decay],
        [CTX, rows - CTX],
    )
    to_last = far_tail + grad_tail
    clock.set(to_last)
    from_next = shift_in_window(to_last, -1, per_window)
    next_turn()
    along_h = fade * past_h * sum_q + part_h
    along_p = fade * (past_h * (sum_r + sum_q) + past_p * sum_q) + part_p
    gone = faded(start_t + 1.0)
    part_in = c_out * along_h
    part_out = c_in * along_h + carried * gone * sum_q
    part_decay = -gate * along_p - c_out * carried * gone * ((start_t + 1.0) * sum_q + sum_r)
    stacked = jnp.concatenate([part_in, part_out, part_decay, part_skip], 0)
    clock.set(stacked)
    grad_normed = grad_seen[CTX:] + jnp.concatenate([grad_rows, clock.hold(from_next)], 0)
    result = mixed + clock.hold(feed) + down_bias
    grad_normed = after(grad_normed, result)
    clock.set(grad_normed)
    grad_normed = lax.psum(grad_normed, "mp")
    next_turn()
    far_stacked = swap_bit(stacked, "mp", 0)
    grad_up_bias = jnp.sum(clock.hold(grad_pre), axis=0)
    clock.set(grad_up_bias)
    next_turn()
    grad_down_bias = jnp.sum(clock.hold(cotangent), axis=0)
    ups = grad_up_bias.reshape(-1, width)
    small = jnp.concatenate(
        [stacked + clock.hold(far_stacked), jnp.stack([gain2, bias2, grad_down_bias]), ups], 0
    )
    clock.set(small)
    for bit in range(bits_of(lax.axis_size("seq"))):
        other = swap_bit(small, "seq", bit)
        next_turn()
        small = small + clock.hold(other)
        clock.set(small)
    while attn_ring.step < attn_ring.count * 2 - 2 - LATE:
        next_turn()
    last = clock.hold(grad_normed)
    grad_gain1 = jnp.sum(last * unit1, axis=0)
    grad_bias1 = jnp.sum(last, axis=0)
    grad_tokens = grad_mixed + norm_back(last, unit1, rate1, norm1_gain)
    late = jnp.stack([grad_gain1, grad_bias1])
    clock.set(grad_tokens, late)
    for bit in range(bits_of(lax.axis_size("seq"))):
        other = swap_bit(late, "seq", bit)
        next_turn()
        late = late + clock.hold(other)
        clock.set(late)
    while attn_ring.step < attn_ring.count * 2 - 2:
        next_turn()
    grad_down = down_ring.results()[0][0]
    grad_up = up_ring.results()[0][0]
    grad_qkv, grad_out = attn_ring.results()
    grad_out = jnp.transpose(grad_out[0])

    channels = in_coef.shape[0]
    at = (place_seq * lax.axis_size("mp") + lax.axis_index("mp")) * channels
    own = jnp.transpose(lax.dynamic_slice_in_dim(small[: 3 * states + 1], at, channels, 1))
    grad_in = own[:, :states]
    grad_out_coef = own[:, states : 2 * states]
    grad_decay = own[:, 2 * states : 3 * states]
    grad_skip = own[:, 3 * states]
    small = small[3 * states + 1 :]
    return (
        result,
        grad_tokens,
        late[0],
        late[1],
        grad_in,
        grad_out_coef,
        grad_decay,
        grad_skip,
        grad_qkv,
        grad_out,
        small[0],
        small[1],
        grad_up,
        small[3:].reshape(-1),
        grad_down,
        small[2],
    )


def solution(mesh):
    owner = P(("seq", "mp"), None)
    return jax.shard_map(
        per_device,
        mesh=mesh,
        in_specs=(
            P("seq", None),
            P(None, ("seq", "mp"), None),
            P(),
            P(),
            owner,
            owner,
            owner,
            P(("seq", "mp")),
            P(None, None, "mp"),
            P("mp", None),
            P(),
            P(),
            P(None, "mp"),
            P("mp"),
            P("mp", None),
            P(),
            P("seq", None),
        ),
        out_specs=(
            P("seq", None),
            P("seq", None),
            P(),
            P(),
            owner,
            owner,
            owner,
            P(("seq", "mp")),
            P(None, None, "mp"),
            P("mp", None),
            P(),
            P(),
            P(None, "mp"),
            P("mp"),
            P("mp", None),
            P(),
        ),
        check_vma=False,
    )
```

time: 628 us -> 558 us (0.89)
  starting transfers between devices: 133 us -> 86 us
  local copies, waits for them, and re-layouts: 64.3 us -> 26.1 us
  other arithmetic: 47.6 us -> 75.5 us
  matrix products: 116 us -> 90.1 us
  between operations: 5.47 us -> 17.9 us
    ppermute x58 -> x44, starting transfers between devices: 89.8 us -> 41.2 us  [the longest x42 36.7 us: turn(): got = clock.hold(lax.ppermute(self.held, 'seq', self.route))]
    dynamic_update_slice x80 -> x0, local copies, waits for them, and re-layouts: 29.2 us -> none  [the longest x62 14 us: put(): new.append(lax.dynamic_update_slice(out, cut, (row, 0)))]
    add x40 -> x38, other arithmetic: 15.8 us -> 43.2 us  [the longest x21 30.8 us: turn(): got + self.chunk((self.place + 2 * self.count - self.step) % self.count)]
    dot_general x41 -> x31, matrix products: 116 us -> 90.1 us  [mm(): lax.dot_general(left, right, (dims, ((), ())), precision=HIGH, preferred_...]
    ppermute x67 -> x52, waiting for transfers between devices: 83.8 us -> 62.8 us  [swap_bit(): return lax.ppermute(value, axis, [(i, i ^ 1 << bit) for i in range(size)])]
    pallas_call x0 -> x3, Pallas kernels: none -> 20.6 us  [results(): pl.pallas_call(functools.partial(assemble_kernel, count, cuts), in_specs=...]
    psum x0 -> x2, waiting for transfers between devices: none -> 19.3 us  [the longest x1 19.3 us: per_device(): feed = lax.psum(feed, 'mp')]
    pallas_call x6, Pallas kernels: 47 us -> 32.3 us  [by_channels(): pl.pallas_call(kernel, grid=(width // cut,), in_specs=[spec(a.shape[0]) f...]
  transfers between devices with their start and end apart: 134 -> 104, of which waited for: 62 -> 37; matrix products, arithmetic and copies ran while one was open for 30% -> 27% of each run, Pallas kernels for 12% -> 12%
where the time goes in v3:
time: 558 us; the launch traced here: 549 us
  waiting for transfers between devices  177 us (32%)
  matrix products  90.1 us (16%)
  starting transfers between devices  86 us (15%)
  Pallas kernels  76.8 us (14%)
  other arithmetic  75.5 us (14%)
  local copies, waits for them, and re-layouts  26.1 us (5%)
  between operations  17.9 us (3%)
    dot_general x31, matrix products, mm(): lax.dot_general(left, right, (dims, ((), ())), precision=HIGH, preferred_...  90.1 us
    ppermute x42, waiting for transfers between devices, turn(): got = clock.hold(lax.ppermute(self.held, 'seq', self.route))  80.1 us
    ppermute x52, waiting for transfers between devices, swap_bit(): return lax.ppermute(value, axis, [(i, i ^ 1 << bit) for i in range(size)])  62.8 us
    ppermute x52, starting transfers between devices, swap_bit(): return lax.ppermute(value, axis, [(i, i ^ 1 << bit) for i in range(size)])  39.3 us
    ppermute x42, starting transfers between devices, turn(): got = clock.hold(lax.ppermute(self.held, 'seq', self.route))  36.7 us
    pallas_call x6, Pallas kernels, by_channels(): pl.pallas_call(kernel, grid=(width // cut,), in_specs=[spec(a.shape[0]) f...  32.3 us
    add x21, other arithmetic, turn(): got + self.chunk((self.place + 2 * self.count - self.step) % self.count)  30.8 us
    pallas_call x4, Pallas kernels, by_heads(): pl.pallas_call(kernel, grid=(heads,), in_specs=specs, out_specs=[pl.Block...  23.9 us
  transfers between devices with their start and end apart: 104, of which 37 were waited for; matrix products, arithmetic and copies ran while one was open for 27% of the time, Pallas kernels for 12%

profile of v3, /device:TPU:0, one launch (start us, length us, event | category | flops | bytes accessed | tf_op | source)
XLA Modules:
  0.0 549.1 jit_solution(6894296511607250264)
XLA Ops:
  27.5 6.9 %collective-permute-start.4 = (f32[81,256]{1,0:T(8,128)S(1)}, f32[81,256]{1,0:T(8,128)S(1)}, u32[]{:S(2)}, u32[]{:S(2)}) collective-permute-start(f32[81,256]{1,0:T(8,128)S(1)} %maximum_select_fusion.5), channel_id=1, source_target_pairs={{0,8},{2,10},{4,12},{6,14},{8,0},{10,2},{12,4},{14,6},{16,24},{18,... | collective-permute-start | bytes 248840 | tf_op jit(solution)/shard_map/ppermute | solution.py:40
  43.3 6.1 %shard_map.315 = (f32[512,512]{1,0:T(8,128)S(1)}, f32[512,512]{1,0:T(8,128)S(1)}, f32[512,512]{1,0:T(8,128)S(1)}) custom-call(f32[512,512]{1,0:T(8,128)S(1)} %fusion.47.q_ref, f32[512,512]{1,0:T(8,128)S(1)} %fusion.44.k_ref, f32[512,512]{1,0:T(8,128)S(1)} %fusion.39.v_ref), custom_call_target="tpu_custom_call" | custom-call | bytes 1024 | tf_op jit(solution)/shard_map/pallas_call | solution.py:475
  53.1 5.0 shard_map.316
  68.9 4.5 shard_map.317.near_ref
  95.3 4.6 fusion.115
  99.9 4.5 collective-permute-done.10
  120.3 5.1 fusion.15
  130.0 5.3 fusion.13
  148.4 5.1 fusion.53
  166.0 7.0 %convolution_add_fusion = f32[512,2048]{1,0:T(8,128)S(1)} fusion(f32[512,2048]{1,0:T(8,128)} %collective-permute-done.18, f32[512,2048]{1,0:T(8,128)} %copy-done.20, f32[512,1024]{1,0:T(8,128)S(1)} %copy-done.52, s32[]{:T(128)S(6)} %select_n.516), kind=kOutput, calls=%fused_computation | convolution fusion | flops 3222274048 | bytes 13631492 | tf_op jit(solution)/shard_map/dot_general | solution.py:20
  178.9 7.7 %shard_map.324 = f32[16,1024]{1,0:T(8,128)} custom-call(f32[128,1024]{1,0:T(8,128)} %collective-permute-done.tail_ref.x_ref, f32[512,1024]{1,0:T(8,128)} %copy-done.14, f32[16,1024]{1,0:T(8,128)} %slice.183.decay_ref), custom_call_target="tpu_custom_call" | custom-call | bytes 1024 | tf_op jit(solution)/shard_map/pallas_call | solution.py:374
  192.0 9.8 %collective-permute-done.24 = f32[256,1024]{1,0:T(8,128)} collective-permute-done((f32[256,1024]{1,0:T(8,128)}, f32[256,1024]{1,0:T(8,128)}, u32[]{:S(2)}, u32[]{:S(2)}) %collective-permute-start.24) | collective-permute-done | bytes 1048608 | tf_op jit(solution)/shard_map/ppermute | solution.py:40
  213.3 11.4 %shard_map.325 = f32[3,640,512]{2,1,0:T(8,128)S(1)} custom-call(s32[1]{0:T(128)} %bitcast.ok_ref, f32[512,512]{1,0:T(8,128)S(1)} %fusion.47.q_ref, f32[512,512]{1,0:T(8,128)S(1)} %copy-done.3, f32[512,512]{1,0:T(8,128)S(1)} %fusion.39.v_ref, f32[128,512]{1,0:T(8,128)S(1)} %copy-done.11, f32[128,512]{1,0:T(8,128)S(1)} %fusion.37.v_ref.vc_ref, ...), custom_call_target="tpu_custom_call" | custom-call | bytes 1024 | tf_op jit(solution)/shard_map/pallas_call | solution.py:475
  250.2 5.9 %fusion.118 = f32[512,1024]{1,0:T(8,128)} fusion(f32[512,2048]{1,0:T(8,128)S(1)} %copy-done.43, bf16[2048,1024]{1,0:T(8,128)(2,1)S(1)} %copy-done.115), kind=kOutput, calls=%fused_computation.287 | convolution fusion | flops 6442450944 | bytes 10485760 | tf_op jit(solution)/shard_map/dot_general | solution.py:20
  278.1 6.8 %collective-permute-done.36 = f32[1,64,2048]{2,1,0:T(8,128)S(1)} collective-permute-done((f32[1,64,2048]{2,1,0:T(8,128)S(1)}, f32[1,64,2048]{2,1,0:T(8,128)S(1)}, u32[]{:S(2)}, u32[]{:S(2)}) %collective-permute-start.36) | collective-permute-done | bytes 524320 | tf_op jit(solution)/shard_map/ppermute | solution.py:164
  298.7 7.7 %shard_map.326 = (f32[16,1024]{1,0:T(8,128)}, f32[16,1024]{1,0:T(8,128)}, f32[16,1024]{1,0:T(8,128)}, f32[16,1024]{1,0:T(8,128)}, f32[1,1024]{1,0:T(1,128)}, /*index=5*/f32[128,1024]{1,0:T(8,128)}) custom-call(f32[128,1024]{1,0:T(8,128)} %collective-permute-done.tail_ref.x_ref, f32[128,1024]{1,0:T(8,128)} %slice_select_fusion.d_ref, ...), custom_call_target="tpu_custom_call" | custom-call | bytes 1024 | tf_op jit(solution)/shard_map/pallas_call | solution.py:374
  320.1 12.4 %collective-permute-done.41 = f32[32,1024]{1,0:T(8,128)S(1)} collective-permute-done((f32[32,1024]{1,0:T(8,128)S(1)}, f32[32,1024]{1,0:T(8,128)S(1)}, u32[]{:S(2)}, u32[]{:S(2)}) %collective-permute-start.41) | collective-permute-done | bytes 131104 | tf_op jit(solution)/shard_map/ppermute | solution.py:77
  338.0 19.3 %all-reduce.3.cloned.1.call-done = f32[512,1024]{1,0:T(8,128)} async-done(((f32[512,1024]{1,0:T(8,128)}), f32[512,1024]{1,0:T(8,128)}) %all-reduce.3.cloned.1.call-update) | async-done | bytes 2097168 | tf_op jit(solution)/shard_map/psum | solution.py:684
  357.3 4.9 shard_map.327
  382.6 8.4 %collective-permute-done.50.refs_3_ = f32[1,64,2048]{2,1,0:T(8,128)} collective-permute-done((f32[1,64,2048]{2,1,0:T(8,128)}, f32[1,64,2048]{2,1,0:T(8,128)}, u32[]{:S(2)}, u32[]{:S(2)}) %collective-permute-start.50) | collective-permute-done | bytes 524320 | tf_op jit(solution)/shard_map/ppermute | solution.py:164
  413.7 5.7 %collective-permute-done.61.refs_1_ = f32[4,64,512]{2,1,0:T(8,128)S(1)} collective-permute-done((f32[4,64,512]{2,1,0:T(8,128)S(1)}, f32[4,64,512]{2,1,0:T(8,128)S(1)}, u32[]{:S(2)}, u32[]{:S(2)}) %collective-permute-start.61) | collective-permute-done | bytes 524320 | tf_op jit(solution)/shard_map/ppermute | solution.py:164
  426.1 9.5 %collective-permute-done.59 = f32[54,1024]{1,0:T(8,128)S(1)} collective-permute-done((f32[54,1024]{1,0:T(8,128)S(1)}, f32[54,1024]{1,0:T(8,128)S(1)}, u32[]{:S(2)}, u32[]{:S(2)}) %collective-permute-start.59) | collective-permute-done | bytes 221216 | tf_op jit(solution)/shard_map/ppermute | solution.py:40
  435.8 5.5 collective-permute-done.63.refs_6_
  441.3 11.6 %collective-permute-done.62 = f32[54,1024]{1,0:T(8,128)S(1)} collective-permute-done((f32[54,1024]{1,0:T(8,128)S(1)}, f32[54,1024]{1,0:T(8,128)S(1)}, u32[]{:S(2)}, u32[]{:S(2)}) %collective-permute-start.62) | collective-permute-done | bytes 221216 | tf_op jit(solution)/shard_map/ppermute | solution.py:40
  456.9 9.6 %collective-permute-done.65 = f32[54,1024]{1,0:T(8,128)S(1)} collective-permute-done((f32[54,1024]{1,0:T(8,128)S(1)}, f32[54,1024]{1,0:T(8,128)S(1)}, u32[]{:S(2)}, u32[]{:S(2)}) %collective-permute-start.65) | collective-permute-done | bytes 221216 | tf_op jit(solution)/shard_map/ppermute | solution.py:40
  471.7 4.6 collective-permute-done.70.refs_4_
  480.2 6.0 %collective-permute-done.73.refs_5_ = f32[4,64,512]{2,1,0:T(8,128)S(1)} collective-permute-done((f32[4,64,512]{2,1,0:T(8,128)}, f32[4,64,512]{2,1,0:T(8,128)S(1)}, u32[]{:S(2)}, u32[]{:S(2)}) %collective-permute-start.73) | collective-permute-done | bytes 524320 | tf_op jit(solution)/shard_map/ppermute | solution.py:164
  491.1 4.8 collective-permute-done.72.refs_7_
  495.9 5.6 %collective-permute-done.71 = f32[2,1024]{1,0:T(2,128)S(1)} collective-permute-done((f32[2,1024]{1,0:T(2,128)S(1)}, f32[2,1024]{1,0:T(2,128)S(1)}, u32[]{:S(2)}, u32[]{:S(2)}) %collective-permute-start.71) | collective-permute-done | bytes 8224 | tf_op jit(solution)/shard_map/ppermute | solution.py:40
  517.6 6.8 %shard_map.330 = f32[1,2,8,128,1024]{4,3,2,1,0:T(8,128)} custom-call(s32[2,16]{1,0:T(2,128)} %pad_add_fusion.where_ref, f32[1,128,1024]{2,1,0:T(8,128)} %copy-done.55, f32[1,128,1024]{2,1,0:T(8,128)} %copy-done.69, f32[1,128,1024]{2,1,0:T(8,128)} %copy-done.70, f32[1,128,1024]{2,1,0:T(8,128)} %collective-permute-done.44.refs_3_, ...), custom_call_target="tpu_custom_call" | custom-call | bytes 16777216 | tf_op jit(solution)/shard_map/pallas_call | solution.py:185
  524.5 6.8 %shard_map.329 = f32[1,2,8,64,2048]{4,3,2,1,0:T(8,128)} custom-call(s32[2,16]{1,0:T(2,128)} %pad_add_fusion.where_ref, f32[1,64,2048]{2,1,0:T(8,128)} %copy-done.58, f32[1,64,2048]{2,1,0:T(8,128)} %collective-permute-done.38.refs_1_, f32[1,64,2048]{2,1,0:T(8,128)} %collective-permute-done.49.refs_2_, f32[1,64,2048]{2,1,0:T(8,128)} %collective-permute-done.50.refs_3_, ...), custom_call_target="tpu_custom_call" | custom-call | bytes 16777216 | tf_op jit(solution)/shard_map/pallas_call | solution.py:185
  532.0 6.9 %shard_map.328 = (f32[3,2,8,64,512]{4,3,2,1,0:T(8,128)}, f32[1,2,8,64,512]{4,3,2,1,0:T(8,128)}) custom-call(s32[2,16]{1,0:T(2,128)} %pad_add_fusion.where_ref, f32[4,64,512]{2,1,0:T(8,128)} %copy-done.57, f32[4,64,512]{2,1,0:T(8,128)} %copy-done.72, f32[4,64,512]{2,1,0:T(8,128)} %copy-done.73, f32[4,64,512]{2,1,0:T(8,128)} %collective-permute-done.67.refs_3_, ...), custom_call_target="tpu_custom_call" | custom-call | bytes 16777216 | tf_op jit(solution)/shard_map/pallas_call | solution.py:185
  (579 shorter events, 299.6 us)
Async XLA Ops:
  7.2 350.1 %all-reduce.3.cloned.1.call-start = ((), (), s32[]{:S(2)}) async-start(), calls=%async_computation | async-start | bytes 4194304 | tf_op jit(solution)/shard_map/psum | solution.py:684
  19.8 33.3 %collective-permute-start = (f32[128,1024]{1,0:T(8,128)}, f32[128,1024]{1,0:T(8,128)}, u32[]{:S(2)}, u32[]{:S(2)}) collective-permute-start(f32[128,1024]{1,0:T(8,128)} %slice.182), channel_id=1, source_target_pairs={{0,2},{2,4},{4,6},{6,8},{8,10},{10,12},{12,14},{16,18},{18,20},{20... | collective-permute-start | bytes 1572872 | tf_op jit(solution)/shard_map/ppermute | solution.py:51
  66.8 26.4 %collective-permute-start.11 = (f32[256,1024]{1,0:T(8,128)}, f32[256,1024]{1,0:T(8,128)}, u32[]{:S(2)}, u32[]{:S(2)}) collective-permute-start(f32[256,1024]{1,0:T(8,128)} %dynamic-slice_convert_fusion), channel_id=1, source_target_pairs={{0,1},{1,0},{2,3},{3,2},{4,5},{5,4},{6,7},{7,6},{8,9},{9,8},{10,11... | collective-permute-start | bytes 3145736 | tf_op jit(solution)/shard_map/ppermute | solution.py:40
  83.7 20.7 %collective-permute-start.10 = (f32[256,512]{1,0:T(8,128)S(1)}, f32[256,512]{1,0:T(8,128)S(1)}, u32[]{:S(2)}, u32[]{:S(2)}) collective-permute-start(f32[256,512]{1,0:T(8,128)S(1)} %get-tuple-element.129), channel_id=1, source_target_pairs={{0,1},{1,0},{2,3},{3,2},{4,5},{5,4},{6,7},{7,6},{8,9},{9,8},{10,11... | collective-permute-start | bytes 1572872 | tf_op jit(solution)/shard_map/ppermute | solution.py:40
  87.7 26.6 %collective-permute-start.13 = (f32[256,512]{1,0:T(8,128)S(1)}, f32[256,512]{1,0:T(8,128)S(1)}, u32[]{:S(2)}, u32[]{:S(2)}) collective-permute-start(f32[256,512]{1,0:T(8,128)S(1)} %get-tuple-element.131), channel_id=1, source_target_pairs={{0,1},{1,0},{2,3},{3,2},{4,5},{5,4},{6,7},{7,6},{8,9},{9,8},{10,11... | collective-permute-start | bytes 1572872 | tf_op jit(solution)/shard_map/ppermute | solution.py:40
  154.9 35.6 %collective-permute-start.23 = (f32[256,1024]{1,0:T(8,128)}, f32[256,1024]{1,0:T(8,128)}, u32[]{:S(2)}, u32[]{:S(2)}) collective-permute-start(f32[256,1024]{1,0:T(8,128)} %fusion.105), channel_id=1, source_target_pairs={{0,1},{1,0},{2,3},{3,2},{4,5},{5,4},{6,7},{7,6},{8,9},{9,8},{10,11... | collective-permute-start | bytes 3145736 | tf_op jit(solution)/shard_map/ppermute | solution.py:40
  174.3 27.5 %collective-permute-start.24 = (f32[256,1024]{1,0:T(8,128)}, f32[256,1024]{1,0:T(8,128)}, u32[]{:S(2)}, u32[]{:S(2)}) collective-permute-start(f32[256,1024]{1,0:T(8,128)} %fusion.11), channel_id=1, source_target_pairs={{0,1},{1,0},{2,3},{3,2},{4,5},{5,4},{6,7},{7,6},{8,9},{9,8},{10,11... | collective-permute-start | bytes 3145736 | tf_op jit(solution)/shard_map/ppermute | solution.py:40
  187.9 18.0 %collective-permute-start.22 = (f32[1,64,2048]{2,1,0:T(8,128)S(1)}, f32[1,64,2048]{2,1,0:T(8,128)S(1)}, u32[]{:S(2)}, u32[]{:S(2)}) collective-permute-start(f32[1,64,2048]{2,1,0:T(8,128)S(1)} %dynamic-slice_add_fusion.6), channel_id=1, source_target_pairs={{0,8},{10,2},{8,16},{18,10},{16,24},{26,18},{24,28},{30,26},{28,20... | collective-permute-start | bytes 1572872 | tf_op jit(solution)/shard_map/ppermute | solution.py:164
  190.5 18.9 %collective-permute-start.21 = (f32[1,128,1024]{2,1,0:T(8,128)S(1)}, f32[1,128,1024]{2,1,0:T(8,128)S(1)}, u32[]{:S(2)}, u32[]{:S(2)}) collective-permute-start(f32[1,128,1024]{2,1,0:T(8,128)S(1)} %add_add_fusion.5), channel_id=1, source_target_pairs={{0,8},{10,2},{8,16},{18,10},{16,24},{26,18},{24,28},{30,26},{28,20... | collective-permute-start | bytes 1572872 | tf_op jit(solution)/shard_map/ppermute | solution.py:164
  207.6 17.2 %collective-permute-start.26 = (f32[1,64,2048]{2,1,0:T(8,128)S(1)}, f32[1,64,2048]{2,1,0:T(8,128)S(1)}, u32[]{:S(2)}, u32[]{:S(2)}) collective-permute-start(f32[1,64,2048]{2,1,0:T(8,128)S(1)} %dynamic-slice_add_fusion.5), channel_id=1, source_target_pairs={{0,8},{10,2},{8,16},{18,10},{16,24},{26,18},{24,28},{30,26},{28,20... | collective-permute-start | bytes 1572872 | tf_op jit(solution)/shard_map/ppermute | solution.py:164
  239.0 21.1 %collective-permute-start.32 = (f32[512,512]{1,0:T(8,128)}, f32[512,512]{1,0:T(8,128)}, u32[]{:S(2)}, u32[]{:S(2)}) collective-permute-start(f32[512,512]{1,0:T(8,128)} %fusion.27), channel_id=1, source_target_pairs={{0,2},{2,0},{4,6},{6,4},{8,10},{10,8},{12,14},{14,12},{16,18},{18,... | collective-permute-start | bytes 3145736 | tf_op jit(solution)/shard_map/ppermute | solution.py:40
  239.0 26.2 %collective-permute-start.33 = (f32[512,512]{1,0:T(8,128)}, f32[512,512]{1,0:T(8,128)}, u32[]{:S(2)}, u32[]{:S(2)}) collective-permute-start(f32[512,512]{1,0:T(8,128)} %fusion.28), channel_id=1, source_target_pairs={{0,2},{2,0},{4,6},{6,4},{8,10},{10,8},{12,14},{14,12},{16,18},{18,... | collective-permute-start | bytes 3145736 | tf_op jit(solution)/shard_map/ppermute | solution.py:40
  239.5 29.5 %collective-permute-start.34 = (f32[512,512]{1,0:T(8,128)}, f32[512,512]{1,0:T(8,128)S(1)}, u32[]{:S(2)}, u32[]{:S(2)}) collective-permute-start(f32[512,512]{1,0:T(8,128)} %fusion.29), channel_id=1, source_target_pairs={{0,2},{2,0},{4,6},{6,4},{8,10},{10,8},{12,14},{14,12},{16,18},{18,... | collective-permute-start | bytes 3145736 | tf_op jit(solution)/shard_map/ppermute | solution.py:40
  260.0 18.1 %collective-permute-start.37 = (f32[1,128,1024]{2,1,0:T(8,128)S(1)}, f32[1,128,1024]{2,1,0:T(8,128)S(1)}, u32[]{:S(2)}, u32[]{:S(2)}) collective-permute-start(f32[1,128,1024]{2,1,0:T(8,128)S(1)} %collective-permute-done.31.refs_1_), channel_id=1, source_target_pairs={{0,8},{10,2},{8,16},{18,10},{16,24},{26,18},{24,28},{30,26},{28,20... | collective-permute-start | bytes 1572872 | tf_op jit(solution)/shard_map/ppermute | solution.py:164
  294.5 172.4 %all-reduce.5.cloned.1.call-start = ((), (), s32[]{:S(2)}) async-start(), calls=%async_computation.1 | async-start | bytes 4194304 | tf_op jit(solution)/shard_map/psum | solution.py:760
  309.5 47.8 %collective-permute-start.44 = (f32[1,128,1024]{2,1,0:T(8,128)S(1)}, f32[1,128,1024]{2,1,0:T(8,128)}, u32[]{:S(2)}, u32[]{:S(2)}) collective-permute-start(f32[1,128,1024]{2,1,0:T(8,128)S(1)} %copy-done.71), channel_id=1, source_target_pairs={{0,8},{10,2},{8,16},{18,10},{16,24},{26,18},{24,28},{30,26},{28,20... | collective-permute-start | bytes 1572872 | tf_op jit(solution)/shard_map/ppermute | solution.py:164
  310.9 60.1 %collective-permute-start.49 = (f32[1,64,2048]{2,1,0:T(8,128)}, f32[1,64,2048]{2,1,0:T(8,128)}, u32[]{:S(2)}, u32[]{:S(2)}) collective-permute-start(f32[1,64,2048]{2,1,0:T(8,128)} %collective-permute-done.38.refs_1_), channel_id=1, source_target_pairs={{0,8},{10,2},{8,16},{18,10},{16,24},{26,18},{24,28},{30,26},{28,20... | collective-permute-start | bytes 1572872 | tf_op jit(solution)/shard_map/ppermute | solution.py:164
  313.7 18.8 %collective-permute-start.41 = (f32[32,1024]{1,0:T(8,128)S(1)}, f32[32,1024]{1,0:T(8,128)S(1)}, u32[]{:S(2)}, u32[]{:S(2)}) collective-permute-start(f32[32,1024]{1,0:T(8,128)S(1)} %pad_maximum_fusion.6), channel_id=1, source_target_pairs={{0,4},{2,6},{4,0},{6,2},{8,12},{10,14},{12,8},{14,10},{16,20},{18,... | collective-permute-start | bytes 393224 | tf_op jit(solution)/shard_map/ppermute | solution.py:77
  314.1 18.5 %collective-permute-start.42 = (f32[32,1024]{1,0:T(8,128)S(1)}, f32[32,1024]{1,0:T(8,128)S(1)}, u32[]{:S(2)}, u32[]{:S(2)}) collective-permute-start(f32[32,1024]{1,0:T(8,128)S(1)} %pad_maximum_fusion.6), channel_id=1, source_target_pairs={{0,8},{2,10},{4,12},{6,14},{8,0},{10,2},{12,4},{14,6},{16,24},{18,... | collective-permute-start | bytes 393224 | tf_op jit(solution)/shard_map/ppermute | solution.py:77
  332.5 32.3 %collective-permute-start.51 = (f32[4,64,512]{2,1,0:T(8,128)}, f32[4,64,512]{2,1,0:T(8,128)}, u32[]{:S(2)}, u32[]{:S(2)}) collective-permute-start(f32[4,64,512]{2,1,0:T(8,128)} %maximum_add_fusion.2), channel_id=1, source_target_pairs={{0,8},{10,2},{8,16},{18,10},{16,24},{26,18},{24,28},{30,26},{28,20... | collective-permute-start | bytes 1572872 | tf_op jit(solution)/shard_map/ppermute | solution.py:164
  371.0 20.0 %collective-permute-start.55 = (f32[1,128,1024]{2,1,0:T(8,128)}, f32[1,128,1024]{2,1,0:T(8,128)}, u32[]{:S(2)}, u32[]{:S(2)}) collective-permute-start(f32[1,128,1024]{2,1,0:T(8,128)} %collective-permute-done.44.refs_3_), channel_id=1, source_target_pairs={{0,8},{10,2},{8,16},{18,10},{16,24},{26,18},{24,28},{30,26},{28,20... | collective-permute-start | bytes 1572872 | tf_op jit(solution)/shard_map/ppermute | solution.py:164
  371.1 19.9 %collective-permute-start.50 = (f32[1,64,2048]{2,1,0:T(8,128)}, f32[1,64,2048]{2,1,0:T(8,128)}, u32[]{:S(2)}, u32[]{:S(2)}) collective-permute-start(f32[1,64,2048]{2,1,0:T(8,128)} %collective-permute-done.49.refs_2_), channel_id=1, source_target_pairs={{0,8},{10,2},{8,16},{18,10},{16,24},{26,18},{24,28},{30,26},{28,20... | collective-permute-start | bytes 1572872 | tf_op jit(solution)/shard_map/ppermute | solution.py:164
  421.4 19.8 %collective-permute-start.63 = (f32[1,128,1024]{2,1,0:T(8,128)}, f32[1,128,1024]{2,1,0:T(8,128)}, u32[]{:S(2)}, u32[]{:S(2)}) collective-permute-start(f32[1,128,1024]{2,1,0:T(8,128)} %collective-permute-done.57.refs_5_), channel_id=1, source_target_pairs={{0,8},{10,2},{8,16},{18,10},{16,24},{26,18},{24,28},{30,26},{28,20... | collective-permute-start | bytes 1572872 | tf_op jit(solution)/shard_map/ppermute | solution.py:164
  435.6 20.8 %collective-permute-start.67 = (f32[4,64,512]{2,1,0:T(8,128)S(1)}, f32[4,64,512]{2,1,0:T(8,128)}, u32[]{:S(2)}, u32[]{:S(2)}) collective-permute-start(f32[4,64,512]{2,1,0:T(8,128)S(1)} %collective-permute-done.64.refs_2_), channel_id=1, source_target_pairs={{0,8},{10,2},{8,16},{18,10},{16,24},{26,18},{24,28},{30,26},{28,20... | collective-permute-start | bytes 1572872 | tf_op jit(solution)/shard_map/ppermute | solution.py:164
  435.7 21.3 %collective-permute-start.66 = (f32[1,64,2048]{2,1,0:T(8,128)S(1)}, f32[1,64,2048]{2,1,0:T(8,128)}, u32[]{:S(2)}, u32[]{:S(2)}) collective-permute-start(f32[1,64,2048]{2,1,0:T(8,128)S(1)} %collective-permute-done.60.refs_5_), channel_id=1, source_target_pairs={{0,8},{10,2},{8,16},{18,10},{16,24},{26,18},{24,28},{30,26},{28,20... | collective-permute-start | bytes 1572872 | tf_op jit(solution)/shard_map/ppermute | solution.py:164
  453.0 23.3 %collective-permute-start.94 = (f32[1,128,1024]{2,1,0:T(8,128)S(1)}, f32[1,128,1024]{2,1,0:T(8,128)}, u32[]{:S(2)}, u32[]{:S(2)}) collective-permute-start(f32[1,128,1024]{2,1,0:T(8,128)S(1)} %copy-done.56), channel_id=1, source_target_pairs={{0,2},{2,0},{4,6},{6,4},{8,10},{10,8},{12,14},{14,12},{16,18},{18,... | collective-permute-start | bytes 1572872 | tf_op jit(solution)/shard_map/ppermute | solution.py:40
  456.4 20.4 %collective-permute-start.95 = (f32[1,128,1024]{2,1,0:T(8,128)}, f32[1,128,1024]{2,1,0:T(8,128)}, u32[]{:S(2)}, u32[]{:S(2)}) collective-permute-start(f32[1,128,1024]{2,1,0:T(8,128)} %copy-done.69), channel_id=1, source_target_pairs={{0,2},{2,0},{4,6},{6,4},{8,10},{10,8},{12,14},{14,12},{16,18},{18,... | collective-permute-start | bytes 1572872 | tf_op jit(solution)/shard_map/ppermute | solution.py:40
  456.4 21.9 %collective-permute-start.96 = (f32[1,128,1024]{2,1,0:T(8,128)}, f32[1,128,1024]{2,1,0:T(8,128)}, u32[]{:S(2)}, u32[]{:S(2)}) collective-permute-start(f32[1,128,1024]{2,1,0:T(8,128)} %copy-done.70), channel_id=1, source_target_pairs={{0,2},{2,0},{4,6},{6,4},{8,10},{10,8},{12,14},{14,12},{16,18},{18,... | collective-permute-start | bytes 1572872 | tf_op jit(solution)/shard_map/ppermute | solution.py:40
  456.9 21.4 %collective-permute-start.69 = (f32[1,128,1024]{2,1,0:T(8,128)}, f32[1,128,1024]{2,1,0:T(8,128)}, u32[]{:S(2)}, u32[]{:S(2)}) collective-permute-start(f32[1,128,1024]{2,1,0:T(8,128)} %collective-permute-done.63.refs_6_), channel_id=1, source_target_pairs={{0,8},{10,2},{8,16},{18,10},{16,24},{26,18},{24,28},{30,26},{28,20... | collective-permute-start | bytes 1572872 | tf_op jit(solution)/shard_map/ppermute | solution.py:164
  513.7 18.3 %collective-permute-start.81 = (f32[4,64,512]{2,1,0:T(8,128)}, f32[4,64,512]{2,1,0:T(8,128)}, u32[]{:S(2)}, u32[]{:S(2)}) collective-permute-start(f32[4,64,512]{2,1,0:T(8,128)} %collective-permute-done.67.refs_3_), channel_id=1, source_target_pairs={{0,2},{2,0},{4,6},{6,4},{8,10},{10,8},{12,14},{14,12},{16,18},{18,... | collective-permute-start | bytes 1572872 | tf_op jit(solution)/shard_map/ppermute | solution.py:40
  513.7 18.3 %collective-permute-start.82 = (f32[4,64,512]{2,1,0:T(8,128)}, f32[4,64,512]{2,1,0:T(8,128)}, u32[]{:S(2)}, u32[]{:S(2)}) collective-permute-start(f32[4,64,512]{2,1,0:T(8,128)} %collective-permute-done.70.refs_4_), channel_id=1, source_target_pairs={{0,2},{2,0},{4,6},{6,4},{8,10},{10,8},{12,14},{14,12},{16,18},{18,... | collective-permute-start | bytes 1572872 | tf_op jit(solution)/shard_map/ppermute | solution.py:40
  514.2 17.8 %collective-permute-start.83 = (f32[4,64,512]{2,1,0:T(8,128)S(1)}, f32[4,64,512]{2,1,0:T(8,128)}, u32[]{:S(2)}, u32[]{:S(2)}) collective-permute-start(f32[4,64,512]{2,1,0:T(8,128)S(1)} %collective-permute-done.73.refs_5_), channel_id=1, source_target_pairs={{0,2},{2,0},{4,6},{6,4},{8,10},{10,8},{12,14},{14,12},{16,18},{18,... | collective-permute-start | bytes 1572872 | tf_op jit(solution)/shard_map/ppermute | solution.py:40
  (190 other events, 2241.6 us)
Sparse Core Ops, SparseCore 0:
  294.6 62.6 all-reduce.2
  399.3 63.5 all-reduce.4

commit v4 on v3

--- a/solution.py
+++ b/solution.py
@@ -160,8 +160,9 @@
     def chunk(self, spot):
         return jnp.stack([sum(pick(a, spot) for a in addends) for addends in self.pieces])
 
-    def turn(self, clock):
-        got = clock.hold(lax.ppermute(self.held, "seq", self.route))
+    def turn(self, clock, kept=()):
+        got = lax.ppermute(self.held, "seq", self.route)
+        got, *kept = lax.optimization_barrier((got, *kept, *clock.last))[: 1 + len(kept)]
         self.step += 1
         if self.step < self.count:
             got = got + self.chunk((self.place + 2 * self.count - self.step) % self.count)
@@ -170,6 +171,7 @@
             self.own.append(got)
             self.far.append(swap_bit(got, "seq", 0))
         clock.set(got)
+        return kept
 
     def results(self):
         count = self.count
@@ -189,9 +191,7 @@
             out_specs=[pl.BlockSpec(memory_space=pl.ANY)] * len(shapes),
             out_shape=[jax.ShapeDtypeStruct(shape, jnp.float32) for shape in shapes],
             scratch_shapes=[pltpu.SemaphoreType.DMA((2 * count * len(shapes),))],
-            cost_estimate=pl.CostEstimate(
-                flops=0, bytes_accessed=8 * sum(math.prod(a) for a in shapes), transcendentals=0
-            ),
+            cost_estimate=pl.CostEstimate(flops=0, bytes_accessed=COST, transcendentals=0),
         )(where, *self.own, *self.far)
         return [out.reshape(out.shape[0], -1, self.cols) for out in outs]
 
@@ -397,7 +397,6 @@
 NN = ((1,), (0,))
 TN = ((0,), (0,))
 TILE = 256
-LATE = 4
 COST = 1024
 SCALE = HDIM ** (-0.5)
 
@@ -468,10 +467,13 @@
 
 
 def by_heads(kernel, ins, outs, scalars=()):
-    heads = ins[0][0].shape[1] // HDIM
+    heads = ins[0][0].shape[-1] // HDIM
     specs = [pl.BlockSpec(memory_space=pltpu.SMEM) for _ in scalars]
-    for _, rows, at in ins:
-        specs.append(pl.BlockSpec((rows, HDIM), lambda h, at=at: (at, h)))
+    for _, rows, *at in ins:
+        if len(at) == 2:
+            specs.append(pl.BlockSpec((None, rows, HDIM), lambda h, at=at: (at[1], at[0], h)))
+        else:
+            specs.append(pl.BlockSpec((rows, HDIM), lambda h, at=at: (at[0], h)))
     return pl.pallas_call(
         kernel,
         grid=(heads,),
@@ -482,7 +484,38 @@
         out_shape=[jax.ShapeDtypeStruct(lead + (heads * HDIM,), jnp.float32) for lead in outs],
         cost_estimate=pl.CostEstimate(flops=0, bytes_accessed=COST, transcendentals=0),
         compiler_params=pltpu.CompilerParams(vmem_limit_bytes=40 << 20),
-    )(*scalars, *[a for a, _, _ in ins])
+    )(*scalars, *[a[0] for a in ins])
+
+
+def project_kernel(x_ref, w_ref, out_ref, high_ref, low_ref):
+    @pl.when(pl.program_id(0) == 0)
+    def _():
+        high_ref[...], low_ref[...] = cut(x_ref[...])
+
+    def one(part):
+        return lax.dot_general(
+            part, w_ref[...], (NN, ((), ())), preferred_element_type=jnp.float32
+        )
+
+    out_ref[...] = one(low_ref[...]) + one(high_ref[...])
+
+
+def project(x, weights, first, count):
+    rows, depth = x.shape
+    width = weights.shape[2]
+    return pl.pallas_call(
+        project_kernel,
+        grid=(count,),
+        in_specs=[
+            pl.BlockSpec((rows, depth), lambda i: (0, 0)),
+            pl.BlockSpec((None, depth, width), lambda i: (first + i, 0, 0)),
+        ],
+        out_specs=pl.BlockSpec((None, rows, width), lambda i: (i, 0, 0)),
+        out_shape=jax.ShapeDtypeStruct((count, rows, width), jnp.float32),
+        scratch_shapes=[pltpu.VMEM((rows, depth), jnp.bfloat16)] * 2,
+        cost_estimate=pl.CostEstimate(flops=0, bytes_accessed=COST, transcendentals=0),
+        compiler_params=pltpu.CompilerParams(vmem_limit_bytes=40 << 20),
+    )(x, weights)
 
 
 def per_device(
@@ -548,12 +581,10 @@
     unit1, rate1 = norm_parts(tokens)
     normed = after(unit1 * norm1_gain + norm1_bias)
     tail = shift_in_window(normed[rows - CTX :], 1, per_window)
-    query = mm(normed, qkv[0])
-    key = mm(normed, qkv[1])
-    value = mm(normed, qkv[2])
+    qkv_rows = project(normed, qkv_weight, 0, 3)
     acc, top, total = by_heads(
         self_kernel,
-        [(after(query, rounds[1]), rows, 0), (key, rows, 0), (value, rows, 0)],
+        [(qkv_rows, rows, 0, i) for i in range(3)],
         [(rows,)] * 3,
     )
 
@@ -591,13 +622,12 @@
     (context,) = by_channels(
         carry_kernel, [near, first, decay], [CTX]
     )
-    key_ctx = mm(context, qkv[1])
-    value_ctx = mm(context, qkv[2])
+    kv_ctx = project(context, qkv_weight, 1, 2)
     heads, logs, far = [], [], []
     for part in range(2):
         o, l = by_heads(
             ctx_kernel,
-            [(query, half, part), (key_ctx, CTX, 0), (after(value_ctx, *heads), CTX, 0)]
+            [(qkv_rows, half, part, 0), (after(kv_ctx, *heads), CTX, 0, 0), (kv_ctx, CTX, 0, 1)]
             + [(a, half, part) for a in (acc, top, total)],
             [(half,)] * 2,
             scalars=(ok,),
@@ -637,76 +667,83 @@
     part2.append(mm(clock.hold(grad_pre)[half:], up, NT))
     clock.set(part2[1])
     gots2 = [swap_bit(p, "mp", 0) for p in part2]
-    down_ring.turn(clock)
+    mixed = jnp.concatenate(mixed, 0)
+    grad_mixed, grad_heads = unset((rows, width)), []
+    gain2, bias2 = 0.0, 0.0
+
+    def norm2_half(part, grad_mixed, gain2, bias2):
+        span = slice(part * half, (part + 1) * half)
+        grad2 = part2[part] + after(gots2[part], *clock.last)
+        unit2, rate2 = norm_parts(after(mixed, grad2)[span])
+        gain2 = gain2 + jnp.sum(grad2 * unit2, axis=0)
+        bias2 = bias2 + jnp.sum(grad2, axis=0)
+        new = cotangent[span] + norm_back(grad2, unit2, rate2, norm2_gain)
+        grad_mixed = lax.dynamic_update_slice(grad_mixed, new, (part * half, 0))
+        clock.set(grad_mixed, gain2, bias2)
+        return grad_mixed, gain2, bias2
+
+    hops = down_ring.count - 1
+
+    def turn(*rings, kept=()):
+        rings = [ring for ring in rings if ring.step < 2 * hops]
+        for ring in rings[:-1]:
+            ring.turn(clock)
+        return rings[-1].turn(clock, kept)
+
+    (gots2[0],) = turn(down_ring, kept=(gots2[0],))
+    grad_mixed, gain2, bias2 = norm2_half(0, grad_mixed, gain2, bias2)
     give = mm(core_half(clock.hold(normed2), 1 - core), grad_pre, TN)
     clock.set(give)
-    down_ring.turn(clock)
+    turn(down_ring)
     keep = mm(core_half(clock.hold(normed2), core), grad_pre, TN) + swap_bit(give, "seq", 0)
     up_ring = Ring([[keep]], (1,))
     clock.set(up_ring.held)
-    hops = down_ring.count - 1
-    down_ring.turn(clock)
-    (sum_p,) = by_channels(moment_kernel, [tail, clock.hold(normed), decay], [states])
-    clock.set(sum_p)
-    up_ring.turn(clock)
-    down_ring.turn(clock)
-
-    grad2 = jnp.concatenate([p + clock.hold(g) for p, g in zip(part2, gots2)], 0)
-    mixed = jnp.concatenate(mixed, 0)
-    unit2, rate2 = norm_parts(after(mixed, grad2))
-    gain2 = jnp.sum(grad2 * unit2, axis=0)
-    bias2 = jnp.sum(grad2, axis=0)
-    grad_mixed = cotangent + norm_back(grad2, unit2, rate2, norm2_gain)
-    clock.set(grad_mixed, gain2, bias2)
-    up_ring.turn(clock)
-    down_ring.turn(clock)
+    (gots2[1],) = turn(down_ring, kept=(gots2[1],))
+    grad_mixed, gain2, bias2 = norm2_half(1, grad_mixed, gain2, bias2)
     grad_heads = mm(clock.hold(grad_mixed), out_own, NT)
     clock.set(grad_heads)
+    turn(down_ring, up_ring)
 
     (grads,) = by_heads(
         back_kernel,
-        [(query, rows, 0), (key, rows, 0), (value, rows, 0), (key_ctx, CTX, 0), (value_ctx, CTX, 0)]
+        [(qkv_rows, rows, 0, i) for i in range(3)]
+        + [(kv_ctx, CTX, 0, i) for i in range(2)]
         + [(a, rows, 0) for a in (outs, log, clock.hold(grad_heads))],
         [(3, CTX + rows)],
         scalars=(ok,),
     )
     clock.set(grads)
-    up_ring.turn(clock)
-    down_ring.turn(clock)
+    turn(down_ring, up_ring)
     gives = [mm(core_half(clock.hold(seen), 1 - core), grads[i], TN) for i in range(3)]
     gives.append(mm(core_half(clock.hold(grad_mixed), 1 - core), outs, TN))
     gots = [swap_bit(g, "seq", 0) for g in gives]
     clock.set(*gives)
-    up_ring.turn(clock)
-    down_ring.turn(clock)
-    feed = mm(clock.hold(hidden), down)
-    clock.set(feed)
-    feed = lax.psum(feed, "mp")
-    up_ring.turn(clock)
-    down_ring.turn(clock)
+    turn(down_ring, up_ring)
     keeps = [mm(core_half(clock.hold(seen), core), grads[i], TN) + gots[i] for i in range(3)]
     keeps.append(mm(core_half(clock.hold(grad_mixed), core), outs, TN) + gots[3])
     attn_ring = Ring([[k] for k in keeps], (3, 1))
     clock.set(attn_ring.held)
-    while up_ring.step < hops:
-        up_ring.turn(clock)
-        if down_ring.step < hops + 2:
-            down_ring.turn(clock)
-
-    left_down, left_up = 2 * hops - down_ring.step, 2 * hops - up_ring.step
-    queue = [up_ring] * (left_up - left_down) + [down_ring, up_ring] * left_down
-
-    def next_turn():
-        if attn_ring.step < attn_ring.count * 2 - 2:
-            attn_ring.turn(clock)
-        if queue:
-            queue.pop(0).turn(clock)
-
-    held = clock.hold(grads)
-    grad_seen = sum(mm(held[i], qkv[i], NT) for i in range(3))
+    turn(down_ring, up_ring)
+
+    feed = mm(clock.hold(hidden), down)
+    clock.set(feed)
+    turn(attn_ring, down_ring, up_ring)
+    grad_seen = sum(mm(clock.hold(grads)[i], qkv[i], NT) for i in range(3))
     grad_context = jnp.where(has_ctx, grad_seen[:CTX], 0.0)
     clock.set(grad_seen)
-    next_turn()
+    quarter = rows // 4
+    result, grad_tokens = unset((rows, width)), unset((rows, width))
+
+    def across(source, k, into, base):
+        span = slice(k * quarter, (k + 1) * quarter)
+        got = swap_bit(source[span], "mp", 0)
+        (got,) = turn(attn_ring, down_ring, up_ring, kept=(got,))
+        return lax.dynamic_update_slice(into, base(span) + (source[span] + got), (k * quarter, 0))
+
+    def result_base(span):
+        return mixed[span] + down_bias
+
+    result = across(feed, 0, result, result_base)
 
     sum_q, sum_r, part_h, part_p, part_skip, grad_tail = by_channels(
         tail_back_kernel,
@@ -714,7 +751,9 @@
         [states, states, states, states, 1, CTX],
     )
     clock.set(sum_q)
-    next_turn()
+    result = across(feed, 1, result, result_base)
+    (sum_p,) = by_channels(moment_kernel, [tail, clock.hold(normed), decay], [states])
+    clock.set(sum_p)
     other = swap_bit(jnp.concatenate([sum_p, sum_q], 0), "seq", 0)
     other_p, other_q = other[:states], other[states:]
     first_p, second_p = jnp.where(core == 0, sum_p, other_p), jnp.where(core == 0, other_p, sum_p)
@@ -726,7 +765,8 @@
     past_p = jnp.zeros_like(sum_p)
     later = jnp.zeros_like(sum_q)
     came = [trade_chips(both, d) for d in range(1, chips)]
-    next_turn()
+    result = across(feed, 2, result, result_base)
+    came[0] = clock.hold(came[0])
     for d in range(1, chips):
         there = chip ^ d
         gap = (jnp.maximum(jnp.abs(chip - there) - 1, 0)).astype(jnp.float32) * (2.0 * length)
@@ -738,59 +778,63 @@
     later = jnp.where(core == 1, later, second_q + faded(length) * later)
     far_tail, grad_rows = by_channels(
         spread_kernel,
-        [clock.hold(gate * later), decay],
+        [gate * later, decay],
         [CTX, rows - CTX],
     )
     to_last = far_tail + grad_tail
     clock.set(to_last)
     from_next = shift_in_window(to_last, -1, per_window)
-    next_turn()
-    along_h = fade * past_h * sum_q + part_h
+    result = across(feed, 3, result, result_base)
+    along_h = fade * clock.hold(past_h) * sum_q + part_h
     along_p = fade * (past_h * (sum_r + sum_q) + past_p * sum_q) + part_p
     gone = faded(start_t + 1.0)
     part_in = c_out * along_h
     part_out = c_in * along_h + carried * gone * sum_q
     part_decay = -gate * along_p - c_out * carried * gone * ((start_t + 1.0) * sum_q + sum_r)
-    stacked = jnp.concatenate([part_in, part_out, part_decay, part_skip], 0)
-    clock.set(stacked)
+    clock.set(part_in, part_out, part_decay)
+
     grad_normed = grad_seen[CTX:] + jnp.concatenate([grad_rows, clock.hold(from_next)], 0)
-    result = mixed + clock.hold(feed) + down_bias
-    grad_normed = after(grad_normed, result)
-    clock.set(grad_normed)
-    grad_normed = lax.psum(grad_normed, "mp")
-    next_turn()
-    far_stacked = swap_bit(stacked, "mp", 0)
-    grad_up_bias = jnp.sum(clock.hold(grad_pre), axis=0)
-    clock.set(grad_up_bias)
-    next_turn()
-    grad_down_bias = jnp.sum(clock.hold(cotangent), axis=0)
+    part_gain1 = jnp.sum(grad_normed * unit1, axis=0, keepdims=True)
+    part_bias1 = jnp.sum(grad_normed, axis=0, keepdims=True)
+    part_tokens = norm_back(grad_normed, unit1, rate1, norm1_gain)
+    clock.set(part_tokens, part_gain1, part_bias1)
+    turn(attn_ring, down_ring, up_ring)
+    stacked = jnp.concatenate([part_in, part_out, part_decay, part_skip, part_gain1, part_bias1], 0)
+    for k in range(4):
+        if k == 1:
+            grad_up_bias = jnp.sum(clock.hold(grad_pre), axis=0)
+            grad_down_bias = jnp.sum(clock.hold(cotangent), axis=0)
+            clock.set(grad_up_bias, grad_down_bias)
+        grad_tokens = across(part_tokens, k, grad_tokens, lambda span: grad_mixed[span])
+
+    (stacked_far,) = turn(attn_ring, down_ring, up_ring, kept=(swap_bit(stacked, "mp", 0),))
+    while up_ring.step < 2 * hops or down_ring.step < 2 * hops:
+        turn(attn_ring, down_ring, up_ring)
     ups = grad_up_bias.reshape(-1, width)
     small = jnp.concatenate(
-        [stacked + clock.hold(far_stacked), jnp.stack([gain2, bias2, grad_down_bias]), ups], 0
-    )
-    clock.set(small)
+        [stacked + stacked_far, jnp.stack([gain2, bias2, grad_down_bias]), ups], 0
+    )
+    todo = [down_ring, up_ring]
+    whole = {}
     for bit in range(bits_of(lax.axis_size("seq"))):
         other = swap_bit(small, "seq", bit)
-        next_turn()
-        small = small + clock.hold(other)
-        clock.set(small)
-    while attn_ring.step < attn_ring.count * 2 - 2 - LATE:
-        next_turn()
-    last = clock.hold(grad_normed)
-    grad_gain1 = jnp.sum(last * unit1, axis=0)
-    grad_bias1 = jnp.sum(last, axis=0)
-    grad_tokens = grad_mixed + norm_back(last, unit1, rate1, norm1_gain)
-    late = jnp.stack([grad_gain1, grad_bias1])
-    clock.set(grad_tokens, late)
-    for bit in range(bits_of(lax.axis_size("seq"))):
-        other = swap_bit(late, "seq", bit)
-        next_turn()
-        late = late + clock.hold(other)
-        clock.set(late)
-    while attn_ring.step < attn_ring.count * 2 - 2:
-        next_turn()
-    grad_down = down_ring.results()[0][0]
-    grad_up = up_ring.results()[0][0]
+        kept = [other]
+        if todo:
+            ring = todo.pop(0)
+            ring.own[0] = clock.hold(ring.own[0])
+            whole[ring] = len(kept)
+            kept.append(ring.results()[0])
+        if attn_ring.step < 2 * hops:
+            other, *made = turn(attn_ring, kept=kept)
+        else:
+            other, *made = kept
+        for ring, at in list(whole.items()):
+            if isinstance(at, int):
+                whole[ring] = made[at - 1]
+        small = small + other
+    while attn_ring.step < 2 * hops:
+        turn(attn_ring)
+    grad_down, grad_up = whole[down_ring][0], whole[up_ring][0]
     grad_qkv, grad_out = attn_ring.results()
     grad_out = jnp.transpose(grad_out[0])
 
@@ -805,20 +849,20 @@
     return (
         result,
         grad_tokens,
-        late[0],
-        late[1],
+        small[0],
+        small[1],
         grad_in,
         grad_out_coef,
         grad_decay,
         grad_skip,
         grad_qkv,
         grad_out,
-        small[0],
-        small[1],
+        small[2],
+        small[3],
         grad_up,
-        small[3:].reshape(-1),
+        small[5:].reshape(-1),
         grad_down,
-        small[2],
+        small[4],
     )
 
 

time: 558 us -> 535 us (0.959)
  waiting for transfers between devices: 177 us -> 150 us
  matrix products: 90.1 us -> 70.6 us
  local copies, waits for them, and re-layouts: 26.1 us -> 44.1 us
  between operations: 17.9 us -> 3.93 us
  starting transfers between devices: 86 us -> 99.7 us
    dot_general x31 -> x26, matrix products: 90.1 us -> 70.6 us  [mm(): lax.dot_general(left, right, (dims, ((), ())), precision=HIGH, preferred_...]
    psum x2 -> x0, waiting for transfers between devices: 19.3 us -> none  [the longest x1 19.3 us: per_device(): feed = lax.psum(feed, 'mp')]
    unnamed x244 -> x234, local copies, waits for them, and re-layouts: 12.5 us -> 30.5 us
    ppermute x6, waiting for transfers between devices: 14.5 us -> 0.02 us  [trade_chips(): lax.ppermute(value, 'seq', [(i, i ^ 2 * distance) for i in range(size)])]
    dynamic_update_slice x0 -> x8, other arithmetic: none -> 12.9 us  [the longest x6 10.9 us: across(): lax.dynamic_update_slice(into, base(span) + (source[span] + got), (k * qu...]
    ppermute x42, starting transfers between devices: 36.7 us -> 46.2 us  [turn(): got = lax.ppermute(self.held, 'seq', self.route)]
    ppermute x6, starting transfers between devices: 5.36 us -> 12.9 us  [trade_chips(): lax.ppermute(value, 'seq', [(i, i ^ 2 * distance) for i in range(size)])]
    add x21, other arithmetic: 30.8 us -> 23.6 us  [turn(): got + self.chunk((self.place + 2 * self.count - self.step) % self.count)]
  transfers between devices with their start and end apart: 104 -> 106, of which waited for: 37 -> 32; matrix products, arithmetic and copies ran while one was open for 27% -> 26% of each run, Pallas kernels for 12% -> 13%
where the time goes in v4:
time: 535 us; the launch traced here: 528 us
  waiting for transfers between devices  150 us (28%)
  starting transfers between devices  99.7 us (19%)
  Pallas kernels  81.6 us (15%)
  other arithmetic  77.9 us (15%)
  matrix products  70.6 us (13%)
  local copies, waits for them, and re-layouts  44.1 us (8%)
    ppermute x42, waiting for transfers between devices, turn(): got = lax.ppermute(self.held, 'seq', self.route)  86.3 us
    dot_general x26, matrix products, mm(): lax.dot_general(left, right, (dims, ((), ())), precision=HIGH, preferred_...  70.6 us
    ppermute x56, waiting for transfers between devices, swap_bit(): return lax.ppermute(value, axis, [(i, i ^ 1 << bit) for i in range(size)])  63.8 us
    ppermute x42, starting transfers between devices, turn(): got = lax.ppermute(self.held, 'seq', self.route)  46.2 us
    ppermute x56, starting transfers between devices, swap_bit(): return lax.ppermute(value, axis, [(i, i ^ 1 << bit) for i in range(size)])  36.6 us
    pallas_call x6, Pallas kernels, by_channels(): pl.pallas_call(kernel, grid=(width // cut,), in_specs=[spec(a.shape[0]) f...  32.1 us
    unnamed x234, local copies, waits for them, and re-layouts  30.5 us
    pallas_call x4, Pallas kernels, by_heads(): pl.pallas_call(kernel, grid=(heads,), in_specs=specs, out_specs=[pl.Block...  23.7 us
  transfers between devices with their start and end apart: 106, of which 32 were waited for; matrix products, arithmetic and copies ran while one was open for 26% of the time, Pallas kernels for 13%

profile of v4, /device:TPU:0, one launch (start us, length us, event | category | flops | bytes accessed | tf_op | source)
XLA Modules:
  0.0 527.9 jit_solution(13578298411179745726)
XLA Ops:
  33.6 6.1 %shard_map.317 = (f32[512,512]{1,0:T(8,128)S(1)}, f32[512,512]{1,0:T(8,128)S(1)}, f32[512,512]{1,0:T(8,128)S(1)}) custom-call(f32[3,512,512]{2,1,0:T(8,128)S(1)} %shard_map.316.q_ref.k_ref.v_ref, f32[3,512,512]{2,1,0:T(8,128)S(1)} %shard_map.316.q_ref.k_ref.v_ref, f32[3,512,512]{2,1,0:T(8,128)S(1)} %shard_map.316.q_ref.k_ref.v_ref), custom_call_target="tpu_custom_call" | custom-call | bytes 1024 | tf_op jit(solution)/shard_map/pallas_call | solution.py:477
  44.5 5.0 shard_map.318
  54.7 8.8 %collective-permute-start.9 = (f32[16,1024]{1,0:T(8,128)}, f32[16,1024]{1,0:T(8,128)}, u32[]{:S(2)}, u32[]{:S(2)}) collective-permute-start(f32[16,1024]{1,0:T(8,128)} %get-tuple-element.305), channel_id=1, source_target_pairs={{0,12},{2,14},{4,8},{6,10},{8,4},{10,6},{12,0},{14,2},{16,28},{18,... | collective-permute-start | bytes 196616 | tf_op jit(solution)/shard_map/ppermute | solution.py:77
  64.7 4.4 shard_map.319.near_ref
  92.6 4.5 fusion.106
  113.6 5.1 fusion.15
  122.8 5.9 %fusion.13 = f32[1024,1024]{1,0:T(8,128)S(1)} fusion(f32[512,1024]{1,0:T(8,128)} %param.36, f32[512,2048]{1,0:T(8,128)} %copy-done.50, s32[]{:T(128)S(6)} %select_n.505), kind=kOutput, calls=%fused_computation.26 | convolution fusion | flops 3221225472 | bytes 8388612 | tf_op jit(solution)/shard_map/dot_general | solution.py:20
  136.3 10.7 %collective-permute-done.16 = f32[256,1024]{1,0:T(8,128)S(1)} collective-permute-done((f32[256,1024]{1,0:T(8,128)}, f32[256,1024]{1,0:T(8,128)S(1)}, u32[]{:S(2)}, u32[]{:S(2)}) %collective-permute-start.16) | collective-permute-done | bytes 1048608 | tf_op jit(solution)/shard_map/ppermute | solution.py:40
  152.7 5.1 fusion.46
  160.8 6.6 %collective-permute-done.17 = f32[1,128,1024]{2,1,0:T(8,128)} collective-permute-done((f32[1,128,1024]{2,1,0:T(8,128)}, f32[1,128,1024]{2,1,0:T(8,128)}, u32[]{:S(2)}, u32[]{:S(2)}) %collective-permute-start.17) | collective-permute-done | bytes 524320 | tf_op jit(solution)/shard_map/ppermute | solution.py:164
  170.4 6.8 %convolution_add_fusion = f32[512,2048]{1,0:T(8,128)S(1)} fusion(f32[512,2048]{1,0:T(8,128)} %collective-permute-done.18, f32[512,2048]{1,0:T(8,128)} %copy-done.24, f32[512,1024]{1,0:T(8,128)S(1)} %copy-done.60, s32[]{:T(128)S(6)} %select_n.516), kind=kOutput, calls=%fused_computation | convolution fusion | flops 3222274048 | bytes 13631492 | tf_op jit(solution)/shard_map/dot_general | solution.py:20
  177.4 7.5 %collective-permute-done.21 = f32[256,1024]{1,0:T(8,128)} collective-permute-done((f32[256,1024]{1,0:T(8,128)}, f32[256,1024]{1,0:T(8,128)}, u32[]{:S(2)}, u32[]{:S(2)}) %collective-permute-start.21) | collective-permute-done | bytes 1048608 | tf_op jit(solution)/shard_map/ppermute | solution.py:40
  204.7 11.4 %shard_map.328 = f32[3,640,512]{2,1,0:T(8,128)S(1)} custom-call(s32[1]{0:T(128)} %bitcast.ok_ref, f32[3,512,512]{2,1,0:T(8,128)S(1)} %shard_map.316.q_ref.k_ref.v_ref, f32[3,512,512]{2,1,0:T(8,128)S(1)} %shard_map.316.q_ref.k_ref.v_ref, f32[3,512,512]{2,1,0:T(8,128)S(1)} %shard_map.316.q_ref.k_ref.v_ref, f32[2,128,512]{2,1,0:T(8,128)S(1)} %copy-done.7, ...), custom_call_target="tpu_custom_call" | custom-call | bytes 1024 | tf_op jit(solution)/shard_map/pallas_call | solution.py:477
  252.6 4.5 fusion.109
  258.7 10.7 %collective-permute-done.35 = f32[4,64,512]{2,1,0:T(8,128)S(1)} collective-permute-done((f32[4,64,512]{2,1,0:T(8,128)S(1)}, f32[4,64,512]{2,1,0:T(8,128)S(1)}, u32[]{:S(2)}, u32[]{:S(2)}) %collective-permute-start.35) | collective-permute-done | bytes 524320 | tf_op jit(solution)/shard_map/ppermute | solution.py:164
  284.7 5.3 collective-permute-done.36
  295.4 7.5 %shard_map.329 = (f32[16,1024]{1,0:T(8,128)}, f32[16,1024]{1,0:T(8,128)}, f32[16,1024]{1,0:T(8,128)}, f32[16,1024]{1,0:T(8,128)}, f32[1,1024]{1,0:T(1,128)}, /*index=5*/f32[128,1024]{1,0:T(8,128)}) custom-call(f32[128,1024]{1,0:T(8,128)} %collective-permute-done.tail_ref.x_ref, f32[128,1024]{1,0:T(8,128)} %slice_select_fusion.d_ref, ...), custom_call_target="tpu_custom_call" | custom-call | bytes 1024 | tf_op jit(solution)/shard_map/pallas_call | solution.py:374
  309.8 7.7 %shard_map.330 = f32[16,1024]{1,0:T(8,128)} custom-call(f32[128,1024]{1,0:T(8,128)} %collective-permute-done.tail_ref.x_ref, f32[512,1024]{1,0:T(8,128)} %copy-done, f32[16,1024]{1,0:T(8,128)} %slice.270.decay_ref), custom_call_target="tpu_custom_call" | custom-call | bytes 1024 | tf_op jit(solution)/shard_map/pallas_call | solution.py:374
  329.6 6.8 %collective-permute-done.46.refs_4_ = f32[1,128,1024]{2,1,0:T(8,128)} collective-permute-done((f32[1,128,1024]{2,1,0:T(8,128)}, f32[1,128,1024]{2,1,0:T(8,128)}, u32[]{:S(2)}, u32[]{:S(2)}) %collective-permute-start.46) | collective-permute-done | bytes 524320 | tf_op jit(solution)/shard_map/ppermute | solution.py:164
  343.8 4.9 shard_map.331
  366.2 13.3 %collective-permute-done.59 = f32[4,64,512]{2,1,0:T(8,128)S(1)} collective-permute-done((f32[4,64,512]{2,1,0:T(8,128)S(1)}, f32[4,64,512]{2,1,0:T(8,128)S(1)}, u32[]{:S(2)}, u32[]{:S(2)}) %collective-permute-start.59) | collective-permute-done | bytes 524320 | tf_op jit(solution)/shard_map/ppermute | solution.py:164
  389.8 4.8 collective-permute-done.62.refs_7_
  394.6 5.6 %collective-permute-done.60.refs_4_ = f32[1,64,2048]{2,1,0:T(8,128)} collective-permute-done((f32[1,64,2048]{2,1,0:T(8,128)}, f32[1,64,2048]{2,1,0:T(8,128)}, u32[]{:S(2)}, u32[]{:S(2)}) %collective-permute-start.60) | collective-permute-done | bytes 524320 | tf_op jit(solution)/shard_map/ppermute | solution.py:164
  411.4 7.3 %collective-permute-done.65 = f32[128,1024]{1,0:T(8,128)} collective-permute-done((f32[128,1024]{1,0:T(8,128)}, f32[128,1024]{1,0:T(8,128)}, u32[]{:S(2)}, u32[]{:S(2)}) %collective-permute-start.65) | collective-permute-done | bytes 524320 | tf_op jit(solution)/shard_map/ppermute | solution.py:40
  421.5 6.0 %collective-permute-done.68 = f32[128,1024]{1,0:T(8,128)S(1)} collective-permute-done((f32[128,1024]{1,0:T(8,128)}, f32[128,1024]{1,0:T(8,128)S(1)}, u32[]{:S(2)}, u32[]{:S(2)}) %collective-permute-start.68) | collective-permute-done | bytes 524320 | tf_op jit(solution)/shard_map/ppermute | solution.py:40
  438.4 8.6 %collective-permute-done.74 = f32[51,1024]{1,0:T(8,128)S(1)} collective-permute-done((f32[51,1024]{1,0:T(8,128)S(1)}, f32[51,1024]{1,0:T(8,128)S(1)}, u32[]{:S(2)}, u32[]{:S(2)}) %collective-permute-start.74) | collective-permute-done | bytes 208928 | tf_op jit(solution)/shard_map/ppermute | solution.py:40
  453.6 5.7 %collective-permute-done.75.refs_5_ = f32[4,64,512]{2,1,0:T(8,128)S(1)} collective-permute-done((f32[4,64,512]{2,1,0:T(8,128)S(1)}, f32[4,64,512]{2,1,0:T(8,128)S(1)}, u32[]{:S(2)}, u32[]{:S(2)}) %collective-permute-start.75) | collective-permute-done | bytes 524320 | tf_op jit(solution)/shard_map/ppermute | solution.py:164
  462.2 6.9 %shard_map.333 = f32[1,2,8,128,1024]{4,3,2,1,0:T(8,128)} custom-call(s32[2,16]{1,0:T(2,128)} %pad_add_fusion.where_ref, f32[1,128,1024]{2,1,0:T(8,128)} %copy-done.62, f32[1,128,1024]{2,1,0:T(8,128)} %copy-done.67, f32[1,128,1024]{2,1,0:T(8,128)} %collective-permute-done.38.refs_2_, f32[1,128,1024]{2,1,0:T(8,128)} %collective-permute-done.42.refs_3_, ...), custom_call_target="tpu_custom_call" | custom-call | bytes 1024 | tf_op jit(solution)/shard_map/pallas_call | solution.py:187
  477.1 6.9 %shard_map.334 = f32[1,2,8,64,2048]{4,3,2,1,0:T(8,128)} custom-call(s32[2,16]{1,0:T(2,128)} %pad_add_fusion.where_ref, f32[1,64,2048]{2,1,0:T(8,128)} %dynamic-slice_add_fusion.refs_0_, f32[1,64,2048]{2,1,0:T(8,128)} %collective-permute-done.44.refs_1_, f32[1,64,2048]{2,1,0:T(8,128)} %collective-permute-done.49.refs_2_, ...), custom_call_target="tpu_custom_call" | custom-call | bytes 1024 | tf_op jit(solution)/shard_map/pallas_call | solution.py:187
  490.7 7.2 %collective-permute-done.96 = f32[56,1024]{1,0:T(8,128)S(1)} collective-permute-done((f32[56,1024]{1,0:T(8,128)S(1)}, f32[56,1024]{1,0:T(8,128)S(1)}, u32[]{:S(2)}, u32[]{:S(2)}) %collective-permute-start.96) | collective-permute-done | bytes 229408 | tf_op jit(solution)/shard_map/ppermute | solution.py:40
  501.5 10.3 %collective-permute-done.97 = f32[56,1024]{1,0:T(8,128)S(1)} collective-permute-done((f32[56,1024]{1,0:T(8,128)S(1)}, f32[56,1024]{1,0:T(8,128)S(1)}, u32[]{:S(2)}, u32[]{:S(2)}) %collective-permute-start.97) | collective-permute-done | bytes 229408 | tf_op jit(solution)/shard_map/ppermute | solution.py:40
  517.9 6.9 %shard_map.335 = (f32[3,2,8,64,512]{4,3,2,1,0:T(8,128)}, f32[1,2,8,64,512]{4,3,2,1,0:T(8,128)}) custom-call(s32[2,16]{1,0:T(2,128)} %pad_add_fusion.where_ref, f32[4,64,512]{2,1,0:T(8,128)} %maximum_add_fusion.6.refs_0_, f32[4,64,512]{2,1,0:T(8,128)} %collective-permute-done.66.refs_1_, f32[4,64,512]{2,1,0:T(8,128)} %copy-done.68, f32[4,64,512]{2,1,0:T(8,128)} %copy-done.70, ...), custom_call_target="tpu_custom_call" | custom-call | bytes 1024 | tf_op jit(solution)/shard_map/pallas_call | solution.py:187
  (582 shorter events, 299.3 us)
Async XLA Ops:
  16.1 28.4 %collective-permute-start = (f32[128,1024]{1,0:T(8,128)}, f32[128,1024]{1,0:T(8,128)}, u32[]{:S(2)}, u32[]{:S(2)}) collective-permute-start(f32[128,1024]{1,0:T(8,128)} %slice.269), channel_id=1, source_target_pairs={{0,2},{2,4},{4,6},{6,8},{8,10},{10,12},{12,14},{16,18},{18,20},{20... | collective-permute-start | bytes 1572872 | tf_op jit(solution)/shard_map/ppermute | solution.py:51
  23.4 19.3 %collective-permute-start.5 = (f32[81,512]{1,0:T(8,128)S(1)}, f32[81,512]{1,0:T(8,128)}, u32[]{:S(2)}, u32[]{:S(2)}) collective-permute-start(f32[81,512]{1,0:T(8,128)S(1)} %maximum_select_fusion.4), channel_id=1, source_target_pairs={{0,16},{2,18},{4,20},{6,22},{8,24},{10,26},{12,28},{14,30},{16,0},... | collective-permute-start | bytes 497672 | tf_op jit(solution)/shard_map/ppermute | solution.py:40
  51.6 37.6 %collective-permute-start.11 = (f32[256,1024]{1,0:T(8,128)}, f32[256,1024]{1,0:T(8,128)}, u32[]{:S(2)}, u32[]{:S(2)}) collective-permute-start(f32[256,1024]{1,0:T(8,128)} %dynamic-slice_convert_fusion), channel_id=1, source_target_pairs={{0,1},{1,0},{2,3},{3,2},{4,5},{5,4},{6,7},{7,6},{8,9},{9,8},{10,11... | collective-permute-start | bytes 3145736 | tf_op jit(solution)/shard_map/ppermute | solution.py:40
  85.1 22.5 %collective-permute-start.13 = (f32[256,512]{1,0:T(8,128)S(1)}, f32[256,512]{1,0:T(8,128)S(1)}, u32[]{:S(2)}, u32[]{:S(2)}) collective-permute-start(f32[256,512]{1,0:T(8,128)S(1)} %get-tuple-element.138), channel_id=1, source_target_pairs={{0,1},{1,0},{2,3},{3,2},{4,5},{5,4},{6,7},{7,6},{8,9},{9,8},{10,11... | collective-permute-start | bytes 1572872 | tf_op jit(solution)/shard_map/ppermute | solution.py:40
  121.3 25.7 %collective-permute-start.16 = (f32[256,1024]{1,0:T(8,128)}, f32[256,1024]{1,0:T(8,128)S(1)}, u32[]{:S(2)}, u32[]{:S(2)}) collective-permute-start(f32[256,1024]{1,0:T(8,128)} %fusion.97), channel_id=1, source_target_pairs={{0,1},{1,0},{2,3},{3,2},{4,5},{5,4},{6,7},{7,6},{8,9},{9,8},{10,11... | collective-permute-start | bytes 3145736 | tf_op jit(solution)/shard_map/ppermute | solution.py:40
  159.4 25.6 %collective-permute-start.21 = (f32[256,1024]{1,0:T(8,128)}, f32[256,1024]{1,0:T(8,128)}, u32[]{:S(2)}, u32[]{:S(2)}) collective-permute-start(f32[256,1024]{1,0:T(8,128)} %fusion.11), channel_id=1, source_target_pairs={{0,1},{1,0},{2,3},{3,2},{4,5},{5,4},{6,7},{7,6},{8,9},{9,8},{10,11... | collective-permute-start | bytes 3145736 | tf_op jit(solution)/shard_map/ppermute | solution.py:40
  177.3 20.9 %collective-permute-start.19 = (f32[1,64,2048]{2,1,0:T(8,128)S(1)}, f32[1,64,2048]{2,1,0:T(8,128)S(1)}, u32[]{:S(2)}, u32[]{:S(2)}) collective-permute-start(f32[1,64,2048]{2,1,0:T(8,128)S(1)} %constant_dynamic-slice_fusion.31), channel_id=1, source_target_pairs={{0,8},{10,2},{8,16},{18,10},{16,24},{26,18},{24,28},{30,26},{28,20... | collective-permute-start | bytes 1572872 | tf_op jit(solution)/shard_map/ppermute | solution.py:164
  197.6 18.6 %collective-permute-start.24 = (f32[1,128,1024]{2,1,0:T(8,128)}, f32[1,128,1024]{2,1,0:T(8,128)}, u32[]{:S(2)}, u32[]{:S(2)}) collective-permute-start(f32[1,128,1024]{2,1,0:T(8,128)} %add_add_fusion.4), channel_id=1, source_target_pairs={{0,8},{10,2},{8,16},{18,10},{16,24},{26,18},{24,28},{30,26},{28,20... | collective-permute-start | bytes 1572872 | tf_op jit(solution)/shard_map/ppermute | solution.py:164
  199.0 19.1 %collective-permute-start.23 = (f32[1,64,2048]{2,1,0:T(8,128)}, f32[1,64,2048]{2,1,0:T(8,128)}, u32[]{:S(2)}, u32[]{:S(2)}) collective-permute-start(f32[1,64,2048]{2,1,0:T(8,128)} %dynamic-slice_add_fusion.6), channel_id=1, source_target_pairs={{0,8},{10,2},{8,16},{18,10},{16,24},{26,18},{24,28},{30,26},{28,20... | collective-permute-start | bytes 1572872 | tf_op jit(solution)/shard_map/ppermute | solution.py:164
  248.9 22.6 %collective-permute-start.33 = (f32[1,64,2048]{2,1,0:T(8,128)S(1)}, f32[1,64,2048]{2,1,0:T(8,128)S(1)}, u32[]{:S(2)}, u32[]{:S(2)}) collective-permute-start(f32[1,64,2048]{2,1,0:T(8,128)S(1)} %dynamic-slice_add_fusion.3), channel_id=1, source_target_pairs={{0,8},{10,2},{8,16},{18,10},{16,24},{26,18},{24,28},{30,26},{28,20... | collective-permute-start | bytes 1572872 | tf_op jit(solution)/shard_map/ppermute | solution.py:164
  249.2 20.6 %collective-permute-start.34 = (f32[1,128,1024]{2,1,0:T(8,128)S(1)}, f32[1,128,1024]{2,1,0:T(8,128)S(1)}, u32[]{:S(2)}, u32[]{:S(2)}) collective-permute-start(f32[1,128,1024]{2,1,0:T(8,128)S(1)} %add_add_fusion.1.refs_0_), channel_id=1, source_target_pairs={{0,8},{10,2},{8,16},{18,10},{16,24},{26,18},{24,28},{30,26},{28,20... | collective-permute-start | bytes 1572872 | tf_op jit(solution)/shard_map/ppermute | solution.py:164
  251.0 18.4 %collective-permute-start.35 = (f32[4,64,512]{2,1,0:T(8,128)S(1)}, f32[4,64,512]{2,1,0:T(8,128)S(1)}, u32[]{:S(2)}, u32[]{:S(2)}) collective-permute-start(f32[4,64,512]{2,1,0:T(8,128)S(1)} %pad_maximum_fusion.2), channel_id=1, source_target_pairs={{0,8},{10,2},{8,16},{18,10},{16,24},{26,18},{24,28},{30,26},{28,20... | collective-permute-start | bytes 1572872 | tf_op jit(solution)/shard_map/ppermute | solution.py:164
  257.2 27.5 %collective-permute-start.37 = (f32[128,1024]{1,0:T(8,128)S(1)}, f32[128,1024]{1,0:T(8,128)S(1)}, u32[]{:S(2)}, u32[]{:S(2)}) collective-permute-start(f32[128,1024]{1,0:T(8,128)S(1)} %slice.280), channel_id=1, source_target_pairs={{0,1},{1,0},{2,3},{3,2},{4,5},{5,4},{6,7},{7,6},{8,9},{9,8},{10,11... | collective-permute-start | bytes 1572872 | tf_op jit(solution)/shard_map/ppermute | solution.py:40
  271.6 18.4 %collective-permute-start.36 = (f32[1,64,2048]{2,1,0:T(8,128)S(1)}, f32[1,64,2048]{2,1,0:T(8,128)S(1)}, u32[]{:S(2)}, u32[]{:S(2)}) collective-permute-start(f32[1,64,2048]{2,1,0:T(8,128)S(1)} %dynamic-slice_add_fusion.2), channel_id=1, source_target_pairs={{0,8},{10,2},{8,16},{18,10},{16,24},{26,18},{24,28},{30,26},{28,20... | collective-permute-start | bytes 1572872 | tf_op jit(solution)/shard_map/ppermute | solution.py:164
  279.6 23.3 %collective-permute-start.43 = (f32[4,64,512]{2,1,0:T(8,128)}, f32[4,64,512]{2,1,0:T(8,128)}, u32[]{:S(2)}, u32[]{:S(2)}) collective-permute-start(f32[4,64,512]{2,1,0:T(8,128)} %maximum_add_fusion.1), channel_id=1, source_target_pairs={{0,8},{10,2},{8,16},{18,10},{16,24},{26,18},{24,28},{30,26},{28,20... | collective-permute-start | bytes 1572872 | tf_op jit(solution)/shard_map/ppermute | solution.py:164
  284.5 22.3 %collective-permute-start.42 = (f32[1,128,1024]{2,1,0:T(8,128)}, f32[1,128,1024]{2,1,0:T(8,128)}, u32[]{:S(2)}, u32[]{:S(2)}) collective-permute-start(f32[1,128,1024]{2,1,0:T(8,128)} %collective-permute-done.38.refs_2_), channel_id=1, source_target_pairs={{0,8},{10,2},{8,16},{18,10},{16,24},{26,18},{24,28},{30,26},{28,20... | collective-permute-start | bytes 1572872 | tf_op jit(solution)/shard_map/ppermute | solution.py:164
  294.9 31.1 %collective-permute-start.45 = (f32[128,1024]{1,0:T(8,128)}, f32[128,1024]{1,0:T(8,128)}, u32[]{:S(2)}, u32[]{:S(2)}) collective-permute-start(f32[128,1024]{1,0:T(8,128)} %get-tuple-element.263), channel_id=1, source_target_pairs={{0,1},{1,0},{2,3},{3,2},{4,5},{5,4},{6,7},{7,6},{8,9},{9,8},{10,11... | collective-permute-start | bytes 1572872 | tf_op jit(solution)/shard_map/ppermute | solution.py:40
  305.0 19.2 %collective-permute-start.47 = (f32[4,64,512]{2,1,0:T(8,128)}, f32[4,64,512]{2,1,0:T(8,128)}, u32[]{:S(2)}, u32[]{:S(2)}) collective-permute-start(f32[4,64,512]{2,1,0:T(8,128)} %maximum_add_fusion.2), channel_id=1, source_target_pairs={{0,8},{10,2},{8,16},{18,10},{16,24},{26,18},{24,28},{30,26},{28,20... | collective-permute-start | bytes 1572872 | tf_op jit(solution)/shard_map/ppermute | solution.py:164
  318.4 19.7 %collective-permute-start.44 = (f32[1,64,2048]{2,1,0:T(8,128)}, f32[1,64,2048]{2,1,0:T(8,128)}, u32[]{:S(2)}, u32[]{:S(2)}) collective-permute-start(f32[1,64,2048]{2,1,0:T(8,128)} %dynamic-slice_add_fusion.refs_0_), channel_id=1, source_target_pairs={{0,8},{10,2},{8,16},{18,10},{16,24},{26,18},{24,28},{30,26},{28,20... | collective-permute-start | bytes 1572872 | tf_op jit(solution)/shard_map/ppermute | solution.py:164
  324.2 17.9 %collective-permute-start.54 = (f32[32,1024]{1,0:T(8,128)}, f32[32,1024]{1,0:T(8,128)}, u32[]{:S(2)}, u32[]{:S(2)}) collective-permute-start(f32[32,1024]{1,0:T(8,128)} %pad_maximum_fusion.4), channel_id=1, source_target_pairs={{0,8},{2,10},{4,12},{6,14},{8,0},{10,2},{12,4},{14,6},{16,24},{18,... | collective-permute-start | bytes 393224 | tf_op jit(solution)/shard_map/ppermute | solution.py:77
  338.1 19.0 %collective-permute-start.50 = (f32[128,1024]{1,0:T(8,128)}, f32[128,1024]{1,0:T(8,128)}, u32[]{:S(2)}, u32[]{:S(2)}) collective-permute-start(f32[128,1024]{1,0:T(8,128)} %get-tuple-element.261), channel_id=1, source_target_pairs={{0,1},{1,0},{2,3},{3,2},{4,5},{5,4},{6,7},{7,6},{8,9},{9,8},{10,11... | collective-permute-start | bytes 1572872 | tf_op jit(solution)/shard_map/ppermute | solution.py:40
  357.1 24.9 %collective-permute-start.57 = (f32[1,64,2048]{2,1,0:T(8,128)}, f32[1,64,2048]{2,1,0:T(8,128)}, u32[]{:S(2)}, u32[]{:S(2)}) collective-permute-start(f32[1,64,2048]{2,1,0:T(8,128)} %collective-permute-done.49.refs_2_), channel_id=1, source_target_pairs={{0,8},{10,2},{8,16},{18,10},{16,24},{26,18},{24,28},{30,26},{28,20... | collective-permute-start | bytes 1572872 | tf_op jit(solution)/shard_map/ppermute | solution.py:164
  358.9 23.1 %collective-permute-start.58 = (f32[1,128,1024]{2,1,0:T(8,128)}, f32[1,128,1024]{2,1,0:T(8,128)}, u32[]{:S(2)}, u32[]{:S(2)}) collective-permute-start(f32[1,128,1024]{2,1,0:T(8,128)} %collective-permute-done.51.refs_5_), channel_id=1, source_target_pairs={{0,8},{10,2},{8,16},{18,10},{16,24},{26,18},{24,28},{30,26},{28,20... | collective-permute-start | bytes 1572872 | tf_op jit(solution)/shard_map/ppermute | solution.py:164
  358.9 20.6 %collective-permute-start.59 = (f32[4,64,512]{2,1,0:T(8,128)S(1)}, f32[4,64,512]{2,1,0:T(8,128)S(1)}, u32[]{:S(2)}, u32[]{:S(2)}) collective-permute-start(f32[4,64,512]{2,1,0:T(8,128)S(1)} %maximum_add_fusion.4), channel_id=1, source_target_pairs={{0,8},{10,2},{8,16},{18,10},{16,24},{26,18},{24,28},{30,26},{28,20... | collective-permute-start | bytes 1572872 | tf_op jit(solution)/shard_map/ppermute | solution.py:164
  382.0 18.2 %collective-permute-start.60 = (f32[1,64,2048]{2,1,0:T(8,128)}, f32[1,64,2048]{2,1,0:T(8,128)}, u32[]{:S(2)}, u32[]{:S(2)}) collective-permute-start(f32[1,64,2048]{2,1,0:T(8,128)} %collective-permute-done.57.refs_3_), channel_id=1, source_target_pairs={{0,8},{10,2},{8,16},{18,10},{16,24},{26,18},{24,28},{30,26},{28,20... | collective-permute-start | bytes 1572872 | tf_op jit(solution)/shard_map/ppermute | solution.py:164
  389.7 17.8 %collective-permute-start.66 = (f32[4,64,512]{2,1,0:T(8,128)}, f32[4,64,512]{2,1,0:T(8,128)}, u32[]{:S(2)}, u32[]{:S(2)}) collective-permute-start(f32[4,64,512]{2,1,0:T(8,128)} %maximum_add_fusion.6.refs_0_), channel_id=1, source_target_pairs={{0,8},{10,2},{8,16},{18,10},{16,24},{26,18},{24,28},{30,26},{28,20... | collective-permute-start | bytes 1572872 | tf_op jit(solution)/shard_map/ppermute | solution.py:164
  407.6 19.9 %collective-permute-start.68 = (f32[128,1024]{1,0:T(8,128)}, f32[128,1024]{1,0:T(8,128)S(1)}, u32[]{:S(2)}, u32[]{:S(2)}) collective-permute-start(f32[128,1024]{1,0:T(8,128)} %get-tuple-element.259), channel_id=1, source_target_pairs={{0,1},{1,0},{2,3},{3,2},{4,5},{5,4},{6,7},{7,6},{8,9},{9,8},{10,11... | collective-permute-start | bytes 1572872 | tf_op jit(solution)/shard_map/ppermute | solution.py:40
  428.1 18.9 %collective-permute-start.71 = (f32[128,1024]{1,0:T(8,128)}, f32[128,1024]{1,0:T(8,128)}, u32[]{:S(2)}, u32[]{:S(2)}) collective-permute-start(f32[128,1024]{1,0:T(8,128)} %get-tuple-element.257), channel_id=1, source_target_pairs={{0,1},{1,0},{2,3},{3,2},{4,5},{5,4},{6,7},{7,6},{8,9},{9,8},{10,11... | collective-permute-start | bytes 1572872 | tf_op jit(solution)/shard_map/ppermute | solution.py:40
  451.3 17.9 %collective-permute-start.87 = (f32[1,64,2048]{2,1,0:T(8,128)}, f32[1,64,2048]{2,1,0:T(8,128)}, u32[]{:S(2)}, u32[]{:S(2)}) collective-permute-start(f32[1,64,2048]{2,1,0:T(8,128)} %dynamic-slice_add_fusion.refs_0_), channel_id=1, source_target_pairs={{0,2},{2,0},{4,6},{6,4},{8,10},{10,8},{12,14},{14,12},{16,18},{18,... | collective-permute-start | bytes 1572872 | tf_op jit(solution)/shard_map/ppermute | solution.py:40
  476.5 35.4 %collective-permute-start.98 = (f32[4,64,512]{2,1,0:T(8,128)}, f32[4,64,512]{2,1,0:T(8,128)}, u32[]{:S(2)}, u32[]{:S(2)}) collective-permute-start(f32[4,64,512]{2,1,0:T(8,128)} %maximum_add_fusion.6.refs_0_), channel_id=1, source_target_pairs={{0,2},{2,0},{4,6},{6,4},{8,10},{10,8},{12,14},{14,12},{16,18},{18,... | collective-permute-start | bytes 1572872 | tf_op jit(solution)/shard_map/ppermute | solution.py:40
  477.0 35.6 %collective-permute-start.99 = (f32[4,64,512]{2,1,0:T(8,128)}, f32[4,64,512]{2,1,0:T(8,128)}, u32[]{:S(2)}, u32[]{:S(2)}) collective-permute-start(f32[4,64,512]{2,1,0:T(8,128)} %collective-permute-done.66.refs_1_), channel_id=1, source_target_pairs={{0,2},{2,0},{4,6},{6,4},{8,10},{10,8},{12,14},{14,12},{16,18},{18,... | collective-permute-start | bytes 1572872 | tf_op jit(solution)/shard_map/ppermute | solution.py:40
  488.2 24.4 %collective-permute-start.100 = (f32[4,64,512]{2,1,0:T(8,128)S(1)}, f32[4,64,512]{2,1,0:T(8,128)S(1)}, u32[]{:S(2)}, u32[]{:S(2)}) collective-permute-start(f32[4,64,512]{2,1,0:T(8,128)S(1)} %copy-done.69), channel_id=1, source_target_pairs={{0,2},{2,0},{4,6},{6,4},{8,10},{10,8},{12,14},{14,12},{16,18},{18,... | collective-permute-start | bytes 1572872 | tf_op jit(solution)/shard_map/ppermute | solution.py:40
  (187 other events, 1748.1 us)

commit v5 on v4

--- a/solution.py
+++ b/solution.py
@@ -108,7 +108,24 @@
         lambda out: None,
         out_shape=jax.ShapeDtypeStruct(shape, jnp.float32),
         out_specs=pl.BlockSpec(memory_space=pl.ANY),
+        compiler_params=pltpu.CompilerParams(vmem_limit_bytes=1 << 20),
     )()
+
+
+def pack_kernel(*refs):
+    low = 0
+    for ref in refs[:-1]:
+        refs[-1][low : low + ref.shape[0], :] = ref[...]
+        low += ref.shape[0]
+
+
+def pack(parts):
+    rows, cols = sum(part.shape[0] for part in parts), parts[0].shape[1]
+    return pl.pallas_call(
+        pack_kernel,
+        out_shape=jax.ShapeDtypeStruct((rows, cols), jnp.float32),
+        compiler_params=pltpu.CompilerParams(vmem_limit_bytes=1 << 20),
+    )(*parts)
 
 
 def pick(value, index):
@@ -154,11 +171,23 @@
             [a.reshape(self.count, self.rows, self.cols) for a in addends] for addends in pieces
         ]
         self.outs = outs
-        self.step, self.own, self.far = 0, [], []
+        self.step, self.own, self.far, self.extras = 0, [], [], []
         self.held = self.chunk(self.place)
 
     def chunk(self, spot):
         return jnp.stack([sum(pick(a, spot) for a in addends) for addends in self.pieces])
+
+    def take(self, extra):
+        self.extras = [extra]
+        self.held = jnp.concatenate([self.held, extra], 0)
+
+    def extra_sum(self):
+        count = self.count
+        seen = jnp.stack(self.extras)
+        return sum(
+            lax.dynamic_index_in_dim(seen, (self.place - i + count) % count, 0, keepdims=False)
+            for i in range(count)
+        )
 
     def turn(self, clock, kept=()):
         got = lax.ppermute(self.held, "seq", self.route)
@@ -170,6 +199,8 @@
         if self.step >= self.count - 1:
             self.own.append(got)
             self.far.append(swap_bit(got, "seq", 0))
+        if self.extras:
+            self.extras.append(got[-self.extras[0].shape[0] :])
         clock.set(got)
         return kept
 
@@ -378,6 +409,7 @@
         out_specs=[spec(r) for r in outs],
         out_shape=[jax.ShapeDtypeStruct((r, width), jnp.float32) for r in outs],
         cost_estimate=pl.CostEstimate(flops=0, bytes_accessed=COST, transcendentals=0),
+        compiler_params=pltpu.CompilerParams(vmem_limit_bytes=12 << 20),
     )(*ins)
 
 
@@ -406,7 +438,7 @@
     return lax.broadcasted_iota(jnp.int32, shape, 1) <= row
 
 
-def self_kernel(q_ref, k_ref, v_ref, acc_ref, top_ref, sum_ref):
+def self_kernel(q_ref, k_ref, v_ref, acc_ref, top_ref):
     rows = q_ref.shape[0]
     k, v = cut(k_ref[...]), cut(v_ref[...])
     for first in range(0, rows, TILE):
@@ -418,21 +450,23 @@
         top = jnp.max(scores, axis=1, keepdims=True)
         weight = jnp.exp(scores - top)
         acc_ref[span, :] = dot3(cut(weight), (v[0][:seen], v[1][:seen]), NN)
-        top_ref[span, :] = jnp.broadcast_to(top, (TILE, HDIM))
-        sum_ref[span, :] = jnp.broadcast_to(jnp.sum(weight, axis=1, keepdims=True), (TILE, HDIM))
-
-
-def ctx_kernel(ok_ref, q_ref, k_ref, v_ref, acc_ref, top_ref, sum_ref, out_ref, log_ref):
+        total = jnp.sum(weight, axis=1, keepdims=True)
+        lane = lax.broadcasted_iota(jnp.int32, (TILE, HDIM), 1)
+        top_ref[span, :] = jnp.where(lane < HDIM // 2, top, total)
+
+
+def ctx_kernel(ok_ref, q_ref, k_ref, v_ref, acc_ref, top_ref, out_ref, log_ref):
     ok = ok_ref[0] > 0
     q = cut(q_ref[...] * SCALE)
     scores = dot3(q, cut(k_ref[...]), NT)
     scores = jnp.where(ok, scores, -1e30)
-    top = jnp.maximum(top_ref[...], jnp.max(scores, axis=1, keepdims=True))
-    weight = jnp.where(ok, jnp.exp(scores - top[:, :1]), 0.0)
-    ease = jnp.exp(top_ref[...] - top)
-    total = sum_ref[...] * ease + jnp.sum(weight, axis=1, keepdims=True)
+    near, near_sum = top_ref[:, :1], top_ref[:, HDIM // 2 : HDIM // 2 + 1]
+    top = jnp.maximum(near, jnp.max(scores, axis=1, keepdims=True))
+    weight = jnp.where(ok, jnp.exp(scores - top), 0.0)
+    ease = jnp.exp(near - top)
+    total = near_sum * ease + jnp.sum(weight, axis=1, keepdims=True)
     out_ref[...] = (acc_ref[...] * ease + dot3(cut(weight), cut(v_ref[...]), NN)) / total
-    log_ref[...] = top + jnp.log(total)
+    log_ref[...] = jnp.broadcast_to(top + jnp.log(total), log_ref.shape)
 
 
 def back_kernel(ok_ref, q_ref, k_ref, v_ref, kc_ref, vc_ref, o_ref, l_ref, g_ref, d_ref):
@@ -483,7 +517,7 @@
         ],
         out_shape=[jax.ShapeDtypeStruct(lead + (heads * HDIM,), jnp.float32) for lead in outs],
         cost_estimate=pl.CostEstimate(flops=0, bytes_accessed=COST, transcendentals=0),
-        compiler_params=pltpu.CompilerParams(vmem_limit_bytes=40 << 20),
+        compiler_params=pltpu.CompilerParams(vmem_limit_bytes=16 << 20),
     )(*scalars, *[a[0] for a in ins])
 
 
@@ -514,7 +548,7 @@
         out_shape=jax.ShapeDtypeStruct((count, rows, width), jnp.float32),
         scratch_shapes=[pltpu.VMEM((rows, depth), jnp.bfloat16)] * 2,
         cost_estimate=pl.CostEstimate(flops=0, bytes_accessed=COST, transcendentals=0),
-        compiler_params=pltpu.CompilerParams(vmem_limit_bytes=40 << 20),
+        compiler_params=pltpu.CompilerParams(vmem_limit_bytes=16 << 20),
     )(x, weights)
 
 
@@ -554,13 +588,13 @@
     up = up_weight.astype(jnp.float32)
     down = down_weight.astype(jnp.float32)
 
-    packed = jnp.concatenate(
-        [jnp.transpose(a) for a in (decay_rate, in_coef, out_coef)]
-        + [jnp.transpose(window_state[w]) for w in range(windows)]
-        + [skip_gain[None]],
-        0,
-    )
-    coefs, rounds = gather_all(packed)
+    coefs, rounds = gather_all(
+        pack(
+            [jnp.transpose(a) for a in (decay_rate, in_coef, out_coef)]
+            + [jnp.transpose(window_state[w]) for w in range(windows)]
+            + [skip_gain[None]]
+        )
+    )
     decay, c_in, c_out = (coefs[i * states : (i + 1) * states] for i in range(3))
     carried = lax.dynamic_slice_in_dim(coefs, (3 + window) * states, states, 0)
     skip = coefs[(3 + windows) * states :]
@@ -571,7 +605,7 @@
         return jnp.exp(-decay * steps)
 
     inner = out_own.shape[0]
-    sent = lax.dynamic_slice_in_dim(out_own, core * (inner // 2), inner // 2, 0)
+    sent = pick(out_weight.reshape(2, inner // 2, width), core).astype(jnp.float32)
     across = swap_bit(after(sent, rounds[1]), "mp", 0)
     beside = swap_bit(across, "seq", 0)
     out_far = jnp.where(
@@ -582,10 +616,10 @@
     normed = after(unit1 * norm1_gain + norm1_bias)
     tail = shift_in_window(normed[rows - CTX :], 1, per_window)
     qkv_rows = project(normed, qkv_weight, 0, 3)
-    acc, top, total = by_heads(
+    acc, top = by_heads(
         self_kernel,
         [(qkv_rows, rows, 0, i) for i in range(3)],
-        [(rows,)] * 3,
+        [(rows,)] * 2,
     )
 
     length = float(rows)
@@ -628,7 +662,7 @@
         o, l = by_heads(
             ctx_kernel,
             [(qkv_rows, half, part, 0), (after(kv_ctx, *heads), CTX, 0, 0), (kv_ctx, CTX, 0, 1)]
-            + [(a, half, part) for a in (acc, top, total)],
+            + [(a, half, part) for a in (acc, top)],
             [(half,)] * 2,
             scalars=(ok,),
         )
@@ -734,16 +768,17 @@
     quarter = rows // 4
     result, grad_tokens = unset((rows, width)), unset((rows, width))
 
-    def across(source, k, into, base):
+    def across(source, k, into, base, kept=()):
         span = slice(k * quarter, (k + 1) * quarter)
         got = swap_bit(source[span], "mp", 0)
-        (got,) = turn(attn_ring, down_ring, up_ring, kept=(got,))
-        return lax.dynamic_update_slice(into, base(span) + (source[span] + got), (k * quarter, 0))
+        got, into, *kept = turn(attn_ring, down_ring, up_ring, kept=(got, into, *kept))
+        new = base(span) + (source[span] + got)
+        return [lax.dynamic_update_slice(into, new, (k * quarter, 0)), *kept]
 
     def result_base(span):
         return mixed[span] + down_bias
 
-    result = across(feed, 0, result, result_base)
+    (result,) = across(feed, 0, result, result_base)
 
     sum_q, sum_r, part_h, part_p, part_skip, grad_tail = by_channels(
         tail_back_kernel,
@@ -751,7 +786,7 @@
         [states, states, states, states, 1, CTX],
     )
     clock.set(sum_q)
-    result = across(feed, 1, result, result_base)
+    (result,) = across(feed, 1, result, result_base)
     (sum_p,) = by_channels(moment_kernel, [tail, clock.hold(normed), decay], [states])
     clock.set(sum_p)
     other = swap_bit(jnp.concatenate([sum_p, sum_q], 0), "seq", 0)
@@ -765,7 +800,7 @@
     past_p = jnp.zeros_like(sum_p)
     later = jnp.zeros_like(sum_q)
     came = [trade_chips(both, d) for d in range(1, chips)]
-    result = across(feed, 2, result, result_base)
+    (result,) = across(feed, 2, result, result_base)
     came[0] = clock.hold(came[0])
     for d in range(1, chips):
         there = chip ^ d
@@ -784,7 +819,7 @@
     to_last = far_tail + grad_tail
     clock.set(to_last)
     from_next = shift_in_window(to_last, -1, per_window)
-    result = across(feed, 3, result, result_base)
+    (result,) = across(feed, 3, result, result_base)
     along_h = fade * clock.hold(past_h) * sum_q + part_h
     along_p = fade * (past_h * (sum_r + sum_q) + past_p * sum_q) + part_p
     gone = faded(start_t + 1.0)
@@ -800,43 +835,65 @@
     clock.set(part_tokens, part_gain1, part_bias1)
     turn(attn_ring, down_ring, up_ring)
     stacked = jnp.concatenate([part_in, part_out, part_decay, part_skip, part_gain1, part_bias1], 0)
-    for k in range(4):
-        if k == 1:
-            grad_up_bias = jnp.sum(clock.hold(grad_pre), axis=0)
-            grad_down_bias = jnp.sum(clock.hold(cotangent), axis=0)
-            clock.set(grad_up_bias, grad_down_bias)
-        grad_tokens = across(part_tokens, k, grad_tokens, lambda span: grad_mixed[span])
-
-    (stacked_far,) = turn(attn_ring, down_ring, up_ring, kept=(swap_bit(stacked, "mp", 0),))
-    while up_ring.step < 2 * hops or down_ring.step < 2 * hops:
-        turn(attn_ring, down_ring, up_ring)
+    whole = {}
+
+    def gather_done():
+        made = []
+        for ring in (down_ring, up_ring):
+            if ring.step == 2 * hops and ring not in whole:
+                ring.own[0] = clock.hold(ring.own[0])
+                whole[ring] = ring.results()[0]
+                made.append(ring)
+        return made
+
+    def tokens_turn(k, grad_tokens, *kept):
+        made = gather_done()
+        kept = [*kept, *[whole[ring] for ring in made]]
+        if k < 4:
+            grad_tokens, *kept = across(
+                part_tokens, k, grad_tokens, lambda span: grad_mixed[span], kept
+            )
+        else:
+            grad_tokens, *kept = turn(
+                attn_ring, down_ring, up_ring, kept=(grad_tokens, *kept)
+            )
+        for ring, out in zip(made, kept[len(kept) - len(made) :]):
+            whole[ring] = out
+        return [grad_tokens, *kept[: len(kept) - len(made)]]
+
+    grad_tokens, stacked_far, result = tokens_turn(
+        0, grad_tokens, swap_bit(stacked, "mp", 0), result
+    )
+    grad_up_bias = jnp.sum(clock.hold(grad_pre), axis=0)
+    grad_down_bias = jnp.sum(clock.hold(cotangent), axis=0)
     ups = grad_up_bias.reshape(-1, width)
     small = jnp.concatenate(
         [stacked + stacked_far, jnp.stack([gain2, bias2, grad_down_bias]), ups], 0
     )
-    todo = [down_ring, up_ring]
-    whole = {}
-    for bit in range(bits_of(lax.axis_size("seq"))):
-        other = swap_bit(small, "seq", bit)
-        kept = [other]
-        if todo:
-            ring = todo.pop(0)
-            ring.own[0] = clock.hold(ring.own[0])
-            whole[ring] = len(kept)
-            kept.append(ring.results()[0])
-        if attn_ring.step < 2 * hops:
-            other, *made = turn(attn_ring, kept=kept)
-        else:
-            other, *made = kept
-        for ring, at in list(whole.items()):
-            if isinstance(at, int):
-                whole[ring] = made[at - 1]
-        small = small + other
+    thin = attn_ring.rows
+    extra = -(-small.shape[0] * width // (2 * thin * inner))
+    side = extra * thin * inner // width
+    small = jnp.pad(small, ((0, 2 * side - small.shape[0]), (0, 0)))
+    small = small + swap_bit(small, "seq", 0)
+    small = lax.dynamic_slice_in_dim(small, core * side, side, 0)
+    turns = 1
+    while attn_ring.step < hops:
+        (grad_tokens,) = tokens_turn(turns, grad_tokens)
+        turns += 1
+    attn_ring.take(small.reshape(extra, thin, inner))
     while attn_ring.step < 2 * hops:
-        turn(attn_ring)
+        (grad_tokens,) = tokens_turn(turns, grad_tokens)
+        turns += 1
+    gather_done()
     grad_down, grad_up = whole[down_ring][0], whole[up_ring][0]
+    small = attn_ring.extra_sum().reshape(side, width)
+    other = swap_bit(small, "seq", 0)
+    attn_ring.own[0] = after(attn_ring.own[0], small)
     grad_qkv, grad_out = attn_ring.results()
     grad_out = jnp.transpose(grad_out[0])
+    small = jnp.where(
+        core == 0, jnp.concatenate([small, other], 0), jnp.concatenate([other, small], 0)
+    )
 
     channels = in_coef.shape[0]
     at = (place_seq * lax.axis_size("mp") + lax.axis_index("mp")) * channels
@@ -860,7 +917,7 @@
         small[2],
         small[3],
         grad_up,
-        small[5:].reshape(-1),
+        small[5 : 5 + ups.shape[0]].reshape(-1),
         grad_down,
         small[4],
     )

time: 535 us -> 522 us (0.976)
  other arithmetic: 77.9 us -> 62.1 us
  local copies, waits for them, and re-layouts: 44.1 us -> 52 us
  starting transfers between devices: 99.7 us -> 92.9 us
  matrix products: 70.6 us -> 76.5 us
    unnamed x234 -> x292, local copies, waits for them, and re-layouts: 30.5 us -> 38.2 us
    pallas_call x6, Pallas kernels: 32.1 us -> 25.8 us  [by_channels(): pl.pallas_call(kernel, grid=(width // cut,), in_specs=[spec(a.shape[0]) f...]
    dot_general x26, matrix products: 70.6 us -> 76.5 us  [mm(): lax.dot_general(left, right, (dims, ((), ())), precision=HIGH, preferred_...]
    ppermute x56 -> x54, waiting for transfers between devices: 63.8 us -> 61.7 us  [swap_bit(): return lax.ppermute(value, axis, [(i, i ^ 1 << bit) for i in range(size)])]
    ppermute x56 -> x54, starting transfers between devices: 36.6 us -> 34.7 us  [swap_bit(): return lax.ppermute(value, axis, [(i, i ^ 1 << bit) for i in range(size)])]
    dynamic_update_slice x7 -> x8, other arithmetic: 11.2 us -> 11.4 us  [across(): return [lax.dynamic_update_slice(into, new, (k * quarter, 0)), *kept]]
  transfers between devices with their start and end apart: 106 -> 104, of which waited for: 32 -> 32; matrix products, arithmetic and copies ran while one was open for 26% -> 25% of each run, Pallas kernels for 13% -> 13%
where the time goes in v5:
time: 522 us; the launch traced here: 515 us
  waiting for transfers between devices  150 us (29%)
  starting transfers between devices  92.9 us (18%)
  Pallas kernels  76.5 us (15%)
  matrix products  76.5 us (15%)
  other arithmetic  62.1 us (12%)
  local copies, waits for them, and re-layouts  52 us (10%)
    ppermute x42, waiting for transfers between devices, turn(): got = lax.ppermute(self.held, 'seq', self.route)  88.4 us
    dot_general x26, matrix products, mm(): lax.dot_general(left, right, (dims, ((), ())), precision=HIGH, preferred_...  76.5 us
    ppermute x54, waiting for transfers between devices, swap_bit(): return lax.ppermute(value, axis, [(i, i ^ 1 << bit) for i in range(size)])  61.7 us
    ppermute x42, starting transfers between devices, turn(): got = lax.ppermute(self.held, 'seq', self.route)  41.1 us
    unnamed x292, local copies, waits for them, and re-layouts  38.2 us
    ppermute x54, starting transfers between devices, swap_bit(): return lax.ppermute(value, axis, [(i, i ^ 1 << bit) for i in range(size)])  34.7 us
    pallas_call x6, Pallas kernels, by_channels(): pl.pallas_call(kernel, grid=(width // cut,), in_specs=[spec(a.shape[0]) f...  25.8 us
    pallas_call x4, Pallas kernels, by_heads(): pl.pallas_call(kernel, grid=(heads,), in_specs=specs, out_specs=[pl.Block...  24.5 us
  transfers between devices with their start and end apart: 104, of which 32 were waited for; matrix products, arithmetic and copies ran while one was open for 25% of the time, Pallas kernels for 13%

profile of v5, /device:TPU:0, one launch (start us, length us, event | category | flops | bytes accessed | tf_op | source)
XLA Modules:
  0.0 514.7 jit_solution(2226635817935696286)
XLA Ops:
  32.7 6.0 %shard_map.317 = (f32[512,512]{1,0:T(8,128)S(1)}, f32[512,512]{1,0:T(8,128)S(1)}) custom-call(f32[3,512,512]{2,1,0:T(8,128)S(1)} %shard_map.316.q_ref.k_ref.v_ref, f32[3,512,512]{2,1,0:T(8,128)S(1)} %shard_map.316.q_ref.k_ref.v_ref, f32[3,512,512]{2,1,0:T(8,128)S(1)} %shard_map.316.q_ref.k_ref.v_ref), custom_call_target="tpu_custom_call" | custom-call | bytes 1024 | tf_op jit(solution)/shard_map/pallas_call | solution.py:511
  44.1 4.1 shard_map.319
  52.5 6.7 %collective-permute-start.7 = (f32[16,1024]{1,0:T(8,128)}, f32[16,1024]{1,0:T(8,128)S(1)}, u32[]{:S(2)}, u32[]{:S(2)}) collective-permute-start(f32[16,1024]{1,0:T(8,128)} %get-tuple-element.329), channel_id=1, source_target_pairs={{0,4},{2,6},{4,0},{6,2},{8,12},{10,14},{12,8},{14,10},{16,20},{18,... | collective-permute-start | bytes 196616 | tf_op jit(solution)/shard_map/ppermute | solution.py:77
  91.6 4.6 fusion.104
  112.6 5.1 fusion.15
  123.4 5.9 %fusion.13 = f32[1024,1024]{1,0:T(8,128)S(1)} fusion(f32[512,1024]{1,0:T(8,128)} %param.36, f32[512,2048]{1,0:T(8,128)} %copy-done.16, s32[]{:T(128)S(6)} %select_n.574), kind=kOutput, calls=%fused_computation.26 | convolution fusion | flops 3221225472 | bytes 8388612 | tf_op jit(solution)/shard_map/dot_general | solution.py:20
  136.9 10.5 %collective-permute-done.16 = f32[256,1024]{1,0:T(8,128)S(1)} collective-permute-done((f32[256,1024]{1,0:T(8,128)}, f32[256,1024]{1,0:T(8,128)S(1)}, u32[]{:S(2)}, u32[]{:S(2)}) %collective-permute-start.16) | collective-permute-done | bytes 1048608 | tf_op jit(solution)/shard_map/ppermute | solution.py:40
  154.0 5.2 %fusion.46 = f32[512,2048]{1,0:T(8,128)} fusion(f32[512,2048]{1,0:T(8,128)S(1)} %copy-done.3, f32[512,1024]{1,0:T(8,128)S(1)} %get-tuple-element.164, s32[]{:T(128)S(6)} %select_n.582), kind=kOutput, calls=%fused_computation.80 | convolution fusion | flops 3221225472 | bytes 9437188 | tf_op jit(solution)/shard_map/dot_general | solution.py:20
  162.1 6.6 %collective-permute-done.17 = f32[1,128,1024]{2,1,0:T(8,128)} collective-permute-done((f32[1,128,1024]{2,1,0:T(8,128)}, f32[1,128,1024]{2,1,0:T(8,128)}, u32[]{:S(2)}, u32[]{:S(2)}) %collective-permute-start.17) | collective-permute-done | bytes 524320 | tf_op jit(solution)/shard_map/ppermute | solution.py:193
  171.7 6.8 %convolution_add_fusion = f32[512,2048]{1,0:T(8,128)S(1)} fusion(f32[512,2048]{1,0:T(8,128)} %collective-permute-done.18, f32[512,2048]{1,0:T(8,128)} %copy-done.2, f32[512,1024]{1,0:T(8,128)S(1)} %copy-done.24, s32[]{:T(128)S(6)} %select_n.585), kind=kOutput, calls=%fused_computation | convolution fusion | flops 3222274048 | bytes 13631492 | tf_op jit(solution)/shard_map/dot_general | solution.py:20
  178.7 7.6 %collective-permute-done.21 = f32[256,1024]{1,0:T(8,128)} collective-permute-done((f32[256,1024]{1,0:T(8,128)}, f32[256,1024]{1,0:T(8,128)}, u32[]{:S(2)}, u32[]{:S(2)}) %collective-permute-start.21) | collective-permute-done | bytes 1048608 | tf_op jit(solution)/shard_map/ppermute | solution.py:40
  206.5 11.4 %shard_map.328 = f32[3,640,512]{2,1,0:T(8,128)S(1)} custom-call(s32[1]{0:T(128)} %bitcast.ok_ref, f32[3,512,512]{2,1,0:T(8,128)S(1)} %shard_map.316.q_ref.k_ref.v_ref, f32[3,512,512]{2,1,0:T(8,128)S(1)} %shard_map.316.q_ref.k_ref.v_ref, f32[3,512,512]{2,1,0:T(8,128)S(1)} %shard_map.316.q_ref.k_ref.v_ref, f32[2,128,512]{2,1,0:T(8,128)S(1)} %copy-done.13, ...), custom_call_target="tpu_custom_call" | custom-call | bytes 1024 | tf_op jit(solution)/shard_map/pallas_call | solution.py:511
  234.2 4.3 collective-permute-done.25
  257.8 4.5 fusion.107
  267.3 5.5 %collective-permute-done.33 = f32[1,64,2048]{2,1,0:T(8,128)S(1)} collective-permute-done((f32[1,64,2048]{2,1,0:T(8,128)S(1)}, f32[1,64,2048]{2,1,0:T(8,128)S(1)}, u32[]{:S(2)}, u32[]{:S(2)}) %collective-permute-start.33) | collective-permute-done | bytes 524320 | tf_op jit(solution)/shard_map/ppermute | solution.py:193
  297.2 6.8 %shard_map.330 = (f32[16,1024]{1,0:T(8,128)S(1)}, f32[16,1024]{1,0:T(8,128)S(1)}, f32[16,1024]{1,0:T(8,128)S(1)}, f32[16,1024]{1,0:T(8,128)S(1)}, f32[1,1024]{1,0:T(1,128)S(1)}, /*index=5*/f32[128,1024]{1,0:T(8,128)S(1)}) custom-call(f32[128,1024]{1,0:T(8,128)} %collective-permute-done.tail_ref.x_ref, f32[128,1024]{1,0:T(8,128)S(1)} %slice_select_fusion.d_ref, ...), custom_call_target="tpu_custom_call" | custom-call | bytes 1024 | tf_op jit(solution)/shard_map/pallas_call | solution.py:405
  310.9 6.8 %shard_map.331 = f32[16,1024]{1,0:T(8,128)S(1)} custom-call(f32[128,1024]{1,0:T(8,128)} %collective-permute-done.tail_ref.x_ref, f32[512,1024]{1,0:T(8,128)S(1)} %copy-done.8, f32[16,1024]{1,0:T(8,128)S(1)} %slice.298.decay_ref), custom_call_target="tpu_custom_call" | custom-call | bytes 1024 | tf_op jit(solution)/shard_map/pallas_call | solution.py:405
  325.2 8.9 %collective-permute-done.45 = f32[128,1024]{1,0:T(8,128)S(1)} collective-permute-done((f32[128,1024]{1,0:T(8,128)S(1)}, f32[128,1024]{1,0:T(8,128)S(1)}, u32[]{:S(2)}, u32[]{:S(2)}) %collective-permute-start.45) | collective-permute-done | bytes 524320 | tf_op jit(solution)/shard_map/ppermute | solution.py:40
  349.5 5.0 collective-permute-done.49.refs_2_
  357.3 8.5 %collective-permute-done.58 = f32[4,64,512]{2,1,0:T(8,128)S(1)} collective-permute-done((f32[4,64,512]{2,1,0:T(8,128)S(1)}, f32[4,64,512]{2,1,0:T(8,128)S(1)}, u32[]{:S(2)}, u32[]{:S(2)}) %collective-permute-start.58) | collective-permute-done | bytes 524320 | tf_op jit(solution)/shard_map/ppermute | solution.py:193
  366.7 4.8 collective-permute-done.57.refs_6_
  378.1 4.6 collective-permute-done.64
  382.7 5.6 %collective-permute-done.63.refs_7_ = f32[1,128,1024]{2,1,0:T(8,128)} collective-permute-done((f32[1,128,1024]{2,1,0:T(8,128)}, f32[1,128,1024]{2,1,0:T(8,128)}, u32[]{:S(2)}, u32[]{:S(2)}) %collective-permute-start.63) | collective-permute-done | bytes 524320 | tf_op jit(solution)/shard_map/ppermute | solution.py:193
  409.0 6.8 %shard_map.334 = f32[1,2,8,128,1024]{4,3,2,1,0:T(8,128)} custom-call(s32[2,16]{1,0:T(2,128)} %pad_add_fusion.where_ref, f32[1,128,1024]{2,1,0:T(8,128)} %add_add_fusion.1.refs_0_, f32[1,128,1024]{2,1,0:T(8,128)} %collective-permute-done.34.refs_1_, f32[1,128,1024]{2,1,0:T(8,128)} %collective-permute-done.38.refs_2_, ...), custom_call_target="tpu_custom_call" | custom-call | bytes 1024 | tf_op jit(solution)/shard_map/pallas_call | solution.py:218
  416.2 4.9 collective-permute-done.69
  427.0 9.3 %collective-permute-done.80 = f32[128,1024]{1,0:T(8,128)S(1)} collective-permute-done((f32[128,1024]{1,0:T(8,128)S(1)}, f32[128,1024]{1,0:T(8,128)S(1)}, u32[]{:S(2)}, u32[]{:S(2)}) %collective-permute-start.80) | collective-permute-done | bytes 524320 | tf_op jit(solution)/shard_map/ppermute | solution.py:40
  440.4 9.2 %collective-permute-done.83 = f32[128,1024]{1,0:T(8,128)S(1)} collective-permute-done((f32[128,1024]{1,0:T(8,128)S(1)}, f32[128,1024]{1,0:T(8,128)S(1)}, u32[]{:S(2)}, u32[]{:S(2)}) %collective-permute-start.83) | collective-permute-done | bytes 524320 | tf_op jit(solution)/shard_map/ppermute | solution.py:40
  457.1 6.8 %shard_map.335 = f32[1,2,8,64,2048]{4,3,2,1,0:T(8,128)} custom-call(s32[2,16]{1,0:T(2,128)} %pad_add_fusion.where_ref, f32[1,64,2048]{2,1,0:T(8,128)} %copy-done.65, f32[1,64,2048]{2,1,0:T(8,128)} %copy-done.78, f32[1,64,2048]{2,1,0:T(8,128)} %copy-done.80, f32[1,64,2048]{2,1,0:T(8,128)} %collective-permute-done.56.refs_3_, ...), custom_call_target="tpu_custom_call" | custom-call | bytes 1024 | tf_op jit(solution)/shard_map/pallas_call | solution.py:218
  465.1 9.7 %collective-permute-done.92.refs_5_ = f32[5,64,512]{2,1,0:T(8,128)S(1)} collective-permute-done((f32[5,64,512]{2,1,0:T(8,128)}, f32[5,64,512]{2,1,0:T(8,128)S(1)}, u32[]{:S(2)}, u32[]{:S(2)}) %collective-permute-start.92) | collective-permute-done | bytes 655392 | tf_op jit(solution)/shard_map/ppermute | solution.py:193
  477.7 7.7 %collective-permute-done.93.refs_6_ = f32[5,64,512]{2,1,0:T(8,128)S(1)} collective-permute-done((f32[5,64,512]{2,1,0:T(8,128)S(1)}, f32[5,64,512]{2,1,0:T(8,128)S(1)}, u32[]{:S(2)}, u32[]{:S(2)}) %collective-permute-start.93) | collective-permute-done | bytes 655392 | tf_op jit(solution)/shard_map/ppermute | solution.py:193
  487.3 8.7 %collective-permute-done.94.refs_7_ = f32[5,64,512]{2,1,0:T(8,128)S(1)} collective-permute-done((f32[5,64,512]{2,1,0:T(8,128)S(1)}, f32[5,64,512]{2,1,0:T(8,128)S(1)}, u32[]{:S(2)}, u32[]{:S(2)}) %collective-permute-start.94) | collective-permute-done | bytes 655392 | tf_op jit(solution)/shard_map/ppermute | solution.py:193
  503.9 7.5 %shard_map.336 = (f32[3,2,8,64,512]{4,3,2,1,0:T(8,128)}, f32[1,2,8,64,512]{4,3,2,1,0:T(8,128)}) custom-call(s32[2,16]{1,0:T(2,128)} %pad_add_fusion.where_ref, f32[4,64,512]{2,1,0:T(8,128)} %copy-done.63, f32[5,64,512]{2,1,0:T(8,128)} %collective-permute-done.66.refs_1_, f32[5,64,512]{2,1,0:T(8,128)} %copy-done.68, ...), custom_call_target="tpu_custom_call" | custom-call | bytes 1024 | tf_op jit(solution)/shard_map/pallas_call | solution.py:218
  (642 shorter events, 293.6 us)
Async XLA Ops:
  15.3 27.2 %collective-permute-start = (f32[128,1024]{1,0:T(8,128)}, f32[128,1024]{1,0:T(8,128)}, u32[]{:S(2)}, u32[]{:S(2)}) collective-permute-start(f32[128,1024]{1,0:T(8,128)} %slice.297), channel_id=1, source_target_pairs={{0,2},{2,4},{4,6},{6,8},{8,10},{10,12},{12,14},{16,18},{18,20},{20... | collective-permute-start | bytes 1572872 | tf_op jit(solution)/shard_map/ppermute | solution.py:51
  22.5 18.1 %collective-permute-start.5 = (f32[81,512]{1,0:T(8,128)S(1)}, f32[81,512]{1,0:T(8,128)}, u32[]{:S(2)}, u32[]{:S(2)}) collective-permute-start(f32[81,512]{1,0:T(8,128)S(1)} %maximum_select_fusion.5), channel_id=1, source_target_pairs={{0,16},{2,18},{4,20},{6,22},{8,24},{10,26},{12,28},{14,30},{16,0},... | collective-permute-start | bytes 497672 | tf_op jit(solution)/shard_map/ppermute | solution.py:40
  49.4 39.2 %collective-permute-start.11 = (f32[256,1024]{1,0:T(8,128)}, f32[256,1024]{1,0:T(8,128)}, u32[]{:S(2)}, u32[]{:S(2)}) collective-permute-start(f32[256,1024]{1,0:T(8,128)} %bitcast_convert_fusion), channel_id=1, source_target_pairs={{0,1},{1,0},{2,3},{3,2},{4,5},{5,4},{6,7},{7,6},{8,9},{9,8},{10,11... | collective-permute-start | bytes 3145736 | tf_op jit(solution)/shard_map/ppermute | solution.py:40
  52.5 17.9 %collective-permute-start.7 = (f32[16,1024]{1,0:T(8,128)}, f32[16,1024]{1,0:T(8,128)S(1)}, u32[]{:S(2)}, u32[]{:S(2)}) collective-permute-start(f32[16,1024]{1,0:T(8,128)} %get-tuple-element.329), channel_id=1, source_target_pairs={{0,4},{2,6},{4,0},{6,2},{8,12},{10,14},{12,8},{14,10},{16,20},{18,... | collective-permute-start | bytes 196616 | tf_op jit(solution)/shard_map/ppermute | solution.py:77
  84.4 22.2 %collective-permute-start.13 = (f32[256,512]{1,0:T(8,128)S(1)}, f32[256,512]{1,0:T(8,128)S(1)}, u32[]{:S(2)}, u32[]{:S(2)}) collective-permute-start(f32[256,512]{1,0:T(8,128)S(1)} %get-tuple-element.147), channel_id=1, source_target_pairs={{0,1},{1,0},{2,3},{3,2},{4,5},{5,4},{6,7},{7,6},{8,9},{9,8},{10,11... | collective-permute-start | bytes 1572872 | tf_op jit(solution)/shard_map/ppermute | solution.py:40
  122.0 25.4 %collective-permute-start.16 = (f32[256,1024]{1,0:T(8,128)}, f32[256,1024]{1,0:T(8,128)S(1)}, u32[]{:S(2)}, u32[]{:S(2)}) collective-permute-start(f32[256,1024]{1,0:T(8,128)} %fusion.97), channel_id=1, source_target_pairs={{0,1},{1,0},{2,3},{3,2},{4,5},{5,4},{6,7},{7,6},{8,9},{9,8},{10,11... | collective-permute-start | bytes 3145736 | tf_op jit(solution)/shard_map/ppermute | solution.py:40
  131.0 16.5 %collective-permute-start.15 = (f32[1,128,1024]{2,1,0:T(8,128)S(1)}, f32[1,128,1024]{2,1,0:T(8,128)S(1)}, u32[]{:S(2)}, u32[]{:S(2)}) collective-permute-start(f32[1,128,1024]{2,1,0:T(8,128)S(1)} %dynamic-slice_add_fusion.7), channel_id=1, source_target_pairs={{0,8},{10,2},{8,16},{18,10},{16,24},{26,18},{24,28},{30,26},{28,20... | collective-permute-start | bytes 1572872 | tf_op jit(solution)/shard_map/ppermute | solution.py:193
  160.7 25.6 %collective-permute-start.21 = (f32[256,1024]{1,0:T(8,128)}, f32[256,1024]{1,0:T(8,128)}, u32[]{:S(2)}, u32[]{:S(2)}) collective-permute-start(f32[256,1024]{1,0:T(8,128)} %fusion.11), channel_id=1, source_target_pairs={{0,1},{1,0},{2,3},{3,2},{4,5},{5,4},{6,7},{7,6},{8,9},{9,8},{10,11... | collective-permute-start | bytes 3145736 | tf_op jit(solution)/shard_map/ppermute | solution.py:40
  178.6 21.4 %collective-permute-start.19 = (f32[1,64,2048]{2,1,0:T(8,128)S(1)}, f32[1,64,2048]{2,1,0:T(8,128)S(1)}, u32[]{:S(2)}, u32[]{:S(2)}) collective-permute-start(f32[1,64,2048]{2,1,0:T(8,128)S(1)} %constant_dynamic-slice_fusion.29), channel_id=1, source_target_pairs={{0,8},{10,2},{8,16},{18,10},{16,24},{26,18},{24,28},{30,26},{28,20... | collective-permute-start | bytes 1572872 | tf_op jit(solution)/shard_map/ppermute | solution.py:193
  199.2 18.7 %collective-permute-start.24 = (f32[1,128,1024]{2,1,0:T(8,128)}, f32[1,128,1024]{2,1,0:T(8,128)}, u32[]{:S(2)}, u32[]{:S(2)}) collective-permute-start(f32[1,128,1024]{2,1,0:T(8,128)} %add_add_fusion.4), channel_id=1, source_target_pairs={{0,8},{10,2},{8,16},{18,10},{16,24},{26,18},{24,28},{30,26},{28,20... | collective-permute-start | bytes 1572872 | tf_op jit(solution)/shard_map/ppermute | solution.py:193
  200.9 18.6 %collective-permute-start.23 = (f32[1,64,2048]{2,1,0:T(8,128)}, f32[1,64,2048]{2,1,0:T(8,128)}, u32[]{:S(2)}, u32[]{:S(2)}) collective-permute-start(f32[1,64,2048]{2,1,0:T(8,128)} %dynamic-slice_add_fusion.6), channel_id=1, source_target_pairs={{0,8},{10,2},{8,16},{18,10},{16,24},{26,18},{24,28},{30,26},{28,20... | collective-permute-start | bytes 1572872 | tf_op jit(solution)/shard_map/ppermute | solution.py:193
  228.4 17.4 %collective-permute-start.31 = (f32[512,512]{1,0:T(8,128)S(1)}, f32[512,512]{1,0:T(8,128)S(1)}, u32[]{:S(2)}, u32[]{:S(2)}) collective-permute-start(f32[512,512]{1,0:T(8,128)S(1)} %fusion.29), channel_id=1, source_target_pairs={{0,2},{2,0},{4,6},{6,4},{8,10},{10,8},{12,14},{14,12},{16,18},{18,... | collective-permute-start | bytes 3145736 | tf_op jit(solution)/shard_map/ppermute | solution.py:40
  240.0 16.8 %collective-permute-start.27 = (f32[1,64,2048]{2,1,0:T(8,128)S(1)}, f32[1,64,2048]{2,1,0:T(8,128)S(1)}, u32[]{:S(2)}, u32[]{:S(2)}) collective-permute-start(f32[1,64,2048]{2,1,0:T(8,128)S(1)} %dynamic-slice_add_fusion.4), channel_id=1, source_target_pairs={{0,8},{10,2},{8,16},{18,10},{16,24},{26,18},{24,28},{30,26},{28,20... | collective-permute-start | bytes 1572872 | tf_op jit(solution)/shard_map/ppermute | solution.py:193
  262.4 24.6 %collective-permute-start.37 = (f32[128,1024]{1,0:T(8,128)S(1)}, f32[128,1024]{1,0:T(8,128)S(1)}, u32[]{:S(2)}, u32[]{:S(2)}) collective-permute-start(f32[128,1024]{1,0:T(8,128)S(1)} %slice.307), channel_id=1, source_target_pairs={{0,1},{1,0},{2,3},{3,2},{4,5},{5,4},{6,7},{7,6},{8,9},{9,8},{10,11... | collective-permute-start | bytes 1572872 | tf_op jit(solution)/shard_map/ppermute | solution.py:40
  264.0 17.5 %collective-permute-start.39 = (f32[4,64,512]{2,1,0:T(8,128)S(1)}, f32[4,64,512]{2,1,0:T(8,128)S(1)}, u32[]{:S(2)}, u32[]{:S(2)}) collective-permute-start(f32[4,64,512]{2,1,0:T(8,128)S(1)} %maximum_add_fusion), channel_id=1, source_target_pairs={{0,8},{10,2},{8,16},{18,10},{16,24},{26,18},{24,28},{30,26},{28,20... | collective-permute-start | bytes 1572872 | tf_op jit(solution)/shard_map/ppermute | solution.py:193
  282.4 21.6 %collective-permute-start.43 = (f32[4,64,512]{2,1,0:T(8,128)}, f32[4,64,512]{2,1,0:T(8,128)}, u32[]{:S(2)}, u32[]{:S(2)}) collective-permute-start(f32[4,64,512]{2,1,0:T(8,128)} %maximum_add_fusion.1), channel_id=1, source_target_pairs={{0,8},{10,2},{8,16},{18,10},{16,24},{26,18},{24,28},{30,26},{28,20... | collective-permute-start | bytes 1572872 | tf_op jit(solution)/shard_map/ppermute | solution.py:193
  285.7 20.1 %collective-permute-start.42 = (f32[1,128,1024]{2,1,0:T(8,128)}, f32[1,128,1024]{2,1,0:T(8,128)}, u32[]{:S(2)}, u32[]{:S(2)}) collective-permute-start(f32[1,128,1024]{2,1,0:T(8,128)} %collective-permute-done.38.refs_2_), channel_id=1, source_target_pairs={{0,8},{10,2},{8,16},{18,10},{16,24},{26,18},{24,28},{30,26},{28,20... | collective-permute-start | bytes 1572872 | tf_op jit(solution)/shard_map/ppermute | solution.py:193
  305.2 16.9 %collective-permute-start.47 = (f32[4,64,512]{2,1,0:T(8,128)S(1)}, f32[4,64,512]{2,1,0:T(8,128)S(1)}, u32[]{:S(2)}, u32[]{:S(2)}) collective-permute-start(f32[4,64,512]{2,1,0:T(8,128)S(1)} %maximum_add_fusion.2), channel_id=1, source_target_pairs={{0,8},{10,2},{8,16},{18,10},{16,24},{26,18},{24,28},{30,26},{28,20... | collective-permute-start | bytes 1572872 | tf_op jit(solution)/shard_map/ppermute | solution.py:193
  305.8 16.7 %collective-permute-start.46 = (f32[1,128,1024]{2,1,0:T(8,128)}, f32[1,128,1024]{2,1,0:T(8,128)S(1)}, u32[]{:S(2)}, u32[]{:S(2)}) collective-permute-start(f32[1,128,1024]{2,1,0:T(8,128)} %collective-permute-done.42.refs_3_), channel_id=1, source_target_pairs={{0,8},{10,2},{8,16},{18,10},{16,24},{26,18},{24,28},{30,26},{28,20... | collective-permute-start | bytes 1572872 | tf_op jit(solution)/shard_map/ppermute | solution.py:193
  309.4 25.3 %collective-permute-start.44 = (f32[1,64,2048]{2,1,0:T(8,128)S(1)}, f32[1,64,2048]{2,1,0:T(8,128)S(1)}, u32[]{:S(2)}, u32[]{:S(2)}) collective-permute-start(f32[1,64,2048]{2,1,0:T(8,128)S(1)} %dynamic-slice_add_fusion.refs_0_), channel_id=1, source_target_pairs={{0,8},{10,2},{8,16},{18,10},{16,24},{26,18},{24,28},{30,26},{28,20... | collective-permute-start | bytes 1572872 | tf_op jit(solution)/shard_map/ppermute | solution.py:193
  336.9 17.7 %collective-permute-start.49 = (f32[1,64,2048]{2,1,0:T(8,128)S(1)}, f32[1,64,2048]{2,1,0:T(8,128)S(1)}, u32[]{:S(2)}, u32[]{:S(2)}) collective-permute-start(f32[1,64,2048]{2,1,0:T(8,128)S(1)} %collective-permute-done.44.refs_1_), channel_id=1, source_target_pairs={{0,8},{10,2},{8,16},{18,10},{16,24},{26,18},{24,28},{30,26},{28,20... | collective-permute-start | bytes 1572872 | tf_op jit(solution)/shard_map/ppermute | solution.py:193
  345.3 20.5 %collective-permute-start.58 = (f32[4,64,512]{2,1,0:T(8,128)S(1)}, f32[4,64,512]{2,1,0:T(8,128)S(1)}, u32[]{:S(2)}, u32[]{:S(2)}) collective-permute-start(f32[4,64,512]{2,1,0:T(8,128)S(1)} %maximum_add_fusion.4), channel_id=1, source_target_pairs={{0,8},{10,2},{8,16},{18,10},{16,24},{26,18},{24,28},{30,26},{28,20... | collective-permute-start | bytes 1572872 | tf_op jit(solution)/shard_map/ppermute | solution.py:193
  348.9 22.6 %collective-permute-start.57 = (f32[1,128,1024]{2,1,0:T(8,128)S(1)}, f32[1,128,1024]{2,1,0:T(8,128)}, u32[]{:S(2)}, u32[]{:S(2)}) collective-permute-start(f32[1,128,1024]{2,1,0:T(8,128)S(1)} %collective-permute-done.51.refs_5_), channel_id=1, source_target_pairs={{0,8},{10,2},{8,16},{18,10},{16,24},{26,18},{24,28},{30,26},{28,20... | collective-permute-start | bytes 1572872 | tf_op jit(solution)/shard_map/ppermute | solution.py:193
  354.5 22.6 %collective-permute-start.56 = (f32[1,64,2048]{2,1,0:T(8,128)S(1)}, f32[1,64,2048]{2,1,0:T(8,128)}, u32[]{:S(2)}, u32[]{:S(2)}) collective-permute-start(f32[1,64,2048]{2,1,0:T(8,128)S(1)} %collective-permute-done.49.refs_2_), channel_id=1, source_target_pairs={{0,8},{10,2},{8,16},{18,10},{16,24},{26,18},{24,28},{30,26},{28,20... | collective-permute-start | bytes 1572872 | tf_op jit(solution)/shard_map/ppermute | solution.py:193
  371.5 16.9 %collective-permute-start.63 = (f32[1,128,1024]{2,1,0:T(8,128)}, f32[1,128,1024]{2,1,0:T(8,128)}, u32[]{:S(2)}, u32[]{:S(2)}) collective-permute-start(f32[1,128,1024]{2,1,0:T(8,128)} %collective-permute-done.57.refs_6_), channel_id=1, source_target_pairs={{0,8},{10,2},{8,16},{18,10},{16,24},{26,18},{24,28},{30,26},{28,20... | collective-permute-start | bytes 1572872 | tf_op jit(solution)/shard_map/ppermute | solution.py:193
  372.4 26.0 %collective-permute-start.70 = (f32[1,128,1024]{2,1,0:T(8,128)}, f32[1,128,1024]{2,1,0:T(8,128)}, u32[]{:S(2)}, u32[]{:S(2)}) collective-permute-start(f32[1,128,1024]{2,1,0:T(8,128)} %add_add_fusion.1.refs_0_), channel_id=1, source_target_pairs={{0,2},{2,0},{4,6},{6,4},{8,10},{10,8},{12,14},{14,12},{16,18},{18,... | collective-permute-start | bytes 1572872 | tf_op jit(solution)/shard_map/ppermute | solution.py:40
  373.3 21.3 %collective-permute-start.61 = (f32[128,1024]{1,0:T(8,128)}, f32[128,1024]{1,0:T(8,128)}, u32[]{:S(2)}, u32[]{:S(2)}) collective-permute-start(f32[128,1024]{1,0:T(8,128)} %slice.322), channel_id=1, source_target_pairs={{0,1},{1,0},{2,3},{3,2},{4,5},{5,4},{6,7},{7,6},{8,9},{9,8},{10,11... | collective-permute-start | bytes 1572872 | tf_op jit(solution)/shard_map/ppermute | solution.py:40
  377.1 17.4 %collective-permute-start.60 = (f32[1,64,2048]{2,1,0:T(8,128)}, f32[1,64,2048]{2,1,0:T(8,128)}, u32[]{:S(2)}, u32[]{:S(2)}) collective-permute-start(f32[1,64,2048]{2,1,0:T(8,128)} %collective-permute-done.56.refs_3_), channel_id=1, source_target_pairs={{0,8},{10,2},{8,16},{18,10},{16,24},{26,18},{24,28},{30,26},{28,20... | collective-permute-start | bytes 1572872 | tf_op jit(solution)/shard_map/ppermute | solution.py:193
  382.7 19.4 %collective-permute-start.71 = (f32[1,128,1024]{2,1,0:T(8,128)}, f32[1,128,1024]{2,1,0:T(8,128)}, u32[]{:S(2)}, u32[]{:S(2)}) collective-permute-start(f32[1,128,1024]{2,1,0:T(8,128)} %collective-permute-done.34.refs_1_), channel_id=1, source_target_pairs={{0,2},{2,0},{4,6},{6,4},{8,10},{10,8},{12,14},{14,12},{16,18},{18,... | collective-permute-start | bytes 1572872 | tf_op jit(solution)/shard_map/ppermute | solution.py:40
  426.7 22.9 %collective-permute-start.78 = (f32[5,64,512]{2,1,0:T(8,128)S(1)}, f32[5,64,512]{2,1,0:T(8,128)}, u32[]{:S(2)}, u32[]{:S(2)}) collective-permute-start(f32[5,64,512]{2,1,0:T(8,128)S(1)} %collective-permute-done.67.refs_2_), channel_id=1, source_target_pairs={{0,8},{10,2},{8,16},{18,10},{16,24},{26,18},{24,28},{30,26},{28,20... | collective-permute-start | bytes 1966088 | tf_op jit(solution)/shard_map/ppermute | solution.py:193
  465.0 33.9 %collective-permute-start.97 = (f32[5,64,512]{2,1,0:T(8,128)}, f32[5,64,512]{2,1,0:T(8,128)}, u32[]{:S(2)}, u32[]{:S(2)}) collective-permute-start(f32[5,64,512]{2,1,0:T(8,128)} %collective-permute-done.66.refs_1_), channel_id=1, source_target_pairs={{0,2},{2,0},{4,6},{6,4},{8,10},{10,8},{12,14},{14,12},{16,18},{18,... | collective-permute-start | bytes 1966088 | tf_op jit(solution)/shard_map/ppermute | solution.py:40
  476.7 22.3 %collective-permute-start.98 = (f32[5,64,512]{2,1,0:T(8,128)S(1)}, f32[5,64,512]{2,1,0:T(8,128)}, u32[]{:S(2)}, u32[]{:S(2)}) collective-permute-start(f32[5,64,512]{2,1,0:T(8,128)S(1)} %copy-done.69), channel_id=1, source_target_pairs={{0,2},{2,0},{4,6},{6,4},{8,10},{10,8},{12,14},{14,12},{16,18},{18,... | collective-permute-start | bytes 1966088 | tf_op jit(solution)/shard_map/ppermute | solution.py:40
  (213 other events, 1757.0 us)

commit v6 on v5

--- a/solution.py
+++ b/solution.py
@@ -728,7 +728,6 @@
     grad_mixed, gain2, bias2 = norm2_half(0, grad_mixed, gain2, bias2)
     give = mm(core_half(clock.hold(normed2), 1 - core), grad_pre, TN)
     clock.set(give)
-    turn(down_ring)
     keep = mm(core_half(clock.hold(normed2), core), grad_pre, TN) + swap_bit(give, "seq", 0)
     up_ring = Ring([[keep]], (1,))
     clock.set(up_ring.held)
@@ -757,7 +756,6 @@
     keeps.append(mm(core_half(clock.hold(grad_mixed), core), outs, TN) + gots[3])
     attn_ring = Ring([[k] for k in keeps], (3, 1))
     clock.set(attn_ring.held)
-    turn(down_ring, up_ring)
 
     feed = mm(clock.hold(hidden), down)
     clock.set(feed)

time: 522 us -> 513 us (0.983)
  starting transfers between devices: 92.9 us -> 84.1 us
    ppermute x54, waiting for transfers between devices: 61.7 us -> 50.4 us  [swap_bit(): return lax.ppermute(value, axis, [(i, i ^ 1 << bit) for i in range(size)])]
    ppermute x42, waiting for transfers between devices: 88.4 us -> 97.3 us  [turn(): got = lax.ppermute(self.held, 'seq', self.route)]
    ppermute x42, starting transfers between devices: 41.1 us -> 33.1 us  [turn(): got = lax.ppermute(self.held, 'seq', self.route)]
    unnamed x292 -> x260, local copies, waits for them, and re-layouts: 38.2 us -> 38.2 us
  transfers between devices with their start and end apart: 104 -> 104, of which waited for: 32 -> 38; matrix products, arithmetic and copies ran while one was open for 25% -> 26% of each run, Pallas kernels for 13% -> 13%
where the time goes in v6:
time: 513 us; the launch traced here: 506 us
  waiting for transfers between devices  148 us (29%)
  starting transfers between devices  84.1 us (16%)
  matrix products  77.2 us (15%)
  Pallas kernels  76.5 us (15%)
  other arithmetic  64.3 us (13%)
  local copies, waits for them, and re-layouts  51.4 us (10%)
    ppermute x42, waiting for transfers between devices, turn(): got = lax.ppermute(self.held, 'seq', self.route)  97.3 us
    dot_general x26, matrix products, mm(): lax.dot_general(left, right, (dims, ((), ())), precision=HIGH, preferred_...  77.2 us
    ppermute x54, waiting for transfers between devices, swap_bit(): return lax.ppermute(value, axis, [(i, i ^ 1 << bit) for i in range(size)])  50.4 us
    unnamed x260, local copies, waits for them, and re-layouts  38.2 us
    ppermute x54, starting transfers between devices, swap_bit(): return lax.ppermute(value, axis, [(i, i ^ 1 << bit) for i in range(size)])  34.6 us
    ppermute x42, starting transfers between devices, turn(): got = lax.ppermute(self.held, 'seq', self.route)  33.1 us
    pallas_call x6, Pallas kernels, by_channels(): pl.pallas_call(kernel, grid=(width // cut,), in_specs=[spec(a.shape[0]) f...  25.8 us
    pallas_call x4, Pallas kernels, by_heads(): pl.pallas_call(kernel, grid=(heads,), in_specs=specs, out_specs=[pl.Block...  24.5 us
  transfers between devices with their start and end apart: 104, of which 38 were waited for; matrix products, arithmetic and copies ran while one was open for 26% of the time, Pallas kernels for 13%

profile of v6, /device:TPU:0, one launch (start us, length us, event | category | flops | bytes accessed | tf_op | source)
XLA Modules:
  0.0 505.7 jit_solution(2292702727939096126)
XLA Ops:
  33.3 6.0 %shard_map.317 = (f32[512,512]{1,0:T(8,128)S(1)}, f32[512,512]{1,0:T(8,128)S(1)}) custom-call(f32[3,512,512]{2,1,0:T(8,128)S(1)} %shard_map.316.q_ref.k_ref.v_ref, f32[3,512,512]{2,1,0:T(8,128)S(1)} %shard_map.316.q_ref.k_ref.v_ref, f32[3,512,512]{2,1,0:T(8,128)S(1)} %shard_map.316.q_ref.k_ref.v_ref), custom_call_target="tpu_custom_call" | custom-call | bytes 1024 | tf_op jit(solution)/shard_map/pallas_call | solution.py:511
  44.9 4.1 shard_map.319
  53.2 8.0 %collective-permute-start.9 = (f32[16,1024]{1,0:T(8,128)}, f32[16,1024]{1,0:T(8,128)S(1)}, u32[]{:S(2)}, u32[]{:S(2)}) collective-permute-start(f32[16,1024]{1,0:T(8,128)} %get-tuple-element.329), channel_id=1, source_target_pairs={{0,12},{2,14},{4,8},{6,10},{8,4},{10,6},{12,0},{14,2},{16,28},{18,... | collective-permute-start | bytes 196616 | tf_op jit(solution)/shard_map/ppermute | solution.py:77
  91.6 4.6 fusion.104
  102.5 4.0 fusion.97
  112.6 5.1 %fusion.15 = f32[1024,1024]{1,0:T(8,128)} fusion(f32[512,1024]{1,0:T(8,128)S(1)} %copy-done.40, f32[512,2048]{1,0:T(8,128)S(1)} %get-tuple-element.180, s32[]{:T(128)S(6)} %select_n.573), kind=kOutput, calls=%fused_computation.28 | convolution fusion | flops 3221225472 | bytes 8388612 | tf_op jit(solution)/shard_map/dot_general | solution.py:20
  123.3 5.9 %fusion.13 = f32[1024,1024]{1,0:T(8,128)S(1)} fusion(f32[512,1024]{1,0:T(8,128)} %param.36, f32[512,2048]{1,0:T(8,128)} %copy-done.16, s32[]{:T(128)S(6)} %select_n.574), kind=kOutput, calls=%fused_computation.26 | convolution fusion | flops 3221225472 | bytes 8388612 | tf_op jit(solution)/shard_map/dot_general | solution.py:20
  136.9 10.5 %collective-permute-done.16 = f32[256,1024]{1,0:T(8,128)S(1)} collective-permute-done((f32[256,1024]{1,0:T(8,128)}, f32[256,1024]{1,0:T(8,128)S(1)}, u32[]{:S(2)}, u32[]{:S(2)}) %collective-permute-start.16) | collective-permute-done | bytes 1048608 | tf_op jit(solution)/shard_map/ppermute | solution.py:40
  154.0 5.2 %fusion.46 = f32[512,2048]{1,0:T(8,128)} fusion(f32[512,2048]{1,0:T(8,128)S(1)} %copy-done.3, f32[512,1024]{1,0:T(8,128)S(1)} %get-tuple-element.163, s32[]{:T(128)S(6)} %select_n.582), kind=kOutput, calls=%fused_computation.80 | convolution fusion | flops 3221225472 | bytes 9437188 | tf_op jit(solution)/shard_map/dot_general | solution.py:20
  162.0 4.6 collective-permute-done.17
  166.6 7.4 %convolution_add_fusion = f32[512,2048]{1,0:T(8,128)S(1)} fusion(f32[512,2048]{1,0:T(8,128)} %collective-permute-done.17, f32[512,2048]{1,0:T(8,128)} %copy-done.2, f32[512,1024]{1,0:T(8,128)} %copy-done.22, s32[]{:T(128)S(6)} %select_n.583), kind=kOutput, calls=%fused_computation | convolution fusion | flops 3222274048 | bytes 13631492 | tf_op jit(solution)/shard_map/dot_general | solution.py:20
  175.6 9.4 %collective-permute-done.20 = f32[256,1024]{1,0:T(8,128)} collective-permute-done((f32[256,1024]{1,0:T(8,128)}, f32[256,1024]{1,0:T(8,128)}, u32[]{:S(2)}, u32[]{:S(2)}) %collective-permute-start.20) | collective-permute-done | bytes 1048608 | tf_op jit(solution)/shard_map/ppermute | solution.py:40
  206.2 11.4 %shard_map.328 = f32[3,640,512]{2,1,0:T(8,128)S(1)} custom-call(s32[1]{0:T(128)} %bitcast.ok_ref, f32[3,512,512]{2,1,0:T(8,128)S(1)} %shard_map.316.q_ref.k_ref.v_ref, f32[3,512,512]{2,1,0:T(8,128)S(1)} %shard_map.316.q_ref.k_ref.v_ref, f32[3,512,512]{2,1,0:T(8,128)S(1)} %shard_map.316.q_ref.k_ref.v_ref, f32[2,128,512]{2,1,0:T(8,128)S(1)} %copy-done.13, ...), custom_call_target="tpu_custom_call" | custom-call | bytes 1024 | tf_op jit(solution)/shard_map/pallas_call | solution.py:511
  249.6 4.5 fusion.107
  283.9 6.8 %shard_map.330 = (f32[16,1024]{1,0:T(8,128)S(1)}, f32[16,1024]{1,0:T(8,128)S(1)}, f32[16,1024]{1,0:T(8,128)S(1)}, f32[16,1024]{1,0:T(8,128)S(1)}, f32[1,1024]{1,0:T(1,128)S(1)}, /*index=5*/f32[128,1024]{1,0:T(8,128)S(1)}) custom-call(f32[128,1024]{1,0:T(8,128)} %collective-permute-done.tail_ref.x_ref, f32[128,1024]{1,0:T(8,128)S(1)} %slice_select_fusion.d_ref, ...), custom_call_target="tpu_custom_call" | custom-call | bytes 1024 | tf_op jit(solution)/shard_map/pallas_call | solution.py:405
  297.6 6.8 %shard_map.331 = f32[16,1024]{1,0:T(8,128)S(1)} custom-call(f32[128,1024]{1,0:T(8,128)} %collective-permute-done.tail_ref.x_ref, f32[512,1024]{1,0:T(8,128)S(1)} %copy-done.8, f32[16,1024]{1,0:T(8,128)S(1)} %slice.298.decay_ref), custom_call_target="tpu_custom_call" | custom-call | bytes 1024 | tf_op jit(solution)/shard_map/pallas_call | solution.py:405
  315.7 5.2 %collective-permute-done.42 = f32[128,1024]{1,0:T(8,128)S(1)} collective-permute-done((f32[128,1024]{1,0:T(8,128)S(1)}, f32[128,1024]{1,0:T(8,128)S(1)}, u32[]{:S(2)}, u32[]{:S(2)}) %collective-permute-start.42) | collective-permute-done | bytes 524320 | tf_op jit(solution)/shard_map/ppermute | solution.py:40
  340.4 6.9 %collective-permute-done.55 = f32[4,64,512]{2,1,0:T(8,128)S(1)} collective-permute-done((f32[4,64,512]{2,1,0:T(8,128)S(1)}, f32[4,64,512]{2,1,0:T(8,128)S(1)}, u32[]{:S(2)}, u32[]{:S(2)}) %collective-permute-start.55) | collective-permute-done | bytes 524320 | tf_op jit(solution)/shard_map/ppermute | solution.py:193
  353.0 5.6 %collective-permute-done.53.refs_2_ = f32[1,64,2048]{2,1,0:T(8,128)} collective-permute-done((f32[1,64,2048]{2,1,0:T(8,128)}, f32[1,64,2048]{2,1,0:T(8,128)}, u32[]{:S(2)}, u32[]{:S(2)}) %collective-permute-start.53) | collective-permute-done | bytes 524320 | tf_op jit(solution)/shard_map/ppermute | solution.py:193
  365.5 4.4 collective-permute-done.60.refs_5_
  369.9 5.6 %collective-permute-done.57.refs_3_ = f32[1,64,2048]{2,1,0:T(8,128)} collective-permute-done((f32[1,64,2048]{2,1,0:T(8,128)}, f32[1,64,2048]{2,1,0:T(8,128)}, u32[]{:S(2)}, u32[]{:S(2)}) %collective-permute-start.57) | collective-permute-done | bytes 524320 | tf_op jit(solution)/shard_map/ppermute | solution.py:193
  383.5 7.1 %collective-permute-done.63.refs_1_ = f32[5,64,512]{2,1,0:T(8,128)S(1)} collective-permute-done((f32[5,64,512]{2,1,0:T(8,128)S(1)}, f32[5,64,512]{2,1,0:T(8,128)S(1)}, u32[]{:S(2)}, u32[]{:S(2)}) %collective-permute-start.63) | collective-permute-done | bytes 655392 | tf_op jit(solution)/shard_map/ppermute | solution.py:193
  391.4 10.5 %collective-permute-done.67.refs_6_ = f32[1,128,1024]{2,1,0:T(8,128)} collective-permute-done((f32[1,128,1024]{2,1,0:T(8,128)}, f32[1,128,1024]{2,1,0:T(8,128)}, u32[]{:S(2)}, u32[]{:S(2)}) %collective-permute-start.67) | collective-permute-done | bytes 524320 | tf_op jit(solution)/shard_map/ppermute | solution.py:193
  409.0 5.6 %collective-permute-done.69.refs_5_ = f32[1,64,2048]{2,1,0:T(8,128)} collective-permute-done((f32[1,64,2048]{2,1,0:T(8,128)}, f32[1,64,2048]{2,1,0:T(8,128)}, u32[]{:S(2)}, u32[]{:S(2)}) %collective-permute-start.69) | collective-permute-done | bytes 524320 | tf_op jit(solution)/shard_map/ppermute | solution.py:193
  423.1 4.1 collective-permute-done.68.refs_3_
  429.3 6.9 %shard_map.334 = f32[1,2,8,128,1024]{4,3,2,1,0:T(8,128)} custom-call(s32[2,16]{1,0:T(2,128)} %pad_add_fusion.where_ref, f32[1,128,1024]{2,1,0:T(8,128)} %add_add_fusion.1.refs_0_, f32[1,128,1024]{2,1,0:T(8,128)} %collective-permute-done.39.refs_1_, f32[1,128,1024]{2,1,0:T(8,128)} %collective-permute-done.43.refs_2_, ...), custom_call_target="tpu_custom_call" | custom-call | bytes 1024 | tf_op jit(solution)/shard_map/pallas_call | solution.py:218
  436.2 4.4 collective-permute-done.74
  441.7 8.5 %collective-permute-done.84.refs_7_ = f32[1,64,2048]{2,1,0:T(8,128)} collective-permute-done((f32[1,64,2048]{2,1,0:T(8,128)}, f32[1,64,2048]{2,1,0:T(8,128)}, u32[]{:S(2)}, u32[]{:S(2)}) %collective-permute-start.84) | collective-permute-done | bytes 524320 | tf_op jit(solution)/shard_map/ppermute | solution.py:193
  457.5 6.8 %shard_map.335 = f32[1,2,8,64,2048]{4,3,2,1,0:T(8,128)} custom-call(s32[2,16]{1,0:T(2,128)} %pad_add_fusion.where_ref, f32[1,64,2048]{2,1,0:T(8,128)} %copy-done.65, f32[1,64,2048]{2,1,0:T(8,128)} %collective-permute-done.46.refs_1_, f32[1,64,2048]{2,1,0:T(8,128)} %collective-permute-done.53.refs_2_, f32[1,64,2048]{2,1,0:T(8,128)} %collective-permute-done.57.refs_3_, ...), custom_call_target="tpu_custom_call" | custom-call | bytes 1024 | tf_op jit(solution)/shard_map/pallas_call | solution.py:218
  468.2 7.0 %collective-permute-done.93.refs_6_ = f32[5,64,512]{2,1,0:T(8,128)S(1)} collective-permute-done((f32[5,64,512]{2,1,0:T(8,128)}, f32[5,64,512]{2,1,0:T(8,128)S(1)}, u32[]{:S(2)}, u32[]{:S(2)}) %collective-permute-start.93) | collective-permute-done | bytes 655392 | tf_op jit(solution)/shard_map/ppermute | solution.py:193
  477.2 8.6 %collective-permute-done.94.refs_7_ = f32[5,64,512]{2,1,0:T(8,128)S(1)} collective-permute-done((f32[5,64,512]{2,1,0:T(8,128)S(1)}, f32[5,64,512]{2,1,0:T(8,128)S(1)}, u32[]{:S(2)}, u32[]{:S(2)}) %collective-permute-start.94) | collective-permute-done | bytes 655392 | tf_op jit(solution)/shard_map/ppermute | solution.py:193
  494.9 7.5 %shard_map.336 = (f32[3,2,8,64,512]{4,3,2,1,0:T(8,128)}, f32[1,2,8,64,512]{4,3,2,1,0:T(8,128)}) custom-call(s32[2,16]{1,0:T(2,128)} %pad_add_fusion.where_ref, f32[4,64,512]{2,1,0:T(8,128)} %copy-done.64, f32[5,64,512]{2,1,0:T(8,128)} %copy-done.68, f32[5,64,512]{2,1,0:T(8,128)} %copy-done.69, f32[5,64,512]{2,1,0:T(8,128)} %collective-permute-done.68.refs_3_, ...), custom_call_target="tpu_custom_call" | custom-call | bytes 1024 | tf_op jit(solution)/shard_map/pallas_call | solution.py:218
  (610 shorter events, 292.3 us)
Async XLA Ops:
  15.3 27.9 %collective-permute-start = (f32[128,1024]{1,0:T(8,128)}, f32[128,1024]{1,0:T(8,128)}, u32[]{:S(2)}, u32[]{:S(2)}) collective-permute-start(f32[128,1024]{1,0:T(8,128)} %slice.297), channel_id=1, source_target_pairs={{0,2},{2,4},{4,6},{6,8},{8,10},{10,12},{12,14},{16,18},{18,20},{20... | collective-permute-start | bytes 1572872 | tf_op jit(solution)/shard_map/ppermute | solution.py:51
  23.2 18.1 %collective-permute-start.5 = (f32[81,512]{1,0:T(8,128)}, f32[81,512]{1,0:T(8,128)}, u32[]{:S(2)}, u32[]{:S(2)}) collective-permute-start(f32[81,512]{1,0:T(8,128)} %maximum_select_fusion.5), channel_id=1, source_target_pairs={{0,16},{2,18},{4,20},{6,22},{8,24},{10,26},{12,28},{14,30},{16,0},... | collective-permute-start | bytes 497672 | tf_op jit(solution)/shard_map/ppermute | solution.py:40
  50.2 38.3 %collective-permute-start.11 = (f32[256,1024]{1,0:T(8,128)}, f32[256,1024]{1,0:T(8,128)}, u32[]{:S(2)}, u32[]{:S(2)}) collective-permute-start(f32[256,1024]{1,0:T(8,128)} %bitcast_convert_fusion), channel_id=1, source_target_pairs={{0,1},{1,0},{2,3},{3,2},{4,5},{5,4},{6,7},{7,6},{8,9},{9,8},{10,11... | collective-permute-start | bytes 3145736 | tf_op jit(solution)/shard_map/ppermute | solution.py:40
  53.2 17.1 %collective-permute-start.9 = (f32[16,1024]{1,0:T(8,128)}, f32[16,1024]{1,0:T(8,128)S(1)}, u32[]{:S(2)}, u32[]{:S(2)}) collective-permute-start(f32[16,1024]{1,0:T(8,128)} %get-tuple-element.329), channel_id=1, source_target_pairs={{0,12},{2,14},{4,8},{6,10},{8,4},{10,6},{12,0},{14,2},{16,28},{18,... | collective-permute-start | bytes 196616 | tf_op jit(solution)/shard_map/ppermute | solution.py:77
  84.3 22.2 %collective-permute-start.13 = (f32[256,512]{1,0:T(8,128)S(1)}, f32[256,512]{1,0:T(8,128)S(1)}, u32[]{:S(2)}, u32[]{:S(2)}) collective-permute-start(f32[256,512]{1,0:T(8,128)S(1)} %get-tuple-element.147), channel_id=1, source_target_pairs={{0,1},{1,0},{2,3},{3,2},{4,5},{5,4},{6,7},{7,6},{8,9},{9,8},{10,11... | collective-permute-start | bytes 1572872 | tf_op jit(solution)/shard_map/ppermute | solution.py:40
  121.9 25.5 %collective-permute-start.16 = (f32[256,1024]{1,0:T(8,128)}, f32[256,1024]{1,0:T(8,128)S(1)}, u32[]{:S(2)}, u32[]{:S(2)}) collective-permute-start(f32[256,1024]{1,0:T(8,128)} %fusion.97), channel_id=1, source_target_pairs={{0,1},{1,0},{2,3},{3,2},{4,5},{5,4},{6,7},{7,6},{8,9},{9,8},{10,11... | collective-permute-start | bytes 3145736 | tf_op jit(solution)/shard_map/ppermute | solution.py:40
  159.1 25.9 %collective-permute-start.20 = (f32[256,1024]{1,0:T(8,128)}, f32[256,1024]{1,0:T(8,128)}, u32[]{:S(2)}, u32[]{:S(2)}) collective-permute-start(f32[256,1024]{1,0:T(8,128)} %fusion.11), channel_id=1, source_target_pairs={{0,1},{1,0},{2,3},{3,2},{4,5},{5,4},{6,7},{7,6},{8,9},{9,8},{10,11... | collective-permute-start | bytes 3145736 | tf_op jit(solution)/shard_map/ppermute | solution.py:40
  160.5 24.5 %collective-permute-start.19 = (f32[1,128,1024]{2,1,0:T(8,128)}, f32[1,128,1024]{2,1,0:T(8,128)S(1)}, u32[]{:S(2)}, u32[]{:S(2)}) collective-permute-start(f32[1,128,1024]{2,1,0:T(8,128)} %add_add_fusion.7), channel_id=1, source_target_pairs={{0,8},{10,2},{8,16},{18,10},{16,24},{26,18},{24,28},{30,26},{28,20... | collective-permute-start | bytes 1572872 | tf_op jit(solution)/shard_map/ppermute | solution.py:193
  174.1 25.4 %collective-permute-start.18 = (f32[1,64,2048]{2,1,0:T(8,128)S(1)}, f32[1,64,2048]{2,1,0:T(8,128)S(1)}, u32[]{:S(2)}, u32[]{:S(2)}) collective-permute-start(f32[1,64,2048]{2,1,0:T(8,128)S(1)} %constant_dynamic-slice_fusion.29), channel_id=1, source_target_pairs={{0,8},{10,2},{8,16},{18,10},{16,24},{26,18},{24,28},{30,26},{28,20... | collective-permute-start | bytes 1572872 | tf_op jit(solution)/shard_map/ppermute | solution.py:193
  199.2 18.4 %collective-permute-start.23 = (f32[1,128,1024]{2,1,0:T(8,128)}, f32[1,128,1024]{2,1,0:T(8,128)}, u32[]{:S(2)}, u32[]{:S(2)}) collective-permute-start(f32[1,128,1024]{2,1,0:T(8,128)} %add_add_fusion.5), channel_id=1, source_target_pairs={{0,8},{10,2},{8,16},{18,10},{16,24},{26,18},{24,28},{30,26},{28,20... | collective-permute-start | bytes 1572872 | tf_op jit(solution)/shard_map/ppermute | solution.py:193
  200.4 20.7 %collective-permute-start.22 = (f32[1,64,2048]{2,1,0:T(8,128)}, f32[1,64,2048]{2,1,0:T(8,128)}, u32[]{:S(2)}, u32[]{:S(2)}) collective-permute-start(f32[1,64,2048]{2,1,0:T(8,128)} %dynamic-slice_add_fusion.6), channel_id=1, source_target_pairs={{0,8},{10,2},{8,16},{18,10},{16,24},{26,18},{24,28},{30,26},{28,20... | collective-permute-start | bytes 1572872 | tf_op jit(solution)/shard_map/ppermute | solution.py:193
  234.0 26.6 %collective-permute-start.26 = (f32[1,64,2048]{2,1,0:T(8,128)S(1)}, f32[1,64,2048]{2,1,0:T(8,128)S(1)}, u32[]{:S(2)}, u32[]{:S(2)}) collective-permute-start(f32[1,64,2048]{2,1,0:T(8,128)S(1)} %dynamic-slice_add_fusion.4), channel_id=1, source_target_pairs={{0,8},{10,2},{8,16},{18,10},{16,24},{26,18},{24,28},{30,26},{28,20... | collective-permute-start | bytes 1572872 | tf_op jit(solution)/shard_map/ppermute | solution.py:193
  236.1 22.8 %collective-permute-start.27 = (f32[1,128,1024]{2,1,0:T(8,128)S(1)}, f32[1,128,1024]{2,1,0:T(8,128)S(1)}, u32[]{:S(2)}, u32[]{:S(2)}) collective-permute-start(f32[1,128,1024]{2,1,0:T(8,128)S(1)} %add_add_fusion.3), channel_id=1, source_target_pairs={{0,8},{10,2},{8,16},{18,10},{16,24},{26,18},{24,28},{30,26},{28,20... | collective-permute-start | bytes 1572872 | tf_op jit(solution)/shard_map/ppermute | solution.py:193
  254.2 21.5 %collective-permute-start.34 = (f32[128,1024]{1,0:T(8,128)S(1)}, f32[128,1024]{1,0:T(8,128)S(1)}, u32[]{:S(2)}, u32[]{:S(2)}) collective-permute-start(f32[128,1024]{1,0:T(8,128)S(1)} %slice.307), channel_id=1, source_target_pairs={{0,1},{1,0},{2,3},{3,2},{4,5},{5,4},{6,7},{7,6},{8,9},{9,8},{10,11... | collective-permute-start | bytes 1572872 | tf_op jit(solution)/shard_map/ppermute | solution.py:40
  268.7 22.1 %collective-permute-start.40 = (f32[4,64,512]{2,1,0:T(8,128)}, f32[4,64,512]{2,1,0:T(8,128)}, u32[]{:S(2)}, u32[]{:S(2)}) collective-permute-start(f32[4,64,512]{2,1,0:T(8,128)} %maximum_add_fusion.1), channel_id=1, source_target_pairs={{0,8},{10,2},{8,16},{18,10},{16,24},{26,18},{24,28},{30,26},{28,20... | collective-permute-start | bytes 1572872 | tf_op jit(solution)/shard_map/ppermute | solution.py:193
  273.2 19.1 %collective-permute-start.39 = (f32[1,128,1024]{2,1,0:T(8,128)}, f32[1,128,1024]{2,1,0:T(8,128)}, u32[]{:S(2)}, u32[]{:S(2)}) collective-permute-start(f32[1,128,1024]{2,1,0:T(8,128)} %add_add_fusion.1.refs_0_), channel_id=1, source_target_pairs={{0,8},{10,2},{8,16},{18,10},{16,24},{26,18},{24,28},{30,26},{28,20... | collective-permute-start | bytes 1572872 | tf_op jit(solution)/shard_map/ppermute | solution.py:193
  291.9 17.0 %collective-permute-start.44 = (f32[4,64,512]{2,1,0:T(8,128)S(1)}, f32[4,64,512]{2,1,0:T(8,128)S(1)}, u32[]{:S(2)}, u32[]{:S(2)}) collective-permute-start(f32[4,64,512]{2,1,0:T(8,128)S(1)} %maximum_add_fusion.2), channel_id=1, source_target_pairs={{0,8},{10,2},{8,16},{18,10},{16,24},{26,18},{24,28},{30,26},{28,20... | collective-permute-start | bytes 1572872 | tf_op jit(solution)/shard_map/ppermute | solution.py:193
  292.3 17.1 %collective-permute-start.43 = (f32[1,128,1024]{2,1,0:T(8,128)}, f32[1,128,1024]{2,1,0:T(8,128)}, u32[]{:S(2)}, u32[]{:S(2)}) collective-permute-start(f32[1,128,1024]{2,1,0:T(8,128)} %collective-permute-done.39.refs_1_), channel_id=1, source_target_pairs={{0,8},{10,2},{8,16},{18,10},{16,24},{26,18},{24,28},{30,26},{28,20... | collective-permute-start | bytes 1572872 | tf_op jit(solution)/shard_map/ppermute | solution.py:193
  295.1 20.6 %collective-permute-start.41 = (f32[1,64,2048]{2,1,0:T(8,128)S(1)}, f32[1,64,2048]{2,1,0:T(8,128)S(1)}, u32[]{:S(2)}, u32[]{:S(2)}) collective-permute-start(f32[1,64,2048]{2,1,0:T(8,128)S(1)} %dynamic-slice_add_fusion.1), channel_id=1, source_target_pairs={{0,8},{10,2},{8,16},{18,10},{16,24},{26,18},{24,28},{30,26},{28,20... | collective-permute-start | bytes 1572872 | tf_op jit(solution)/shard_map/ppermute | solution.py:193
  333.4 19.6 %collective-permute-start.54 = (f32[1,128,1024]{2,1,0:T(8,128)}, f32[1,128,1024]{2,1,0:T(8,128)}, u32[]{:S(2)}, u32[]{:S(2)}) collective-permute-start(f32[1,128,1024]{2,1,0:T(8,128)} %collective-permute-done.48.refs_3_), channel_id=1, source_target_pairs={{0,8},{10,2},{8,16},{18,10},{16,24},{26,18},{24,28},{30,26},{28,20... | collective-permute-start | bytes 1572872 | tf_op jit(solution)/shard_map/ppermute | solution.py:193
  337.1 21.5 %collective-permute-start.53 = (f32[1,64,2048]{2,1,0:T(8,128)}, f32[1,64,2048]{2,1,0:T(8,128)}, u32[]{:S(2)}, u32[]{:S(2)}) collective-permute-start(f32[1,64,2048]{2,1,0:T(8,128)} %collective-permute-done.46.refs_1_), channel_id=1, source_target_pairs={{0,8},{10,2},{8,16},{18,10},{16,24},{26,18},{24,28},{30,26},{28,20... | collective-permute-start | bytes 1572872 | tf_op jit(solution)/shard_map/ppermute | solution.py:193
  349.4 20.5 %collective-permute-start.58 = (f32[128,1024]{1,0:T(8,128)}, f32[128,1024]{1,0:T(8,128)}, u32[]{:S(2)}, u32[]{:S(2)}) collective-permute-start(f32[128,1024]{1,0:T(8,128)} %slice.322), channel_id=1, source_target_pairs={{0,1},{1,0},{2,3},{3,2},{4,5},{5,4},{6,7},{7,6},{8,9},{9,8},{10,11... | collective-permute-start | bytes 1572872 | tf_op jit(solution)/shard_map/ppermute | solution.py:40
  350.6 19.3 %collective-permute-start.59 = (f32[51,1024]{1,0:T(8,128)S(1)}, f32[51,1024]{1,0:T(8,128)S(1)}, u32[]{:S(2)}, u32[]{:S(2)}) collective-permute-start(f32[51,1024]{1,0:T(8,128)S(1)} %concatenate.133), channel_id=1, source_target_pairs={{0,1},{1,0},{2,3},{3,2},{4,5},{5,4},{6,7},{7,6},{8,9},{9,8},{10,11... | collective-permute-start | bytes 626696 | tf_op jit(solution)/shard_map/ppermute | solution.py:40
  358.7 16.9 %collective-permute-start.57 = (f32[1,64,2048]{2,1,0:T(8,128)}, f32[1,64,2048]{2,1,0:T(8,128)}, u32[]{:S(2)}, u32[]{:S(2)}) collective-permute-start(f32[1,64,2048]{2,1,0:T(8,128)} %collective-permute-done.53.refs_2_), channel_id=1, source_target_pairs={{0,8},{10,2},{8,16},{18,10},{16,24},{26,18},{24,28},{30,26},{28,20... | collective-permute-start | bytes 1572872 | tf_op jit(solution)/shard_map/ppermute | solution.py:193
  380.0 21.9 %collective-permute-start.65 = (f32[1,64,2048]{2,1,0:T(8,128)}, f32[1,64,2048]{2,1,0:T(8,128)}, u32[]{:S(2)}, u32[]{:S(2)}) collective-permute-start(f32[1,64,2048]{2,1,0:T(8,128)} %collective-permute-done.57.refs_3_), channel_id=1, source_target_pairs={{0,8},{10,2},{8,16},{18,10},{16,24},{26,18},{24,28},{30,26},{28,20... | collective-permute-start | bytes 1572872 | tf_op jit(solution)/shard_map/ppermute | solution.py:193
  380.1 21.8 %collective-permute-start.67 = (f32[1,128,1024]{2,1,0:T(8,128)}, f32[1,128,1024]{2,1,0:T(8,128)}, u32[]{:S(2)}, u32[]{:S(2)}) collective-permute-start(f32[1,128,1024]{2,1,0:T(8,128)} %collective-permute-done.60.refs_5_), channel_id=1, source_target_pairs={{0,8},{10,2},{8,16},{18,10},{16,24},{26,18},{24,28},{30,26},{28,20... | collective-permute-start | bytes 1572872 | tf_op jit(solution)/shard_map/ppermute | solution.py:193
  382.5 19.4 %collective-permute-start.66 = (f32[128,1024]{1,0:T(8,128)S(1)}, f32[128,1024]{1,0:T(8,128)S(1)}, u32[]{:S(2)}, u32[]{:S(2)}) collective-permute-start(f32[128,1024]{1,0:T(8,128)S(1)} %get-tuple-element.282), channel_id=1, source_target_pairs={{0,1},{1,0},{2,3},{3,2},{4,5},{5,4},{6,7},{7,6},{8,9},{9,8},{10,11... | collective-permute-start | bytes 1572872 | tf_op jit(solution)/shard_map/ppermute | solution.py:40
  391.4 17.4 %collective-permute-start.64 = (f32[5,64,512]{2,1,0:T(8,128)S(1)}, f32[5,64,512]{2,1,0:T(8,128)S(1)}, u32[]{:S(2)}, u32[]{:S(2)}) collective-permute-start(f32[5,64,512]{2,1,0:T(8,128)S(1)} %collective-permute-done.63.refs_1_), channel_id=1, source_target_pairs={{0,8},{10,2},{8,16},{18,10},{16,24},{26,18},{24,28},{30,26},{28,20... | collective-permute-start | bytes 1966088 | tf_op jit(solution)/shard_map/ppermute | solution.py:193
  391.4 17.4 %collective-permute-start.75 = (f32[1,128,1024]{2,1,0:T(8,128)}, f32[1,128,1024]{2,1,0:T(8,128)}, u32[]{:S(2)}, u32[]{:S(2)}) collective-permute-start(f32[1,128,1024]{2,1,0:T(8,128)} %add_add_fusion.1.refs_0_), channel_id=1, source_target_pairs={{0,2},{2,0},{4,6},{6,4},{8,10},{10,8},{12,14},{14,12},{16,18},{18,... | collective-permute-start | bytes 1572872 | tf_op jit(solution)/shard_map/ppermute | solution.py:40
  408.8 18.4 %collective-permute-start.68 = (f32[5,64,512]{2,1,0:T(8,128)S(1)}, f32[5,64,512]{2,1,0:T(8,128)}, u32[]{:S(2)}, u32[]{:S(2)}) collective-permute-start(f32[5,64,512]{2,1,0:T(8,128)S(1)} %collective-permute-done.64.refs_2_), channel_id=1, source_target_pairs={{0,8},{10,2},{8,16},{18,10},{16,24},{26,18},{24,28},{30,26},{28,20... | collective-permute-start | bytes 1966088 | tf_op jit(solution)/shard_map/ppermute | solution.py:193
  455.8 33.7 %collective-permute-start.97 = (f32[5,64,512]{2,1,0:T(8,128)}, f32[5,64,512]{2,1,0:T(8,128)}, u32[]{:S(2)}, u32[]{:S(2)}) collective-permute-start(f32[5,64,512]{2,1,0:T(8,128)} %copy-done.68), channel_id=1, source_target_pairs={{0,2},{2,0},{4,6},{6,4},{8,10},{10,8},{12,14},{14,12},{16,18},{18,... | collective-permute-start | bytes 1966088 | tf_op jit(solution)/shard_map/ppermute | solution.py:40
  465.3 24.4 %collective-permute-start.98 = (f32[5,64,512]{2,1,0:T(8,128)S(1)}, f32[5,64,512]{2,1,0:T(8,128)}, u32[]{:S(2)}, u32[]{:S(2)}) collective-permute-start(f32[5,64,512]{2,1,0:T(8,128)S(1)} %copy-done.70), channel_id=1, source_target_pairs={{0,2},{2,0},{4,6},{6,4},{8,10},{10,8},{12,14},{14,12},{16,18},{18,... | collective-permute-start | bytes 1966088 | tf_op jit(solution)/shard_map/ppermute | solution.py:40
  (197 other events, 1583.7 us)

commit v7 on v6

--- a/solution.py
+++ b/solution.py
@@ -725,9 +725,9 @@
         return rings[-1].turn(clock, kept)
 
     (gots2[0],) = turn(down_ring, kept=(gots2[0],))
-    grad_mixed, gain2, bias2 = norm2_half(0, grad_mixed, gain2, bias2)
     give = mm(core_half(clock.hold(normed2), 1 - core), grad_pre, TN)
     clock.set(give)
+    grad_mixed, gain2, bias2 = norm2_half(0, grad_mixed, gain2, bias2)
     keep = mm(core_half(clock.hold(normed2), core), grad_pre, TN) + swap_bit(give, "seq", 0)
     up_ring = Ring([[keep]], (1,))
     clock.set(up_ring.held)

time: 513 us -> 510 us (level)
  waiting for transfers between devices: 148 us -> 135 us
  matrix products: 77.2 us -> 71.1 us
  other arithmetic: 64.3 us -> 69.9 us
  local copies, waits for them, and re-layouts: 51.4 us -> 56.6 us
    ppermute x42, waiting for transfers between devices: 97.3 us -> 88 us  [turn(): got = lax.ppermute(self.held, 'seq', self.route)]
    dot_general x26, matrix products: 77.2 us -> 71.1 us  [mm(): lax.dot_general(left, right, (dims, ((), ())), precision=HIGH, preferred_...]
    unnamed x260 -> x290, local copies, waits for them, and re-layouts: 38.2 us -> 37.8 us
  transfers between devices with their start and end apart: 104 -> 104, of which waited for: 38 -> 38; matrix products, arithmetic and copies ran while one was open for 26% -> 27% of each run, Pallas kernels for 13% -> 13%
where the time goes in v7:
time: 510 us; the launch traced here: 503 us
  waiting for transfers between devices  135 us (26%)
  starting transfers between devices  88.8 us (17%)
  Pallas kernels  76.6 us (15%)
  matrix products  71.1 us (14%)
  other arithmetic  69.9 us (14%)
  local copies, waits for them, and re-layouts  56.6 us (11%)
    ppermute x42, waiting for transfers between devices, turn(): got = lax.ppermute(self.held, 'seq', self.route)  88 us
    dot_general x26, matrix products, mm(): lax.dot_general(left, right, (dims, ((), ())), precision=HIGH, preferred_...  71.1 us
    ppermute x54, waiting for transfers between devices, swap_bit(): return lax.ppermute(value, axis, [(i, i ^ 1 << bit) for i in range(size)])  47.3 us
    ppermute x42, starting transfers between devices, turn(): got = lax.ppermute(self.held, 'seq', self.route)  37.9 us
    unnamed x290, local copies, waits for them, and re-layouts  37.8 us
    ppermute x54, starting transfers between devices, swap_bit(): return lax.ppermute(value, axis, [(i, i ^ 1 << bit) for i in range(size)])  34.1 us
    pallas_call x6, Pallas kernels, by_channels(): pl.pallas_call(kernel, grid=(width // cut,), in_specs=[spec(a.shape[0]) f...  25.8 us
    pallas_call x4, Pallas kernels, by_heads(): pl.pallas_call(kernel, grid=(heads,), in_specs=specs, out_specs=[pl.Block...  24.5 us
  transfers between devices with their start and end apart: 104, of which 38 were waited for; matrix products, arithmetic and copies ran while one was open for 27% of the time, Pallas kernels for 13%

profile of v7, /device:TPU:0, one launch (start us, length us, event | category | flops | bytes accessed | tf_op | source)
XLA Modules:
  0.0 503.0 jit_solution(18267726199160910452)
XLA Ops:
  29.3 4.0 shard_map.316.q_ref.k_ref.v_ref
  33.4 6.0 %shard_map.317 = (f32[512,512]{1,0:T(8,128)S(1)}, f32[512,512]{1,0:T(8,128)S(1)}) custom-call(f32[3,512,512]{2,1,0:T(8,128)S(1)} %shard_map.316.q_ref.k_ref.v_ref, f32[3,512,512]{2,1,0:T(8,128)S(1)} %shard_map.316.q_ref.k_ref.v_ref, f32[3,512,512]{2,1,0:T(8,128)S(1)} %shard_map.316.q_ref.k_ref.v_ref), custom_call_target="tpu_custom_call" | custom-call | bytes 1024 | tf_op jit(solution)/shard_map/pallas_call | solution.py:511
  44.9 4.1 shard_map.319
  53.3 8.0 %collective-permute-start.9 = (f32[16,1024]{1,0:T(8,128)}, f32[16,1024]{1,0:T(8,128)S(1)}, u32[]{:S(2)}, u32[]{:S(2)}) collective-permute-start(f32[16,1024]{1,0:T(8,128)} %get-tuple-element.329), channel_id=1, source_target_pairs={{0,12},{2,14},{4,8},{6,10},{8,4},{10,6},{12,0},{14,2},{16,28},{18,... | collective-permute-start | bytes 196616 | tf_op jit(solution)/shard_map/ppermute | solution.py:77
  91.6 4.6 fusion.104
  102.5 4.1 fusion.97
  112.6 5.1 %fusion.15 = f32[1024,1024]{1,0:T(8,128)} fusion(f32[512,1024]{1,0:T(8,128)S(1)} %copy-done.44, f32[512,2048]{1,0:T(8,128)S(1)} %get-tuple-element.180, s32[]{:T(128)S(6)} %select_n.573), kind=kOutput, calls=%fused_computation.28 | convolution fusion | flops 3221225472 | bytes 8388612 | tf_op jit(solution)/shard_map/dot_general | solution.py:20
  123.6 5.9 %fusion.13 = f32[1024,1024]{1,0:T(8,128)S(1)} fusion(f32[512,1024]{1,0:T(8,128)} %param.36, f32[512,2048]{1,0:T(8,128)} %copy-done.21, s32[]{:T(128)S(6)} %select_n.574), kind=kOutput, calls=%fused_computation.26 | convolution fusion | flops 3221225472 | bytes 8388612 | tf_op jit(solution)/shard_map/dot_general | solution.py:20
  137.9 9.6 %collective-permute-done.16 = f32[256,1024]{1,0:T(8,128)S(1)} collective-permute-done((f32[256,1024]{1,0:T(8,128)}, f32[256,1024]{1,0:T(8,128)S(1)}, u32[]{:S(2)}, u32[]{:S(2)}) %collective-permute-start.16) | collective-permute-done | bytes 1048608 | tf_op jit(solution)/shard_map/ppermute | solution.py:40
  149.9 5.1 %fusion.46 = f32[512,2048]{1,0:T(8,128)} fusion(f32[512,2048]{1,0:T(8,128)S(1)} %copy-done.3, f32[512,1024]{1,0:T(8,128)S(1)} %fusion.51, s32[]{:T(128)S(6)} %select_n.582), kind=kOutput, calls=%fused_computation.84 | convolution fusion | flops 3221225472 | bytes 9437188 | tf_op jit(solution)/shard_map/dot_general | solution.py:20
  165.8 5.4 %convolution_add_fusion = f32[512,2048]{1,0:T(8,128)S(1)} fusion(f32[512,2048]{1,0:T(8,128)} %collective-permute-done.17, f32[512,2048]{1,0:T(8,128)S(1)} %copy-done.4, f32[512,1024]{1,0:T(8,128)S(1)} %copy-done.28, s32[]{:T(128)S(6)} %select_n.583), kind=kOutput, calls=%fused_computation | convolution fusion | flops 3222274048 | bytes 13631492 | tf_op jit(solution)/shard_map/dot_general | solution.py:20
  171.3 12.6 %collective-permute-done.20 = f32[256,1024]{1,0:T(8,128)S(1)} collective-permute-done((f32[256,1024]{1,0:T(8,128)S(1)}, f32[256,1024]{1,0:T(8,128)S(1)}, u32[]{:S(2)}, u32[]{:S(2)}) %collective-permute-start.20) | collective-permute-done | bytes 1048608 | tf_op jit(solution)/shard_map/ppermute | solution.py:40
  204.1 11.4 %shard_map.328 = f32[3,640,512]{2,1,0:T(8,128)S(1)} custom-call(s32[1]{0:T(128)} %bitcast.ok_ref, f32[3,512,512]{2,1,0:T(8,128)S(1)} %shard_map.316.q_ref.k_ref.v_ref, f32[3,512,512]{2,1,0:T(8,128)S(1)} %shard_map.316.q_ref.k_ref.v_ref, f32[3,512,512]{2,1,0:T(8,128)S(1)} %shard_map.316.q_ref.k_ref.v_ref, f32[2,128,512]{2,1,0:T(8,128)S(1)} %copy-done.18, ...), custom_call_target="tpu_custom_call" | custom-call | bytes 1024 | tf_op jit(solution)/shard_map/pallas_call | solution.py:511
  245.4 4.5 fusion.107
  279.3 6.8 %shard_map.330 = (f32[16,1024]{1,0:T(8,128)S(1)}, f32[16,1024]{1,0:T(8,128)S(1)}, f32[16,1024]{1,0:T(8,128)S(1)}, f32[16,1024]{1,0:T(8,128)S(1)}, f32[1,1024]{1,0:T(1,128)S(1)}, /*index=5*/f32[128,1024]{1,0:T(8,128)S(1)}) custom-call(f32[128,1024]{1,0:T(8,128)} %collective-permute-done.tail_ref.x_ref, f32[128,1024]{1,0:T(8,128)S(1)} %slice_select_fusion.d_ref, ...), custom_call_target="tpu_custom_call" | custom-call | bytes 1024 | tf_op jit(solution)/shard_map/pallas_call | solution.py:405
  293.1 6.8 %shard_map.331 = f32[16,1024]{1,0:T(8,128)S(1)} custom-call(f32[128,1024]{1,0:T(8,128)} %collective-permute-done.tail_ref.x_ref, f32[512,1024]{1,0:T(8,128)S(1)} %copy-done.9, f32[16,1024]{1,0:T(8,128)S(1)} %slice.298.decay_ref), custom_call_target="tpu_custom_call" | custom-call | bytes 1024 | tf_op jit(solution)/shard_map/pallas_call | solution.py:405
  312.4 4.0 collective-permute-done.42
  338.4 4.5 collective-permute-done.55
  347.3 5.1 %concatenate.133 = f32[51,1024]{1,0:T(8,128)} concatenate(f32[16,1024]{1,0:T(8,128)} %get-tuple-element.326, f32[16,1024]{1,0:T(8,128)} %get-tuple-element.325, f32[16,1024]{1,0:T(8,128)} %multiply_subtract_fusion, f32[1,1024]{1,0:T(1,128)S(1)} %get-tuple-element.218, f32[1,1024]{1,0:T(1,128)S(1)} %bitcast.154, f32[1,1024]{1,0:T(1,128)S(1)} %bitcast.155), dimensions={0} | concatenate | bytes 417792 | tf_op jit(solution)/shard_map/concatenate | solution.py:835
  361.1 4.5 collective-permute-done.60.refs_5_
  366.0 5.1 %collective-permute-done.57.refs_3_ = f32[1,64,2048]{2,1,0:T(8,128)} collective-permute-done((f32[1,64,2048]{2,1,0:T(8,128)}, f32[1,64,2048]{2,1,0:T(8,128)}, u32[]{:S(2)}, u32[]{:S(2)}) %collective-permute-start.57) | collective-permute-done | bytes 524320 | tf_op jit(solution)/shard_map/ppermute | solution.py:193
  384.0 4.9 collective-permute-done.63.refs_1_
  389.0 11.3 %collective-permute-done.67.refs_6_ = f32[1,128,1024]{2,1,0:T(8,128)} collective-permute-done((f32[1,128,1024]{2,1,0:T(8,128)}, f32[1,128,1024]{2,1,0:T(8,128)}, u32[]{:S(2)}, u32[]{:S(2)}) %collective-permute-start.67) | collective-permute-done | bytes 524320 | tf_op jit(solution)/shard_map/ppermute | solution.py:193
  402.4 4.9 collective-permute-done.64.refs_2_
  408.2 4.7 collective-permute-done.69.refs_5_
  427.5 6.9 %shard_map.334 = f32[1,2,8,128,1024]{4,3,2,1,0:T(8,128)} custom-call(s32[2,16]{1,0:T(2,128)} %pad_add_fusion.where_ref, f32[1,128,1024]{2,1,0:T(8,128)} %add_add_fusion.1.refs_0_, f32[1,128,1024]{2,1,0:T(8,128)} %collective-permute-done.39.refs_1_, f32[1,128,1024]{2,1,0:T(8,128)} %collective-permute-done.43.refs_2_, ...), custom_call_target="tpu_custom_call" | custom-call | bytes 1024 | tf_op jit(solution)/shard_map/pallas_call | solution.py:218
  434.4 4.4 collective-permute-done.74
  439.9 8.5 %collective-permute-done.84.refs_7_ = f32[1,64,2048]{2,1,0:T(8,128)} collective-permute-done((f32[1,64,2048]{2,1,0:T(8,128)}, f32[1,64,2048]{2,1,0:T(8,128)}, u32[]{:S(2)}, u32[]{:S(2)}) %collective-permute-start.84) | collective-permute-done | bytes 524320 | tf_op jit(solution)/shard_map/ppermute | solution.py:193
  455.7 6.8 %shard_map.335 = f32[1,2,8,64,2048]{4,3,2,1,0:T(8,128)} custom-call(s32[2,16]{1,0:T(2,128)} %pad_add_fusion.where_ref, f32[1,64,2048]{2,1,0:T(8,128)} %copy-done.68, f32[1,64,2048]{2,1,0:T(8,128)} %collective-permute-done.46.refs_1_, f32[1,64,2048]{2,1,0:T(8,128)} %collective-permute-done.53.refs_2_, f32[1,64,2048]{2,1,0:T(8,128)} %collective-permute-done.57.refs_3_, ...), custom_call_target="tpu_custom_call" | custom-call | bytes 1024 | tf_op jit(solution)/shard_map/pallas_call | solution.py:218
  465.5 7.9 %collective-permute-done.93.refs_6_ = f32[5,64,512]{2,1,0:T(8,128)S(1)} collective-permute-done((f32[5,64,512]{2,1,0:T(8,128)}, f32[5,64,512]{2,1,0:T(8,128)S(1)}, u32[]{:S(2)}, u32[]{:S(2)}) %collective-permute-start.93) | collective-permute-done | bytes 655392 | tf_op jit(solution)/shard_map/ppermute | solution.py:193
  476.5 7.5 %collective-permute-done.94.refs_7_ = f32[5,64,512]{2,1,0:T(8,128)S(1)} collective-permute-done((f32[5,64,512]{2,1,0:T(8,128)S(1)}, f32[5,64,512]{2,1,0:T(8,128)S(1)}, u32[]{:S(2)}, u32[]{:S(2)}) %collective-permute-start.94) | collective-permute-done | bytes 655392 | tf_op jit(solution)/shard_map/ppermute | solution.py:193
  492.2 7.5 %shard_map.336 = (f32[3,2,8,64,512]{4,3,2,1,0:T(8,128)}, f32[1,2,8,64,512]{4,3,2,1,0:T(8,128)}) custom-call(s32[2,16]{1,0:T(2,128)} %pad_add_fusion.where_ref, f32[4,64,512]{2,1,0:T(8,128)} %copy-done.66, f32[5,64,512]{2,1,0:T(8,128)} %copy-done.74, f32[5,64,512]{2,1,0:T(8,128)} %collective-permute-done.64.refs_2_, f32[5,64,512]{2,1,0:T(8,128)} %copy-done.75, ...), custom_call_target="tpu_custom_call" | custom-call | bytes 1024 | tf_op jit(solution)/shard_map/pallas_call | solution.py:218
  (642 shorter events, 296.0 us)
Async XLA Ops:
  15.3 28.0 %collective-permute-start = (f32[128,1024]{1,0:T(8,128)}, f32[128,1024]{1,0:T(8,128)}, u32[]{:S(2)}, u32[]{:S(2)}) collective-permute-start(f32[128,1024]{1,0:T(8,128)} %slice.297), channel_id=1, source_target_pairs={{0,2},{2,4},{4,6},{6,8},{8,10},{10,12},{12,14},{16,18},{18,20},{20... | collective-permute-start | bytes 1572872 | tf_op jit(solution)/shard_map/ppermute | solution.py:51
  23.2 18.1 %collective-permute-start.5 = (f32[81,512]{1,0:T(8,128)}, f32[81,512]{1,0:T(8,128)}, u32[]{:S(2)}, u32[]{:S(2)}) collective-permute-start(f32[81,512]{1,0:T(8,128)} %maximum_select_fusion.5), channel_id=1, source_target_pairs={{0,16},{2,18},{4,20},{6,22},{8,24},{10,26},{12,28},{14,30},{16,0},... | collective-permute-start | bytes 497672 | tf_op jit(solution)/shard_map/ppermute | solution.py:40
  50.2 38.4 %collective-permute-start.11 = (f32[256,1024]{1,0:T(8,128)}, f32[256,1024]{1,0:T(8,128)}, u32[]{:S(2)}, u32[]{:S(2)}) collective-permute-start(f32[256,1024]{1,0:T(8,128)} %bitcast_convert_fusion), channel_id=1, source_target_pairs={{0,1},{1,0},{2,3},{3,2},{4,5},{5,4},{6,7},{7,6},{8,9},{9,8},{10,11... | collective-permute-start | bytes 3145736 | tf_op jit(solution)/shard_map/ppermute | solution.py:40
  84.4 22.2 %collective-permute-start.13 = (f32[256,512]{1,0:T(8,128)S(1)}, f32[256,512]{1,0:T(8,128)S(1)}, u32[]{:S(2)}, u32[]{:S(2)}) collective-permute-start(f32[256,512]{1,0:T(8,128)S(1)} %get-tuple-element.147), channel_id=1, source_target_pairs={{0,1},{1,0},{2,3},{3,2},{4,5},{5,4},{6,7},{7,6},{8,9},{9,8},{10,11... | collective-permute-start | bytes 1572872 | tf_op jit(solution)/shard_map/ppermute | solution.py:40
  122.1 25.5 %collective-permute-start.16 = (f32[256,1024]{1,0:T(8,128)}, f32[256,1024]{1,0:T(8,128)S(1)}, u32[]{:S(2)}, u32[]{:S(2)}) collective-permute-start(f32[256,1024]{1,0:T(8,128)} %fusion.97), channel_id=1, source_target_pairs={{0,1},{1,0},{2,3},{3,2},{4,5},{5,4},{6,7},{7,6},{8,9},{9,8},{10,11... | collective-permute-start | bytes 3145736 | tf_op jit(solution)/shard_map/ppermute | solution.py:40
  158.3 25.6 %collective-permute-start.20 = (f32[256,1024]{1,0:T(8,128)S(1)}, f32[256,1024]{1,0:T(8,128)S(1)}, u32[]{:S(2)}, u32[]{:S(2)}) collective-permute-start(f32[256,1024]{1,0:T(8,128)S(1)} %copy-done.71), channel_id=1, source_target_pairs={{0,1},{1,0},{2,3},{3,2},{4,5},{5,4},{6,7},{7,6},{8,9},{9,8},{10,11... | collective-permute-start | bytes 3145736 | tf_op jit(solution)/shard_map/ppermute | solution.py:40
  159.8 24.1 %collective-permute-start.19 = (f32[1,128,1024]{2,1,0:T(8,128)S(1)}, f32[1,128,1024]{2,1,0:T(8,128)S(1)}, u32[]{:S(2)}, u32[]{:S(2)}) collective-permute-start(f32[1,128,1024]{2,1,0:T(8,128)S(1)} %copy-done.84), channel_id=1, source_target_pairs={{0,8},{10,2},{8,16},{18,10},{16,24},{26,18},{24,28},{30,26},{28,20... | collective-permute-start | bytes 1572872 | tf_op jit(solution)/shard_map/ppermute | solution.py:193
  171.3 26.7 %collective-permute-start.18 = (f32[1,64,2048]{2,1,0:T(8,128)S(1)}, f32[1,64,2048]{2,1,0:T(8,128)S(1)}, u32[]{:S(2)}, u32[]{:S(2)}) collective-permute-start(f32[1,64,2048]{2,1,0:T(8,128)S(1)} %constant_dynamic-slice_fusion.29), channel_id=1, source_target_pairs={{0,8},{10,2},{8,16},{18,10},{16,24},{26,18},{24,28},{30,26},{28,20... | collective-permute-start | bytes 1572872 | tf_op jit(solution)/shard_map/ppermute | solution.py:193
  196.6 19.0 %collective-permute-start.23 = (f32[1,128,1024]{2,1,0:T(8,128)}, f32[1,128,1024]{2,1,0:T(8,128)}, u32[]{:S(2)}, u32[]{:S(2)}) collective-permute-start(f32[1,128,1024]{2,1,0:T(8,128)} %add_add_fusion.5), channel_id=1, source_target_pairs={{0,8},{10,2},{8,16},{18,10},{16,24},{26,18},{24,28},{30,26},{28,20... | collective-permute-start | bytes 1572872 | tf_op jit(solution)/shard_map/ppermute | solution.py:193
  198.9 19.4 %collective-permute-start.22 = (f32[1,64,2048]{2,1,0:T(8,128)}, f32[1,64,2048]{2,1,0:T(8,128)}, u32[]{:S(2)}, u32[]{:S(2)}) collective-permute-start(f32[1,64,2048]{2,1,0:T(8,128)} %dynamic-slice_add_fusion.6), channel_id=1, source_target_pairs={{0,8},{10,2},{8,16},{18,10},{16,24},{26,18},{24,28},{30,26},{28,20... | collective-permute-start | bytes 1572872 | tf_op jit(solution)/shard_map/ppermute | solution.py:193
  232.0 26.0 %collective-permute-start.26 = (f32[1,64,2048]{2,1,0:T(8,128)S(1)}, f32[1,64,2048]{2,1,0:T(8,128)S(1)}, u32[]{:S(2)}, u32[]{:S(2)}) collective-permute-start(f32[1,64,2048]{2,1,0:T(8,128)S(1)} %dynamic-slice_add_fusion.4), channel_id=1, source_target_pairs={{0,8},{10,2},{8,16},{18,10},{16,24},{26,18},{24,28},{30,26},{28,20... | collective-permute-start | bytes 1572872 | tf_op jit(solution)/shard_map/ppermute | solution.py:193
  233.2 21.1 %collective-permute-start.27 = (f32[1,128,1024]{2,1,0:T(8,128)S(1)}, f32[1,128,1024]{2,1,0:T(8,128)S(1)}, u32[]{:S(2)}, u32[]{:S(2)}) collective-permute-start(f32[1,128,1024]{2,1,0:T(8,128)S(1)} %add_add_fusion.3), channel_id=1, source_target_pairs={{0,8},{10,2},{8,16},{18,10},{16,24},{26,18},{24,28},{30,26},{28,20... | collective-permute-start | bytes 1572872 | tf_op jit(solution)/shard_map/ppermute | solution.py:193
  250.0 21.0 %collective-permute-start.34 = (f32[128,1024]{1,0:T(8,128)S(1)}, f32[128,1024]{1,0:T(8,128)S(1)}, u32[]{:S(2)}, u32[]{:S(2)}) collective-permute-start(f32[128,1024]{1,0:T(8,128)S(1)} %slice.307), channel_id=1, source_target_pairs={{0,1},{1,0},{2,3},{3,2},{4,5},{5,4},{6,7},{7,6},{8,9},{9,8},{10,11... | collective-permute-start | bytes 1572872 | tf_op jit(solution)/shard_map/ppermute | solution.py:40
  266.0 20.1 %collective-permute-start.40 = (f32[4,64,512]{2,1,0:T(8,128)}, f32[4,64,512]{2,1,0:T(8,128)}, u32[]{:S(2)}, u32[]{:S(2)}) collective-permute-start(f32[4,64,512]{2,1,0:T(8,128)} %maximum_add_fusion.1), channel_id=1, source_target_pairs={{0,8},{10,2},{8,16},{18,10},{16,24},{26,18},{24,28},{30,26},{28,20... | collective-permute-start | bytes 1572872 | tf_op jit(solution)/shard_map/ppermute | solution.py:193
  270.8 19.1 %collective-permute-start.39 = (f32[1,128,1024]{2,1,0:T(8,128)}, f32[1,128,1024]{2,1,0:T(8,128)}, u32[]{:S(2)}, u32[]{:S(2)}) collective-permute-start(f32[1,128,1024]{2,1,0:T(8,128)} %add_add_fusion.1.refs_0_), channel_id=1, source_target_pairs={{0,8},{10,2},{8,16},{18,10},{16,24},{26,18},{24,28},{30,26},{28,20... | collective-permute-start | bytes 1572872 | tf_op jit(solution)/shard_map/ppermute | solution.py:193
  287.3 18.1 %collective-permute-start.44 = (f32[4,64,512]{2,1,0:T(8,128)S(1)}, f32[4,64,512]{2,1,0:T(8,128)S(1)}, u32[]{:S(2)}, u32[]{:S(2)}) collective-permute-start(f32[4,64,512]{2,1,0:T(8,128)S(1)} %maximum_add_fusion.2), channel_id=1, source_target_pairs={{0,8},{10,2},{8,16},{18,10},{16,24},{26,18},{24,28},{30,26},{28,20... | collective-permute-start | bytes 1572872 | tf_op jit(solution)/shard_map/ppermute | solution.py:193
  289.9 17.2 %collective-permute-start.43 = (f32[1,128,1024]{2,1,0:T(8,128)}, f32[1,128,1024]{2,1,0:T(8,128)}, u32[]{:S(2)}, u32[]{:S(2)}) collective-permute-start(f32[1,128,1024]{2,1,0:T(8,128)} %collective-permute-done.39.refs_1_), channel_id=1, source_target_pairs={{0,8},{10,2},{8,16},{18,10},{16,24},{26,18},{24,28},{30,26},{28,20... | collective-permute-start | bytes 1572872 | tf_op jit(solution)/shard_map/ppermute | solution.py:193
  292.8 17.1 %collective-permute-start.41 = (f32[1,64,2048]{2,1,0:T(8,128)S(1)}, f32[1,64,2048]{2,1,0:T(8,128)S(1)}, u32[]{:S(2)}, u32[]{:S(2)}) collective-permute-start(f32[1,64,2048]{2,1,0:T(8,128)S(1)} %dynamic-slice_add_fusion.1), channel_id=1, source_target_pairs={{0,8},{10,2},{8,16},{18,10},{16,24},{26,18},{24,28},{30,26},{28,20... | collective-permute-start | bytes 1572872 | tf_op jit(solution)/shard_map/ppermute | solution.py:193
  303.7 17.4 %collective-permute-start.52 = (f32[32,1024]{1,0:T(8,128)S(1)}, f32[32,1024]{1,0:T(8,128)S(1)}, u32[]{:S(2)}, u32[]{:S(2)}) collective-permute-start(f32[32,1024]{1,0:T(8,128)S(1)} %pad_maximum_fusion.5), channel_id=1, source_target_pairs={{0,12},{2,14},{4,8},{6,10},{8,4},{10,6},{12,0},{14,2},{16,28},{18,... | collective-permute-start | bytes 393224 | tf_op jit(solution)/shard_map/ppermute | solution.py:77
  305.4 17.2 %collective-permute-start.51 = (f32[32,1024]{1,0:T(8,128)S(1)}, f32[32,1024]{1,0:T(8,128)S(1)}, u32[]{:S(2)}, u32[]{:S(2)}) collective-permute-start(f32[32,1024]{1,0:T(8,128)S(1)} %pad_maximum_fusion.5), channel_id=1, source_target_pairs={{0,8},{2,10},{4,12},{6,14},{8,0},{10,2},{12,4},{14,6},{16,24},{18,... | collective-permute-start | bytes 393224 | tf_op jit(solution)/shard_map/ppermute | solution.py:77
  309.9 19.5 %collective-permute-start.49 = (f32[4,64,512]{2,1,0:T(8,128)S(1)}, f32[4,64,512]{2,1,0:T(8,128)S(1)}, u32[]{:S(2)}, u32[]{:S(2)}) collective-permute-start(f32[4,64,512]{2,1,0:T(8,128)S(1)} %maximum_add_fusion.3), channel_id=1, source_target_pairs={{0,8},{10,2},{8,16},{18,10},{16,24},{26,18},{24,28},{30,26},{28,20... | collective-permute-start | bytes 1572872 | tf_op jit(solution)/shard_map/ppermute | solution.py:193
  331.8 21.8 %collective-permute-start.54 = (f32[1,128,1024]{2,1,0:T(8,128)}, f32[1,128,1024]{2,1,0:T(8,128)}, u32[]{:S(2)}, u32[]{:S(2)}) collective-permute-start(f32[1,128,1024]{2,1,0:T(8,128)} %collective-permute-done.48.refs_3_), channel_id=1, source_target_pairs={{0,8},{10,2},{8,16},{18,10},{16,24},{26,18},{24,28},{30,26},{28,20... | collective-permute-start | bytes 1572872 | tf_op jit(solution)/shard_map/ppermute | solution.py:193
  333.6 20.7 %collective-permute-start.53 = (f32[1,64,2048]{2,1,0:T(8,128)}, f32[1,64,2048]{2,1,0:T(8,128)}, u32[]{:S(2)}, u32[]{:S(2)}) collective-permute-start(f32[1,64,2048]{2,1,0:T(8,128)} %collective-permute-done.46.refs_1_), channel_id=1, source_target_pairs={{0,8},{10,2},{8,16},{18,10},{16,24},{26,18},{24,28},{30,26},{28,20... | collective-permute-start | bytes 1572872 | tf_op jit(solution)/shard_map/ppermute | solution.py:193
  346.5 19.5 %collective-permute-start.58 = (f32[128,1024]{1,0:T(8,128)}, f32[128,1024]{1,0:T(8,128)}, u32[]{:S(2)}, u32[]{:S(2)}) collective-permute-start(f32[128,1024]{1,0:T(8,128)} %slice.322), channel_id=1, source_target_pairs={{0,1},{1,0},{2,3},{3,2},{4,5},{5,4},{6,7},{7,6},{8,9},{9,8},{10,11... | collective-permute-start | bytes 1572872 | tf_op jit(solution)/shard_map/ppermute | solution.py:40
  378.3 21.9 %collective-permute-start.65 = (f32[1,64,2048]{2,1,0:T(8,128)}, f32[1,64,2048]{2,1,0:T(8,128)}, u32[]{:S(2)}, u32[]{:S(2)}) collective-permute-start(f32[1,64,2048]{2,1,0:T(8,128)} %collective-permute-done.57.refs_3_), channel_id=1, source_target_pairs={{0,8},{10,2},{8,16},{18,10},{16,24},{26,18},{24,28},{30,26},{28,20... | collective-permute-start | bytes 1572872 | tf_op jit(solution)/shard_map/ppermute | solution.py:193
  379.3 21.0 %collective-permute-start.67 = (f32[1,128,1024]{2,1,0:T(8,128)}, f32[1,128,1024]{2,1,0:T(8,128)}, u32[]{:S(2)}, u32[]{:S(2)}) collective-permute-start(f32[1,128,1024]{2,1,0:T(8,128)} %collective-permute-done.60.refs_5_), channel_id=1, source_target_pairs={{0,8},{10,2},{8,16},{18,10},{16,24},{26,18},{24,28},{30,26},{28,20... | collective-permute-start | bytes 1572872 | tf_op jit(solution)/shard_map/ppermute | solution.py:193
  382.5 17.7 %collective-permute-start.66 = (f32[128,1024]{1,0:T(8,128)S(1)}, f32[128,1024]{1,0:T(8,128)S(1)}, u32[]{:S(2)}, u32[]{:S(2)}) collective-permute-start(f32[128,1024]{1,0:T(8,128)S(1)} %get-tuple-element.282), channel_id=1, source_target_pairs={{0,1},{1,0},{2,3},{3,2},{4,5},{5,4},{6,7},{7,6},{8,9},{9,8},{10,11... | collective-permute-start | bytes 1572872 | tf_op jit(solution)/shard_map/ppermute | solution.py:40
  388.9 18.4 %collective-permute-start.64 = (f32[5,64,512]{2,1,0:T(8,128)S(1)}, f32[5,64,512]{2,1,0:T(8,128)}, u32[]{:S(2)}, u32[]{:S(2)}) collective-permute-start(f32[5,64,512]{2,1,0:T(8,128)S(1)} %collective-permute-done.63.refs_1_), channel_id=1, source_target_pairs={{0,8},{10,2},{8,16},{18,10},{16,24},{26,18},{24,28},{30,26},{28,20... | collective-permute-start | bytes 1966088 | tf_op jit(solution)/shard_map/ppermute | solution.py:193
  388.9 18.4 %collective-permute-start.75 = (f32[1,128,1024]{2,1,0:T(8,128)}, f32[1,128,1024]{2,1,0:T(8,128)}, u32[]{:S(2)}, u32[]{:S(2)}) collective-permute-start(f32[1,128,1024]{2,1,0:T(8,128)} %add_add_fusion.1.refs_0_), channel_id=1, source_target_pairs={{0,2},{2,0},{4,6},{6,4},{8,10},{10,8},{12,14},{14,12},{16,18},{18,... | collective-permute-start | bytes 1572872 | tf_op jit(solution)/shard_map/ppermute | solution.py:40
  407.3 18.1 %collective-permute-start.68 = (f32[5,64,512]{2,1,0:T(8,128)}, f32[5,64,512]{2,1,0:T(8,128)S(1)}, u32[]{:S(2)}, u32[]{:S(2)}) collective-permute-start(f32[5,64,512]{2,1,0:T(8,128)} %collective-permute-done.64.refs_2_), channel_id=1, source_target_pairs={{0,8},{10,2},{8,16},{18,10},{16,24},{26,18},{24,28},{30,26},{28,20... | collective-permute-start | bytes 1966088 | tf_op jit(solution)/shard_map/ppermute | solution.py:193
  454.0 33.7 %collective-permute-start.97 = (f32[5,64,512]{2,1,0:T(8,128)S(1)}, f32[5,64,512]{2,1,0:T(8,128)}, u32[]{:S(2)}, u32[]{:S(2)}) collective-permute-start(f32[5,64,512]{2,1,0:T(8,128)S(1)} %collective-permute-done.63.refs_1_), channel_id=1, source_target_pairs={{0,2},{2,0},{4,6},{6,4},{8,10},{10,8},{12,14},{14,12},{16,18},{18,... | collective-permute-start | bytes 1966088 | tf_op jit(solution)/shard_map/ppermute | solution.py:40
  463.8 24.1 %collective-permute-start.98 = (f32[5,64,512]{2,1,0:T(8,128)}, f32[5,64,512]{2,1,0:T(8,128)}, u32[]{:S(2)}, u32[]{:S(2)}) collective-permute-start(f32[5,64,512]{2,1,0:T(8,128)} %collective-permute-done.64.refs_2_), channel_id=1, source_target_pairs={{0,2},{2,0},{4,6},{6,4},{8,10},{10,8},{12,14},{14,12},{16,18},{18,... | collective-permute-start | bytes 1966088 | tf_op jit(solution)/shard_map/ppermute | solution.py:40
  (212 other events, 1784.1 us)
